TPU v7x, 32 devices: a whole 2x2x4 slice. The times are simulated.
32 devices in a mesh: dp: 8 (over z, x), tensor: 4 (over y, core).
Axes of the slice: x: 2, y: 2, z: 4, core: 2. Of those that a mesh axis runs over, the one named last changes fastest.
Arguments:
- tokens: bfloat16 [2, 4096, 2048], P(None, ('dp', 'tensor')), may hold values from -6 to 6
- cotangent: bfloat16 [2, 4096, 2048], P(None, ('dp', 'tensor')), may hold values from -6 to 6
- token_slots: int32 [2, 4096], P(None, ('dp', 'tensor')), may hold values from 0 to 4095, as said below
- lengths: int32 [2, 8, 3], P(None, 'dp'), may hold values from 1 to 256, 512 in all within a row
- query_weight: bfloat16 [2048, 2048], P('dp', 'tensor'), may hold values from -0.125 to 0.125
- key_projection_weight: bfloat16 [2048, 1024], P('dp', 'tensor'), may hold values from -0.125 to 0.125
- value_projection_weight: bfloat16 [2048, 1024], P('dp', 'tensor'), may hold values from -0.125 to 0.125
- output_weight: bfloat16 [2048, 2048], P(('tensor', 'dp')), may hold values from -0.75 to 0.75
- gate_weight: bfloat16 [2048, 8192], P('dp', 'tensor'), may hold values from -0.125 to 0.125
- up_weight: bfloat16 [2048, 8192], P('dp', 'tensor'), may hold values from -0.125 to 0.125
- down_weight: bfloat16 [8192, 2048], P(('tensor', 'dp')), may hold values from -0.0625 to 0.0625
- prenorm_gain: bfloat16 [2048], P('dp'), may hold values from 0.5 to 1.5
- midnorm_gain: bfloat16 [2048], P('dp'), may hold values from 0.5 to 1.5
Outputs:
- layer_out: bfloat16 [2, 4096, 2048], P(None, ('dp', 'tensor'))
- tokens_grad: bfloat16 [2, 4096, 2048], P(None, ('dp', 'tensor'))
- query_grad: float32 [2048, 2048], P('dp', 'tensor')
- key_grad: float32 [2048, 1024], P('dp', 'tensor')
- value_grad: float32 [2048, 1024], P('dp', 'tensor')
- output_grad: float32 [2048, 2048], P(('tensor', 'dp'))
- gate_grad: float32 [2048, 8192], P('dp', 'tensor')
- up_grad: float32 [2048, 8192], P('dp', 'tensor')
- down_grad: float32 [8192, 2048], P(('tensor', 'dp'))
- prenorm_grad: float32 [2048], P('dp')
- midnorm_grad: float32 [2048], P('dp')
Inputs may be any that keep to these rules, and one draw needn't show every extreme that they name: `token_slots`: for each micro-batch a permutation of the token positions; the tokens of one device go 4 to each device of the work layout. Each row of 3 lengths fills the 512 tokens of one data index in one micro-batch.
All inputs are finite; a program needn't handle non-finite values.
Results may differ from a plain program's by a relative error of at most 0.024.
Values may be sent and summed in bfloat16 or wider, within the bound.
No kernel may reach another device: no remote copies, remote signals or barrier semaphores. Data moves between devices by JAX's collectives and lax.ppermute only.
A program may use at most 192 MiB of HBM per device.

v0:
```python
import math

import jax
import jax.numpy as jnp
from jax import lax
from jax.sharding import PartitionSpec as P

HEAD_SIZE = 256


EPSILON = 1e-06
ROPE_BASE = 1000042.0
BLOCK = 512
NEGATIVE = -1e30


def rms_scale(value_heads):
    return lax.rsqrt(jnp.mean(value_heads * value_heads, axis=-1, keepdims=True) + EPSILON)


def rope_tables(positions, head):
    half = head // 2
    frequency = jnp.exp(jnp.arange(half, dtype=jnp.float32) * (-2.0 * math.log(ROPE_BASE) / head))
    angles = positions.astype(jnp.float32)[:, None] * frequency[None, :]
    return (jnp.cos(angles), jnp.sin(angles))


def apply_rotary(value_heads, cosine_table, sine_table):
    half = value_heads.shape[-1] // 2
    first = value_heads[..., :half]
    second = value_heads[..., half:]
    cosine_table = cosine_table[:, None, :]
    sine_table = sine_table[:, None, :]
    return jnp.concatenate(
        [first * cosine_table - second * sine_table, second * cosine_table + first * sine_table],
        axis=-1,
    )


def rotate_back(value_heads, cosine_table, sine_table):
    half = value_heads.shape[-1] // 2
    first = value_heads[..., :half]
    second = value_heads[..., half:]
    cosine_table = cosine_table[:, None, :]
    sine_table = sine_table[:, None, :]
    return jnp.concatenate(
        [first * cosine_table + second * sine_table, second * cosine_table - first * sine_table],
        axis=-1,
    )


def sequence_layout(lens, total_count):
    rows = jnp.arange(total_count, dtype=jnp.int32)
    ends = jnp.cumsum(lens)
    segment = jnp.sum((rows[:, None] >= ends[None, :]).astype(jnp.int32), axis=1)
    starts = ends - lens
    which = segment[:, None] == jnp.arange(lens.shape[0], dtype=jnp.int32)[None, :]
    begin = jnp.sum(jnp.where(which, starts[None, :], 0), axis=1)
    return (segment, rows - begin)


def outer_sum(left, right):
    return lax.dot_general(
        left, right, (((0,), (0,)), ((), ())), preferred_element_type=jnp.float32
    )


def times_transposed(left, right):
    return lax.dot_general(
        left, right, (((1,), (1,)), ((), ())), preferred_element_type=jnp.float32
    )


def block_scores(query_rotated, key_rot, segment, start, scale):
    total_count = key_rot.shape[0]
    rows = jnp.arange(total_count, dtype=jnp.int32)
    row_block = start + jnp.arange(BLOCK, dtype=jnp.int32)
    allowed = (segment[:, None] == segment[None, :]) & (row_block[:, None] >= rows[None, :])
    scores = (
        jnp.einsum("qcgd,kcd->cgqk", query_rotated, key_rot, preferred_element_type=jnp.float32)
        * scale
    )
    return (query_rotated, jnp.where(allowed, scores, NEGATIVE))


def attend_forward(query_rotated, key_rot, value_low, segment, scale):
    total_count = query_rotated.shape[0]

    def one_block(index):
        start = index * BLOCK
        query_block, scores = block_scores(query_rotated, key_rot, segment, start, scale)
        row_max = jnp.max(scores, axis=-1, keepdims=True)
        expo = jnp.exp(scores - row_max)
        row_total = jnp.sum(expo, axis=-1, keepdims=True)
        probs = (expo / row_total).astype(jnp.bfloat16)
        heads = jnp.einsum("cgqk,kcd->qcgd", probs, value_low, preferred_element_type=jnp.float32)
        return (heads.astype(jnp.bfloat16), row_max + jnp.log(row_total))

    heads, log_totals = lax.map(one_block, jnp.arange(total_count // BLOCK, dtype=jnp.int32))
    return (heads.reshape(query_rotated.shape), log_totals)


def attend_backward(query_rotated, key_rot, value_low, d_heads, log_totals, segment, scale):
    total_count = query_rotated.shape[0]

    def one_block(carry, index):
        key_acc, value_acc = carry
        start = index * BLOCK
        query_block, scores = block_scores(query_rotated, key_rot, segment, start, scale)
        probs = jnp.exp(scores - log_totals[index])
        d_probs = jnp.einsum(
            "qcgd,kcd->cgqk", d_heads, value_low, preferred_element_type=jnp.float32
        )
        delta = jnp.sum(probs * d_probs, axis=-1, keepdims=True)
        d_scores = (probs * (d_probs - delta)).astype(jnp.bfloat16)
        query_part = (
            jnp.einsum("cgqk,kcd->qcgd", d_scores, key_rot, preferred_element_type=jnp.float32)
            * scale
        )
        key_acc = (
            key_acc
            + jnp.einsum(
                "cgqk,qcgd->kcd", d_scores, query_block, preferred_element_type=jnp.float32
            )
            * scale
        )
        value_acc = value_acc + jnp.einsum(
            "cgqk,qcgd->kcd",
            probs.astype(jnp.bfloat16),
            d_heads,
            preferred_element_type=jnp.float32,
        )
        return ((key_acc, value_acc), query_part)

    empty = jnp.zeros(key_rot.shape, jnp.float32)
    (key_grads, value_grads), query_grads = lax.scan(
        one_block, (empty, empty), jnp.arange(total_count // BLOCK, dtype=jnp.int32)
    )
    return (query_grads.reshape(query_rotated.shape), key_grads, value_grads)


def norm_backward(value_heads, scale, gain, d_normed):
    weighted = d_normed * gain
    d_values = scale * weighted - value_heads * scale * scale * scale * jnp.mean(
        weighted * value_heads, axis=-1, keepdims=True
    )
    return (d_values, jnp.sum(d_normed * value_heads * scale, axis=0))


def fetch_attention(
    query_weight, key_projection_weight, value_projection_weight, output_weight, prenorm_gain
):
    return (
        lax.all_gather(query_weight, "dp", axis=0, tiled=True),
        lax.all_gather(key_projection_weight, "dp", axis=0, tiled=True),
        lax.all_gather(value_projection_weight, "dp", axis=0, tiled=True),
        lax.all_gather(output_weight, "dp", axis=0, tiled=True),
        lax.all_gather(prenorm_gain, "dp", axis=0, tiled=True),
    )


def fetch_feedforward(gate_weight, up_weight, down_weight, midnorm_gain):
    return (
        lax.all_gather(gate_weight, "dp", axis=0, tiled=True),
        lax.all_gather(up_weight, "dp", axis=0, tiled=True),
        lax.all_gather(down_weight, "dp", axis=0, tiled=True),
        lax.all_gather(midnorm_gain, "dp", axis=0, tiled=True),
    )


def body(
    tokens,
    cotangent,
    token_slots,
    lengths,
    query_weight,
    key_projection_weight,
    value_projection_weight,
    output_weight,
    gate_weight,
    up_weight,
    down_weight,
    prenorm_gain,
    midnorm_gain,
):
    tensor_size = lax.axis_size("tensor")
    micro_count, local_rows, width = tokens.shape
    group_rows = local_rows * tensor_size
    scale = 1.0 / math.sqrt(HEAD_SIZE)
    query_cols = query_weight.shape[1]
    kv_cols = key_projection_weight.shape[1]
    query_local = query_cols // HEAD_SIZE
    kv_local = kv_cols // HEAD_SIZE
    per_group = query_local // kv_local
    hidden_cols = gate_weight.shape[1]

    def attention_params():
        return fetch_attention(
            query_weight,
            key_projection_weight,
            value_projection_weight,
            output_weight,
            prenorm_gain,
        )

    def feedforward_params():
        return fetch_feedforward(gate_weight, up_weight, down_weight, midnorm_gain)

    query_acc = jnp.zeros((width, query_cols), jnp.float32)
    key_acc = jnp.zeros((width, kv_cols), jnp.float32)
    value_acc = jnp.zeros((width, kv_cols), jnp.float32)
    output_acc = jnp.zeros((query_cols, width), jnp.float32)
    gate_acc = jnp.zeros((width, hidden_cols), jnp.float32)
    upward_acc = jnp.zeros((width, hidden_cols), jnp.float32)
    down_acc = jnp.zeros((hidden_cols, width), jnp.float32)
    prenorm_acc = jnp.zeros((width,), jnp.float32)
    midnorm_acc = jnp.zeros((width,), jnp.float32)
    outputs_list = []
    grads_list = []
    for batch_index in range(micro_count):
        slots = token_slots[batch_index]
        sending = jnp.argsort(slots)
        slot_rows = (slots % local_rows)[sending]
        arrived_tokens, arrived_cot, arrived_slots = (
            lax.all_to_all(
                tokens[batch_index][sending],
                ("dp", "tensor"),
                split_axis=0,
                concat_axis=0,
                tiled=True,
            ),
            lax.all_to_all(
                cotangent[batch_index][sending],
                ("dp", "tensor"),
                split_axis=0,
                concat_axis=0,
                tiled=True,
            ),
            lax.all_to_all(slot_rows, ("dp", "tensor"), split_axis=0, concat_axis=0, tiled=True),
        )
        placing = jnp.argsort(arrived_slots)
        dealt_tokens = arrived_tokens[placing]
        dealt_cot = arrived_cot[placing]
        segment, positions = sequence_layout(lengths[batch_index, 0], group_rows)
        cosine_table, sine_table = rope_tables(positions, HEAD_SIZE)
        query_full, key_full, value_full, output_full, first_gain = attention_params()
        gain_one = first_gain.astype(jnp.float32)
        inputs = dealt_tokens.astype(jnp.float32)
        first_scale = rms_scale(inputs)
        first_normed_rows = (inputs * first_scale * gain_one).astype(jnp.bfloat16)
        normed_all = lax.all_gather(first_normed_rows, "tensor", axis=0, tiled=True)
        query_heads = jnp.dot(normed_all, query_full, preferred_element_type=jnp.float32)
        key_heads = jnp.dot(normed_all, key_full, preferred_element_type=jnp.float32)
        value_heads = jnp.dot(normed_all, value_full, preferred_element_type=jnp.float32)
        query_rotated = (
            apply_rotary(
                query_heads.reshape(group_rows, query_local, HEAD_SIZE), cosine_table, sine_table
            )
            .astype(jnp.bfloat16)
            .reshape(group_rows, kv_local, per_group, HEAD_SIZE)
        )
        key_rot = apply_rotary(
            key_heads.reshape(group_rows, kv_local, HEAD_SIZE), cosine_table, sine_table
        ).astype(jnp.bfloat16)
        value_low = value_heads.reshape(group_rows, kv_local, HEAD_SIZE).astype(jnp.bfloat16)
        heads, log_totals = attend_forward(query_rotated, key_rot, value_low, segment, scale)
        heads_flat = heads.reshape(group_rows, query_cols)
        residual = inputs + lax.psum_scatter(
            jnp.dot(heads_flat, output_full, preferred_element_type=jnp.float32).astype(
                jnp.bfloat16
            ),
            "tensor",
            scatter_dimension=0,
            tiled=True,
        ).astype(jnp.float32)
        gate_full, upward_full, down_full, second_gain = feedforward_params()
        gain_two = second_gain.astype(jnp.float32)
        second_scale = rms_scale(residual)
        normed_two = (residual * second_scale * gain_two).astype(jnp.bfloat16)
        normed_two_all = lax.all_gather(normed_two, "tensor", axis=0, tiled=True)
        gate = jnp.dot(normed_two_all, gate_full, preferred_element_type=jnp.float32)
        upward = jnp.dot(normed_two_all, upward_full, preferred_element_type=jnp.float32)
        sigmoid_gate = jax.nn.sigmoid(gate)
        silu_gate = gate * sigmoid_gate
        hidden = (silu_gate * upward).astype(jnp.bfloat16)
        layer_rows = residual + lax.psum_scatter(
            jnp.dot(hidden, down_full, preferred_element_type=jnp.float32).astype(jnp.bfloat16),
            "tensor",
            scatter_dimension=0,
            tiled=True,
        ).astype(jnp.float32)
        gate_full, upward_full, down_full, second_gain = feedforward_params()
        grad_rows = dealt_cot.astype(jnp.float32)
        out_grad_all = lax.all_gather(dealt_cot, "tensor", axis=0, tiled=True)
        down_acc = down_acc + outer_sum(hidden, out_grad_all)
        d_hidden = times_transposed(out_grad_all, down_full)
        d_gate = (d_hidden * upward * sigmoid_gate * (1.0 + gate * (1.0 - sigmoid_gate))).astype(
            jnp.bfloat16
        )
        d_upward = (d_hidden * silu_gate).astype(jnp.bfloat16)
        gate_acc = gate_acc + outer_sum(normed_two_all, d_gate)
        upward_acc = upward_acc + outer_sum(normed_two_all, d_upward)
        d_normed_two = lax.psum_scatter(
            (times_transposed(d_gate, gate_full) + times_transposed(d_upward, upward_full)).astype(
                jnp.bfloat16
            ),
            "tensor",
            scatter_dimension=0,
            tiled=True,
        ).astype(jnp.float32)
        d_through, d_gain_two = norm_backward(residual, second_scale, gain_two, d_normed_two)
        midnorm_acc = midnorm_acc + d_gain_two
        d_residual = grad_rows + d_through
        query_full, key_full, value_full, output_full, first_gain = attention_params()
        residual_grad_all = lax.all_gather(
            d_residual.astype(jnp.bfloat16), "tensor", axis=0, tiled=True
        )
        output_acc = output_acc + outer_sum(heads_flat, residual_grad_all)
        d_heads = (
            times_transposed(residual_grad_all, output_full)
            .astype(jnp.bfloat16)
            .reshape(group_rows, kv_local, per_group, HEAD_SIZE)
        )
        d_query_rot, d_key_rot, d_value = attend_backward(
            query_rotated, key_rot, value_low, d_heads, log_totals, segment, scale
        )
        d_query = (
            rotate_back(
                d_query_rot.reshape(group_rows, query_local, HEAD_SIZE), cosine_table, sine_table
            )
            .reshape(group_rows, query_cols)
            .astype(jnp.bfloat16)
        )
        d_key = (
            rotate_back(d_key_rot, cosine_table, sine_table)
            .reshape(group_rows, kv_cols)
            .astype(jnp.bfloat16)
        )
        d_value_low = d_value.reshape(group_rows, kv_cols).astype(jnp.bfloat16)
        query_acc = query_acc + outer_sum(normed_all, d_query)
        key_acc = key_acc + outer_sum(normed_all, d_key)
        value_acc = value_acc + outer_sum(normed_all, d_value_low)
        d_normed_one = lax.psum_scatter(
            (
                times_transposed(d_query, query_full)
                + times_transposed(d_key, key_full)
                + times_transposed(d_value_low, value_full)
            ).astype(jnp.bfloat16),
            "tensor",
            scatter_dimension=0,
            tiled=True,
        ).astype(jnp.float32)
        d_first, d_gain_one = norm_backward(inputs, first_scale, gain_one, d_normed_one)
        prenorm_acc = prenorm_acc + d_gain_one
        input_grads = (d_residual + d_first).astype(jnp.bfloat16)
        returned_out, returned_grad = (
            lax.all_to_all(
                layer_rows.astype(jnp.bfloat16)[arrived_slots],
                ("dp", "tensor"),
                split_axis=0,
                concat_axis=0,
                tiled=True,
            ),
            lax.all_to_all(
                input_grads[arrived_slots],
                ("dp", "tensor"),
                split_axis=0,
                concat_axis=0,
                tiled=True,
            ),
        )
        undoing = jnp.argsort(sending)
        outputs_list.append(returned_out[undoing])
        grads_list.append(returned_grad[undoing])
    shards = (
        lax.psum_scatter(
            query_acc.astype(jnp.bfloat16), "dp", scatter_dimension=0, tiled=True
        ).astype(jnp.float32),
        lax.psum_scatter(
            key_acc.astype(jnp.bfloat16), "dp", scatter_dimension=0, tiled=True
        ).astype(jnp.float32),
        lax.psum_scatter(
            value_acc.astype(jnp.bfloat16), "dp", scatter_dimension=0, tiled=True
        ).astype(jnp.float32),
        lax.psum_scatter(
            output_acc.astype(jnp.bfloat16), "dp", scatter_dimension=0, tiled=True
        ).astype(jnp.float32),
        lax.psum_scatter(
            gate_acc.astype(jnp.bfloat16), "dp", scatter_dimension=0, tiled=True
        ).astype(jnp.float32),
        lax.psum_scatter(
            upward_acc.astype(jnp.bfloat16), "dp", scatter_dimension=0, tiled=True
        ).astype(jnp.float32),
        lax.psum_scatter(
            down_acc.astype(jnp.bfloat16), "dp", scatter_dimension=0, tiled=True
        ).astype(jnp.float32),
        lax.psum_scatter(
            prenorm_acc.astype(jnp.bfloat16), "dp", scatter_dimension=0, tiled=True
        ).astype(jnp.float32),
        lax.psum_scatter(
            midnorm_acc.astype(jnp.bfloat16), "dp", scatter_dimension=0, tiled=True
        ).astype(jnp.float32),
    )
    gain_first, gain_second = lax.psum((shards[7], shards[8]), "tensor")
    return (
        jnp.stack(outputs_list, axis=0),
        jnp.stack(grads_list, axis=0),
        shards[0],
        shards[1],
        shards[2],
        shards[3],
        shards[4],
        shards[5],
        shards[6],
        gain_first,
        gain_second,
    )


def solution(mesh):
    placed = (
        P(None, ("dp", "tensor"), None),
        P(None, ("dp", "tensor"), None),
        P(None, ("dp", "tensor")),
        P(None, "dp", None),
        P("dp", "tensor"),
        P("dp", "tensor"),
        P("dp", "tensor"),
        P(("tensor", "dp"), None),
        P("dp", "tensor"),
        P("dp", "tensor"),
        P(("tensor", "dp"), None),
        P("dp"),
        P("dp"),
    )
    return jax.shard_map(
        body,
        mesh=mesh,
        in_specs=placed,
        out_specs=(
            P(None, ("dp", "tensor"), None),
            P(None, ("dp", "tensor"), None),
            P("dp", "tensor"),
            P("dp", "tensor"),
            P("dp", "tensor"),
            P(("tensor", "dp"), None),
            P("dp", "tensor"),
            P("dp", "tensor"),
            P(("tensor", "dp"), None),
            P("dp"),
            P("dp"),
        ),
        check_vma=False,
    )
```

profile of v0, /device:TPU:0, one launch (start us, length us, event | category | flops | bytes accessed | tf_op | source)
XLA Modules:
  0.0 1923.5 jit_solution(2866556886310624779)
XLA Ops:
  31.5 25.3 %all-gather.2 = bf16[8,1,256]{2,1,0:T(2,128)(2,1)S(1)} all-gather(bf16[1,1,256]{2,1,0:T(2,128)(2,1)S(1)} %reshape.814), channel_id=1, replica_groups=mesh['dp'=8,'tensor'=4] {'dp'}, dimensions={0}, use_global_device_ids=true | all-gather | bytes 4608 | tf_op jit(solution)/shard_map/all_gather | solution.py:158
  69.9 20.1 %all-gather.20.cloned.1.call-done = bf16[512,2048]{1,0:T(8,128)(2,1)} async-done(((bf16[128,2048]{1,0:T(8,128)(2,1)}), bf16[512,2048]{1,0:T(8,128)(2,1)}) %all-gather.20.cloned.1.call-update) | async-done | bytes 2097168 | tf_op jit(solution)/shard_map/all_gather | solution.py:251
  98.7 33.7 %all-gather.24.cloned.1.call-done = bf16[2048,256]{1,0:T(8,128)(2,1)} async-done(((bf16[256,256]{1,0:T(8,128)(2,1)}), bf16[2048,256]{1,0:T(8,128)(2,1)}) %all-gather.24.cloned.1.call-update) | async-done | bytes 1048592 | tf_op jit(solution)/shard_map/all_gather | solution.py:155
  138.3 35.0 %all-gather.22.cloned.1.call-done = bf16[2048,256]{1,0:T(8,128)(2,1)} async-done(((bf16[256,256]{1,0:T(8,128)(2,1)}), bf16[2048,256]{1,0:T(8,128)(2,1)}) %all-gather.22.cloned.1.call-update) | async-done | bytes 1048592 | tf_op jit(solution)/shard_map/all_gather | solution.py:156
  176.0 47.4 %all-gather.28.cloned.1.call-done = bf16[512,2048]{1,0:T(8,128)(2,1)} async-done(((bf16[64,2048]{1,0:T(8,128)(2,1)}), bf16[512,2048]{1,0:T(8,128)(2,1)}) %all-gather.28.cloned.1.call-update) | async-done | bytes 2097168 | tf_op jit(solution)/shard_map/all_gather | solution.py:157
  264.2 19.9 %all_to_all.126 = bf16[32,4,2048]{2,1,0:T(4,128)(2,1)S(1)} all-to-all(bf16[32,4,2048]{2,1,0:T(4,128)(2,1)S(1)} %all_to_all.104), channel_id=1, replica_groups=mesh['dp'=8,'tensor'=4] {'dp','tensor'}, dimensions={0} | all-to-all | bytes 1048576 | tf_op jit(solution)/shard_map/all_to_all | solution.py:232
  289.5 127.3 %all-gather.32.cloned.1.call-done = bf16[2048,2048]{1,0:T(8,128)(2,1)} async-done(((bf16[256,2048]{1,0:T(8,128)(2,1)}), bf16[2048,2048]{1,0:T(8,128)(2,1)}) %all-gather.32.cloned.1.call-update) | async-done | bytes 8388624 | tf_op jit(solution)/shard_map/all_gather | solution.py:164
  427.4 114.9 %all-gather.34.cloned.1.call-done = bf16[2048,2048]{1,0:T(8,128)(2,1)} async-done(((bf16[256,2048]{1,0:T(8,128)(2,1)}), bf16[2048,2048]{1,0:T(8,128)(2,1)}) %all-gather.34.cloned.1.call-update) | async-done | bytes 8388624 | tf_op jit(solution)/shard_map/all_gather | solution.py:165
  565.2 127.3 %all-gather.36.cloned.1.call-done = bf16[2048,2048]{1,0:T(8,128)(2,1)} async-done(((bf16[256,2048]{1,0:T(8,128)(2,1)}), bf16[2048,2048]{1,0:T(8,128)(2,1)}) %all-gather.36.cloned.1.call-update) | async-done | bytes 8388624 | tf_op jit(solution)/shard_map/all_gather | solution.py:166
  725.1 29.7 %reduce-scatter.24.cloned.1.call-done = bf16[128,2048]{1,0:T(8,128)(2,1)} async-done(((bf16[512,2048]{1,0:T(8,128)(2,1)}), bf16[128,2048]{1,0:T(8,128)(2,1)}) %reduce-scatter.24.cloned.1.call-update) | async-done | bytes 524304 | tf_op jit(solution)/shard_map/reduce_scatter | solution.py:303
  759.3 22.7 %all-gather.42.cloned.1.call-done = bf16[512,2048]{1,0:T(8,128)(2,1)} async-done(((bf16[128,2048]{1,0:T(8,128)(2,1)}), bf16[512,2048]{1,0:T(8,128)(2,1)}) %all-gather.42.cloned.1.call-update) | async-done | bytes 2097168 | tf_op jit(solution)/shard_map/all_gather | solution.py:315
  842.3 21.8 %all-gather.38.cloned.1.call-done = bf16[512,2048]{1,0:T(8,128)(2,1)} async-done(((bf16[128,2048]{1,0:T(8,128)(2,1)}), bf16[512,2048]{1,0:T(8,128)(2,1)}) %all-gather.38.cloned.1.call-update) | async-done | bytes 2097168 | tf_op jit(solution)/shard_map/all_gather | solution.py:251
  895.0 20.4 %reduce-scatter.20.cloned.1.call-done = bf16[128,2048]{1,0:T(8,128)(2,1)} async-done(((bf16[512,2048]{1,0:T(8,128)(2,1)}), bf16[128,2048]{1,0:T(8,128)(2,1)}) %reduce-scatter.20.cloned.1.call-update) | async-done | bytes 524304 | tf_op jit(solution)/shard_map/reduce_scatter | solution.py:268
  917.2 32.6 %reduce-scatter.18.cloned.1.call-done = bf16[128,2048]{1,0:T(8,128)(2,1)} async-done(((bf16[512,2048]{1,0:T(8,128)(2,1)}), bf16[128,2048]{1,0:T(8,128)(2,1)}) %reduce-scatter.18.cloned.1.call-update) | async-done | bytes 524304 | tf_op jit(solution)/shard_map/reduce_scatter | solution.py:286
  954.9 20.0 %all_to_all.127 = bf16[32,4,2048]{2,1,0:T(4,128)(2,1)S(1)} all-to-all(bf16[32,4,2048]{2,1,0:T(4,128)(2,1)S(1)} %all_to_all.110), channel_id=1, replica_groups=mesh['dp'=8,'tensor'=4] {'dp','tensor'}, dimensions={0} | all-to-all | bytes 1048576 | tf_op jit(solution)/shard_map/all_to_all | solution.py:232
  1036.4 31.3 %reduce-scatter.28.cloned.1.call-done = bf16[128,2048]{1,0:T(8,128)(2,1)} async-done(((bf16[512,2048]{1,0:T(8,128)(2,1)}), bf16[128,2048]{1,0:T(8,128)(2,1)}) %reduce-scatter.28.cloned.1.call-update) | async-done | bytes 524304 | tf_op jit(solution)/shard_map/reduce_scatter | solution.py:303
  1072.2 22.6 %all-gather.44.cloned.1.call-done = bf16[512,2048]{1,0:T(8,128)(2,1)} async-done(((bf16[128,2048]{1,0:T(8,128)(2,1)}), bf16[512,2048]{1,0:T(8,128)(2,1)}) %all-gather.44.cloned.1.call-update) | async-done | bytes 2097168 | tf_op jit(solution)/shard_map/all_gather | solution.py:315
  1289.5 28.4 %reduce-scatter.34.cloned.1.call-done = bf16[256,256]{1,0:T(8,128)(2,1)} async-done(((bf16[2048,256]{1,0:T(8,128)(2,1)}), bf16[256,256]{1,0:T(8,128)(2,1)}) %reduce-scatter.34.cloned.1.call-update) | async-done | bytes 131088 | tf_op jit(solution)/shard_map/reduce_scatter | solution.py:379
  1319.5 68.5 %reduce-scatter.38.cloned.1.call-done = bf16[64,2048]{1,0:T(8,128)(2,1)} async-done(((bf16[512,2048]{1,0:T(8,128)(2,1)}), bf16[64,2048]{1,0:T(8,128)(2,1)}) %reduce-scatter.38.cloned.1.call-update) | async-done | bytes 262160 | tf_op jit(solution)/shard_map/reduce_scatter | solution.py:385
  1389.8 68.4 %reduce-scatter.32.cloned.1.call-done = bf16[256,512]{1,0:T(8,128)(2,1)} async-done(((bf16[2048,512]{1,0:T(8,128)(2,1)}), bf16[256,512]{1,0:T(8,128)(2,1)}) %reduce-scatter.32.cloned.1.call-update) | async-done | bytes 262160 | tf_op jit(solution)/shard_map/reduce_scatter | solution.py:376
  1460.0 20.0 %all-reduce.3 = (bf16[2048]{0:T(1024)(128)(2,1)S(1)}, bf16[2048]{0:T(1024)(128)(2,1)S(1)}) all-reduce(bf16[2048]{0:T(1024)(128)(2,1)S(1)} %add_convert_fusion.16, bf16[2048]{0:T(1024)(128)(2,1)S(1)} %add_convert_fusion.15), channel_id=19, replica_groups=mesh['dp'=8,'tensor'=4] {'dp'}, use_global_device_ids=true, to_apply=%region_43.44.clone | all-reduce | flops 4096 | bytes 16384
  1490.3 119.7 %reduce-scatter.42.cloned.1.call-done = bf16[256,2048]{1,0:T(8,128)(2,1)} async-done(((bf16[2048,2048]{1,0:T(8,128)(2,1)}), bf16[256,2048]{1,0:T(8,128)(2,1)}) %reduce-scatter.42.cloned.1.call-update) | async-done | bytes 1048592 | tf_op jit(solution)/shard_map/reduce_scatter | solution.py:391
  1612.8 149.3 %reduce-scatter.40.cloned.1.call-done = bf16[256,2048]{1,0:T(8,128)(2,1)} async-done(((bf16[2048,2048]{1,0:T(8,128)(2,1)}), bf16[256,2048]{1,0:T(8,128)(2,1)}) %reduce-scatter.40.cloned.1.call-update) | async-done | bytes 1048592 | tf_op jit(solution)/shard_map/reduce_scatter | solution.py:388
  1764.9 148.7 %reduce-scatter.44.cloned.1.call-done = bf16[256,2048]{1,0:T(8,128)(2,1)} async-done(((bf16[2048,2048]{1,0:T(8,128)(2,1)}), bf16[256,2048]{1,0:T(8,128)(2,1)}) %reduce-scatter.44.cloned.1.call-update) | async-done | bytes 1048592 | tf_op jit(solution)/shard_map/reduce_scatter | solution.py:394
  (573 shorter events, 551.1 us)
Async XLA Ops:
  63.0 69.3 %all-gather.24.cloned.1.call-start = ((), (), s32[]{:S(2)}) async-start(), calls=%async_computation.27 | async-start | bytes 1179648 | tf_op jit(solution)/shard_map/all_gather | solution.py:155
  63.8 109.5 %all-gather.22.cloned.1.call-start = ((), (), s32[]{:S(2)}) async-start(), calls=%async_computation.26 | async-start | bytes 1179648 | tf_op jit(solution)/shard_map/all_gather | solution.py:156
  64.3 159.0 %all-gather.28.cloned.1.call-start = ((), (), s32[]{:S(2)}) async-start(), calls=%async_computation.29 | async-start | bytes 2359296 | tf_op jit(solution)/shard_map/all_gather | solution.py:157
  64.9 192.7 %reduce-scatter.16.cloned.1.call-start = ((), (), s32[]{:S(2)}) async-start(), calls=%async_computation.30 | async-start | bytes 2621440 | tf_op jit(solution)/shard_map/reduce_scatter | solution.py:268
  261.1 155.6 %all-gather.32.cloned.1.call-start = ((), (), s32[]{:S(2)}) async-start(), calls=%async_computation.32 | async-start | bytes 9437184 | tf_op jit(solution)/shard_map/all_gather | solution.py:164
  261.9 280.4 %all-gather.34.cloned.1.call-start = ((), (), s32[]{:S(2)}) async-start(), calls=%async_computation.33 | async-start | bytes 9437184 | tf_op jit(solution)/shard_map/all_gather | solution.py:165
  262.6 302.5 %all-gather.46.cloned.1.call-start = ((), (), s32[]{:S(2)}) async-start(), calls=%async_computation.53 | async-start | bytes 2621440 | tf_op jit(solution)/shard_map/all_gather | solution.py:294
  286.2 406.3 %all-gather.36.cloned.1.call-start = ((), (), s32[]{:S(2)}) async-start(), calls=%async_computation.34 | async-start | bytes 9437184 | tf_op jit(solution)/shard_map/all_gather | solution.py:166
  286.9 467.9 %reduce-scatter.24.cloned.1.call-start = ((), (), s32[]{:S(2)}) async-start(), calls=%async_computation.40 | async-start | bytes 2621440 | tf_op jit(solution)/shard_map/reduce_scatter | solution.py:303
  759.3 79.2 %reduce-scatter.26.cloned.1.call-start = ((), (), s32[]{:S(2)}) async-start(), calls=%async_computation.42 | async-start | bytes 2621440 | tf_op jit(solution)/shard_map/reduce_scatter | solution.py:343
  841.3 74.1 %reduce-scatter.20.cloned.1.call-start = ((), (), s32[]{:S(2)}) async-start(), calls=%async_computation.37 | async-start | bytes 2621440 | tf_op jit(solution)/shard_map/reduce_scatter | solution.py:268
  883.8 66.0 %reduce-scatter.18.cloned.1.call-start = ((), (), s32[]{:S(2)}) async-start(), calls=%async_computation.35 | async-start | bytes 2621440 | tf_op jit(solution)/shard_map/reduce_scatter | solution.py:286
  893.7 87.2 %all-gather.40.cloned.1.call-start = ((), (), s32[]{:S(2)}) async-start(), calls=%async_computation.38 | async-start | bytes 2621440 | tf_op jit(solution)/shard_map/all_gather | solution.py:280
  976.9 90.8 %reduce-scatter.28.cloned.1.call-start = ((), (), s32[]{:S(2)}) async-start(), calls=%async_computation.43 | async-start | bytes 2621440 | tf_op jit(solution)/shard_map/reduce_scatter | solution.py:303
  1072.1 162.9 %reduce-scatter.30.cloned.1.call-start = ((), (), s32[]{:S(2)}) async-start(), calls=%async_computation.45 | async-start | bytes 2621440 | tf_op jit(solution)/shard_map/reduce_scatter | solution.py:343
  1111.9 124.5 %reduce-scatter.22.cloned.1.call-start = ((), (), s32[]{:S(2)}) async-start(), calls=%async_computation.39 | async-start | bytes 2621440 | tf_op jit(solution)/shard_map/reduce_scatter | solution.py:286
  1122.5 165.4 %reduce-scatter.36.cloned.1.call-start = ((), (), s32[]{:S(2)}) async-start(), calls=%async_computation.48 | async-start | bytes 1179648 | tf_op jit(solution)/shard_map/reduce_scatter | solution.py:382
  1127.4 190.5 %reduce-scatter.34.cloned.1.call-start = ((), (), s32[]{:S(2)}) async-start(), calls=%async_computation.47 | async-start | bytes 1179648 | tf_op jit(solution)/shard_map/reduce_scatter | solution.py:379
  1131.3 256.7 %reduce-scatter.38.cloned.1.call-start = ((), (), s32[]{:S(2)}) async-start(), calls=%async_computation.49 | async-start | bytes 2359296 | tf_op jit(solution)/shard_map/reduce_scatter | solution.py:385
  1137.2 321.0 %reduce-scatter.32.cloned.1.call-start = ((), (), s32[]{:S(2)}) async-start(), calls=%async_computation.46 | async-start | bytes 2359296 | tf_op jit(solution)/shard_map/reduce_scatter | solution.py:376
  1142.6 467.5 %reduce-scatter.42.cloned.1.call-start = ((), (), s32[]{:S(2)}) async-start(), calls=%async_computation.51 | async-start | bytes 9437184 | tf_op jit(solution)/shard_map/reduce_scatter | solution.py:391
  1165.1 597.1 %reduce-scatter.40.cloned.1.call-start = ((), (), s32[]{:S(2)}) async-start(), calls=%async_computation.50 | async-start | bytes 9437184 | tf_op jit(solution)/shard_map/reduce_scatter | solution.py:388
  1186.0 727.6 %reduce-scatter.44.cloned.1.call-start = ((), (), s32[]{:S(2)}) async-start(), calls=%async_computation.52 | async-start | bytes 9437184 | tf_op jit(solution)/shard_map/reduce_scatter | solution.py:394
  1276.7 211.0 %all-to-all-start.5 = ((bf16[32,4,2048]{2,1,0:T(4,128)(2,1)}), bf16[32,4,2048]{2,1,0:T(4,128)(2,1)S(1)}, u32[]{:S(2)}, u32[]{:S(2)}) async-start(bf16[32,4,2048]{2,1,0:T(4,128)(2,1)} %all_to_all.101), calls=%async_computation.9 | async-start | bytes 1048576 | tf_op jit(solution)/shard_map/all_to_all | solution.py:357
  (154 other events, 2719.0 us)
Sparse Core Ops, SparseCore 0:
  10.1 53.9 all-gather.25
  92.1 40.2 all-gather.23
  134.3 38.8 all-gather.21
  175.3 48.0 all-gather.27
  227.7 29.9 reduce-scatter.15
  261.3 28.1 all-gather.29
  291.8 124.9 all-gather.31
  419.1 123.1 all-gather.33
  567.5 124.9 all-gather.35
  725.2 29.6 reduce-scatter.23
  801.3 37.0 reduce-scatter.25
  883.9 31.4 reduce-scatter.19
  918.4 31.4 reduce-scatter.17
  953.7 27.1 all-gather.39
  1036.2 31.4 reduce-scatter.27
  1112.0 31.4 reduce-scatter.29
  1146.1 31.4 reduce-scatter.21
  1181.5 67.0 reduce-scatter.35
  1253.0 64.8 reduce-scatter.33
  1321.3 66.6 reduce-scatter.37
  1391.4 66.7 reduce-scatter.31
  1461.8 148.1 reduce-scatter.41
  1614.1 147.9 reduce-scatter.39
  1765.6 147.9 reduce-scatter.43
  (6 shorter events, 134.1 us)
where the time goes:
time: 1930 us; the launch traced here: 1920 us
  waiting for transfers between devices  1370 us (71%)
  matrix products  248 us (13%)
  blocking collectives  110 us (6%)
  other arithmetic  77.1 us (4%)
  local copies, waits for them, and re-layouts  65.2 us (3%)
  starting transfers between devices  33.5 us (2%)
    reduce_scatter x1, waiting for transfers between devices, body(): lax.psum_scatter(gate_acc.astype(jnp.bfloat16), 'dp', scatter_dimension=0...  149 us
    reduce_scatter x1, waiting for transfers between devices, body(): lax.psum_scatter(down_acc.astype(jnp.bfloat16), 'dp', scatter_dimension=0...  149 us
    all_gather x1, waiting for transfers between devices, fetch_feedforward(): lax.all_gather(down_weight, 'dp', axis=0, tiled=True)  127 us
    all_gather x1, waiting for transfers between devices, fetch_feedforward(): lax.all_gather(gate_weight, 'dp', axis=0, tiled=True)  127 us
    reduce_scatter x1, waiting for transfers between devices, body(): lax.psum_scatter(upward_acc.astype(jnp.bfloat16), 'dp', scatter_dimension...  120 us
    all_gather x1, waiting for transfers between devices, fetch_feedforward(): lax.all_gather(up_weight, 'dp', axis=0, tiled=True)  115 us
    dot_general x14, matrix products, times_transposed(): lax.dot_general(left, right, (((1,), (1,)), ((), ())), preferred_element_...  80.7 us
    dot_general x14, matrix products, outer_sum(): lax.dot_general(left, right, (((0,), (0,)), ((), ())), preferred_element_...  76.6 us
  transfers between devices with their start and end apart: 38, of which 32 were waited for; matrix products, arithmetic and copies ran while one was open for 11% of the time, Pallas kernels for 0%

commit v1 on v0

v1 whole, which is shorter than its diff:
```python
import math

import jax
import jax.numpy as jnp
from jax import lax
from jax.sharding import Mesh, PartitionSpec as P

HEAD_SIZE = 256
EPSILON = 1e-06
ROPE_BASE = 1000042.0
NEGATIVE = -1e30
CHUNKS = 2
F32 = jnp.float32
BF16 = jnp.bfloat16

SWAP = [(0, 1), (1, 0)]
DIAGONAL = [(0, 3), (3, 0), (1, 2), (2, 1)]
Z_NEAR = [(0, 1), (1, 0), (2, 3), (3, 2)]
Z_FAR = [(0, 2), (2, 0), (1, 3), (3, 1)]
Z_ACROSS = [(0, 3), (3, 0), (1, 2), (2, 1)]
Z_MIDDLE = [(1, 2), (2, 1)]
Z_OUTWARD = [(2, 3), (1, 0)]
Z_INWARD = [(3, 2), (0, 1)]


def rms_scale(values):
    return lax.rsqrt(jnp.mean(values * values, axis=-1, keepdims=True) + EPSILON)


def rope_tables(positions, head):
    half = head // 2
    frequency = jnp.exp(jnp.arange(half, dtype=F32) * (-2.0 * math.log(ROPE_BASE) / head))
    angles = positions.astype(F32)[:, None] * frequency[None, :]
    return (jnp.cos(angles), jnp.sin(angles))


def rotate(values, cosine, sine):
    half = values.shape[-1] // 2
    first, second = values[..., :half], values[..., half:]
    cosine, sine = cosine[:, None, :], sine[:, None, :]
    return jnp.concatenate(
        [first * cosine - second * sine, second * cosine + first * sine], axis=-1
    )


def sequence_layout(lens, total):
    rows = jnp.arange(total, dtype=jnp.int32)
    ends = jnp.cumsum(lens)
    segment = jnp.sum((rows[:, None] >= ends[None, :]).astype(jnp.int32), axis=1)
    starts = ends - lens
    which = segment[:, None] == jnp.arange(lens.shape[0], dtype=jnp.int32)[None, :]
    begin = jnp.sum(jnp.where(which, starts[None, :], 0), axis=1)
    return (segment, rows - begin)


def mm(left, right):
    return jnp.dot(left, right, preferred_element_type=F32)


def outer_sum(left, right):
    return lax.dot_general(left, right, (((0,), (0,)), ((), ())), preferred_element_type=F32)


def times_transposed(left, right):
    return lax.dot_general(left, right, (((1,), (1,)), ((), ())), preferred_element_type=F32)


def attend_forward(query, key, value, allowed, scale):
    scores = jnp.einsum("qcgd,kcd->cgqk", query, key, preferred_element_type=F32) * scale
    scores = jnp.where(allowed, scores, NEGATIVE)
    row_max = jnp.max(scores, axis=-1, keepdims=True)
    expo = jnp.exp(scores - row_max)
    row_total = jnp.sum(expo, axis=-1, keepdims=True)
    probs = (expo / row_total).astype(BF16)
    heads = jnp.einsum("cgqk,kcd->qcgd", probs, value, preferred_element_type=F32)
    return (heads.astype(BF16), row_max + jnp.log(row_total))


def attend_backward(query, key, value, d_heads, log_totals, allowed, scale):
    scores = jnp.einsum("qcgd,kcd->cgqk", query, key, preferred_element_type=F32) * scale
    scores = jnp.where(allowed, scores, NEGATIVE)
    probs = jnp.exp(scores - log_totals)
    d_probs = jnp.einsum("qcgd,kcd->cgqk", d_heads, value, preferred_element_type=F32)
    delta = jnp.sum(probs * d_probs, axis=-1, keepdims=True)
    d_scores = (probs * (d_probs - delta)).astype(BF16)
    d_query = jnp.einsum("cgqk,kcd->qcgd", d_scores, key, preferred_element_type=F32) * scale
    d_key = jnp.einsum("cgqk,qcgd->kcd", d_scores, query, preferred_element_type=F32) * scale
    d_value = jnp.einsum(
        "cgqk,qcgd->kcd", probs.astype(BF16), d_heads, preferred_element_type=F32
    )
    return (d_query, d_key, d_value)


def norm_backward(values, scale, gain, d_normed):
    weighted = d_normed * gain
    d_values = scale * weighted - values * scale * scale * scale * jnp.mean(
        weighted * values, axis=-1, keepdims=True
    )
    return (d_values, jnp.sum(d_normed * values * scale, axis=0))


def take(array, index, axis=0):
    return lax.dynamic_index_in_dim(array, index, axis, keepdims=False)


def put(array, piece, index, axis=0):
    return lax.dynamic_update_index_in_dim(array, piece, index, axis)


def in_order(position, own, other, axis=0):
    first = jnp.where(position == 0, own, other)
    second = jnp.where(position == 0, other, own)
    return jnp.stack([first, second], axis=axis)


def gather_z(piece):
    size, here = lax.axis_size("z"), lax.axis_index("z")
    if size != 4:
        return lax.all_gather(piece, "z", axis=0)
    far = lax.ppermute(piece, "z", Z_FAR)
    near = lax.ppermute(piece, "z", Z_NEAR)
    middle = lax.ppermute(piece, "z", Z_MIDDLE)
    outward = lax.ppermute(far, "z", Z_OUTWARD)
    across = jnp.where((here == 1) | (here == 2), middle, outward)
    whole = jnp.zeros((size,) + piece.shape, piece.dtype)
    for step, part in enumerate((piece, near, far, across)):
        whole = put(whole, part, here ^ step)
    return whole


def reduce_z(parts):
    size, here = lax.axis_size("z"), lax.axis_index("z")
    if size != 4:
        return lax.psum_scatter(parts, "z", scatter_dimension=0).astype(F32)
    own, near, far, across = [take(parts, here ^ step) for step in range(4)]
    inward = lax.ppermute(across, "z", Z_INWARD)
    from_near = lax.ppermute(near, "z", Z_NEAR)
    from_middle = lax.ppermute(across, "z", Z_MIDDLE)
    relay = (far.astype(F32) + inward.astype(F32)).astype(BF16)
    from_far = lax.ppermute(relay, "z", Z_FAR)
    return (
        own.astype(F32)
        + from_near.astype(F32)
        + from_middle.astype(F32)
        + from_far.astype(F32)
    )


def gather_tensor(rows):
    here_y, here_c = lax.axis_index("y"), lax.axis_index("c")
    beside = lax.ppermute(rows, "y", SWAP)
    pieces = (
        (rows, here_y, here_c),
        (beside, 1 - here_y, here_c),
        (lax.ppermute(rows, "c", SWAP), here_y, 1 - here_c),
        (lax.ppermute(beside, "c", SWAP), 1 - here_y, 1 - here_c),
    )
    whole = jnp.zeros((rows.shape[0], 4) + rows.shape[1:], rows.dtype)
    for piece, at_y, at_c in pieces:
        whole = put(whole, piece, 2 * at_y + at_c, axis=1)
    return whole


def reduce_tensor(parts):
    here_y, here_c = lax.axis_index("y"), lax.axis_index("c")
    micro, _, rows, width = parts.shape
    parts = parts.reshape(micro, 2, 2, rows, width)
    arrived = lax.ppermute(take(parts, 1 - here_c, 2), "c", SWAP)
    both = take(parts, here_c, 2).astype(F32) + arrived.astype(F32)
    sent = lax.ppermute(take(both, 1 - here_y, 1).astype(BF16), "y", SWAP)
    return take(both, here_y, 1) + sent.astype(F32)


def gather_eight(rows):
    planes = (
        rows,
        lax.ppermute(rows, "x", SWAP),
        lax.ppermute(rows, "y", SWAP),
        lax.ppermute(rows, ("x", "y"), DIAGONAL),
    )
    return jnp.concatenate(planes + tuple(lax.ppermute(plane, "c", SWAP) for plane in planes))


def reduce_eight(parts):
    parts = parts.reshape((8, parts.shape[0] // 8) + parts.shape[1:])
    arrived = lax.ppermute(parts[4:], "c", SWAP)
    sums = parts[:4].astype(F32) + arrived.astype(F32)
    low = sums[1:].astype(BF16)
    return (
        sums[0]
        + lax.ppermute(low[0], "x", SWAP).astype(F32)
        + lax.ppermute(low[1], "y", SWAP).astype(F32)
        + lax.ppermute(low[2], ("x", "y"), DIAGONAL).astype(F32)
    )


def gather_gains(gains):
    size, here = lax.axis_size("z"), lax.axis_index("z")
    pair = in_order(lax.axis_index("x"), gains, lax.ppermute(gains, "x", SWAP))
    if size != 4:
        whole = lax.all_gather(pair, "z", axis=0)
    else:
        whole = jnp.zeros((size,) + pair.shape, pair.dtype)
        whole = put(whole, pair, here)
        for step, pairs in ((1, Z_NEAR), (2, Z_FAR), (3, Z_ACROSS)):
            whole = put(whole, lax.ppermute(pair, "z", pairs), here ^ step)
    return jnp.moveaxis(whole, 2, 0).reshape(gains.shape[0], -1)


def reduce_gains(grads):
    size, here_z, here_x = lax.axis_size("z"), lax.axis_index("z"), lax.axis_index("x")
    parts = grads.reshape(grads.shape[0], size, 2, -1)
    parts = take(parts, here_x, 2) + lax.ppermute(take(parts, 1 - here_x, 2), "x", SWAP)
    if size != 4:
        total = lax.psum_scatter(parts, "z", scatter_dimension=1)
    else:
        total = take(parts, here_z, 1)
        for step, pairs in ((1, Z_NEAR), (2, Z_FAR), (3, Z_ACROSS)):
            total = total + lax.ppermute(take(parts, here_z ^ step, 1), "z", pairs)
    total = total + lax.ppermute(total, "c", SWAP)
    return total + lax.ppermute(total, "y", SWAP)


def body(
    tokens,
    cotangent,
    token_slots,
    lengths,
    query_weight,
    key_projection_weight,
    value_projection_weight,
    output_weight,
    gate_weight,
    up_weight,
    down_weight,
    prenorm_gain,
    midnorm_gain,
):
    z_size = lax.axis_size("z")
    here_x = lax.axis_index("x")
    devices = 8 * z_size
    micro, local_rows, width = tokens.shape
    flat_rows = micro * local_rows
    sends = local_rows // devices
    group_rows = 4 * local_rows
    all_rows = micro * group_rows
    scale = 1.0 / math.sqrt(HEAD_SIZE)
    query_cols = query_weight.shape[1]
    kv_cols = key_projection_weight.shape[1]
    query_local = query_cols // HEAD_SIZE
    kv_local = kv_cols // HEAD_SIZE
    per_group = query_local // kv_local
    fused_cols = query_cols + 2 * kv_cols
    shard_rows = query_weight.shape[0]
    hidden_cols = gate_weight.shape[1]
    block = hidden_cols // (2 * z_size)
    piece = block // CHUNKS
    chunk_cols = z_size * piece
    everywhere = ("z", "x", "y", "c")

    rank = jnp.sum(
        (token_slots[:, None, :] < token_slots[:, :, None]).astype(jnp.int32), axis=2
    )
    order = (
        (rank // sends) * (micro * sends)
        + jnp.arange(micro, dtype=jnp.int32)[:, None] * sends
        + rank % sends
    ).reshape(flat_rows)
    places = jnp.arange(flat_rows, dtype=jnp.int32)
    to_send = (places[:, None] == order[None, :]).astype(BF16)
    local_slot = (token_slots % local_rows).reshape(flat_rows)
    sent_slots = jnp.sum(
        jnp.where(places[:, None] == order[None, :], local_slot[None, :], 0), axis=1
    )

    def exchange(rows):
        return lax.all_to_all(
            rows.reshape((devices, micro * sends) + rows.shape[1:]),
            everywhere,
            split_axis=0,
            concat_axis=0,
            tiled=True,
        ).reshape(rows.shape)

    arrived_slots = exchange(sent_slots)
    arrived_tokens = exchange(mm(to_send, tokens.reshape(flat_rows, width)).astype(BF16))
    arrived_micro = (places // sends) % micro
    to_place = (
        (arrived_slots + arrived_micro * local_rows)[:, None] == places[None, :]
    ).astype(BF16)

    gains = gather_gains(jnp.stack([prenorm_gain, midnorm_gain])).astype(F32)
    gain_one, gain_two = gains[0:1], gains[1:2]

    fused_shard = jnp.concatenate(
        [query_weight, key_projection_weight, value_projection_weight], axis=1
    )
    fused_pair = in_order(here_x, fused_shard, lax.ppermute(fused_shard, "x", SWAP))
    output_pair = in_order(here_x, output_weight, lax.ppermute(output_weight, "x", SWAP))
    fused_full = gather_z(fused_pair).reshape(width, fused_cols)
    output_full = gather_z(output_pair).reshape(query_cols, width)

    def by_parity(weight):
        blocks = weight.reshape(shard_rows, z_size, 2, CHUNKS, piece)
        return (blocks[:, :, 0], blocks[:, :, 1])

    gate_parts, up_parts = by_parity(gate_weight), by_parity(up_weight)
    ff_shards = []
    for chunk in range(CHUNKS):
        even, odd = [
            jnp.concatenate(
                [
                    parts[parity][:, :, chunk].reshape(shard_rows, chunk_cols)
                    for parts in (gate_parts, up_parts)
                ],
                axis=1,
            )
            for parity in range(2)
        ]
        kept = jnp.where(here_x == 0, even, odd)
        leaving = jnp.where(here_x == 0, odd, even)
        ff_shards.append(
            (
                in_order(here_x, kept, lax.ppermute(leaving, "x", SWAP)),
                down_weight[chunk * piece : (chunk + 1) * piece],
            )
        )

    inputs = outer_sum(to_place, arrived_tokens)
    first_scale = rms_scale(inputs)
    first_normed = (inputs * first_scale * gain_one).astype(BF16)
    normed_all = gather_tensor(first_normed.reshape(micro, local_rows, width)).reshape(
        all_rows, width
    )
    fused_heads = mm(normed_all, fused_full)
    saved = []
    heads_list = []
    for index in range(micro):
        segment, positions = sequence_layout(lengths[index, 0], group_rows)
        cosine, sine = rope_tables(positions, HEAD_SIZE)
        row_ids = jnp.arange(group_rows, dtype=jnp.int32)
        allowed = (segment[:, None] == segment[None, :]) & (row_ids[:, None] >= row_ids[None, :])
        mine = fused_heads[index * group_rows : (index + 1) * group_rows]
        query = rotate(
            mine[:, :query_cols].reshape(group_rows, query_local, HEAD_SIZE), cosine, sine
        ).astype(BF16)
        query = query.reshape(group_rows, kv_local, per_group, HEAD_SIZE)
        key = rotate(
            mine[:, query_cols : query_cols + kv_cols].reshape(group_rows, kv_local, HEAD_SIZE),
            cosine,
            sine,
        ).astype(BF16)
        value = (
            mine[:, query_cols + kv_cols :].reshape(group_rows, kv_local, HEAD_SIZE).astype(BF16)
        )
        heads, log_totals = attend_forward(query, key, value, allowed, scale)
        heads_list.append(heads.reshape(group_rows, query_cols))
        saved.append((query, key, value, log_totals, allowed, cosine, sine))
    heads_flat = jnp.concatenate(heads_list)
    attended = reduce_tensor(
        mm(heads_flat, output_full).astype(BF16).reshape(micro, 4, local_rows, width)
    ).reshape(flat_rows, width)
    residual = inputs + attended

    second_scale = rms_scale(residual)
    normed_two = (residual * second_scale * gain_two).astype(BF16)
    normed_two_all = gather_eight(normed_two)
    arrived_cot = exchange(mm(to_send, cotangent.reshape(flat_rows, width)).astype(BF16))
    cot_rows = outer_sum(to_place, arrived_cot).astype(BF16)
    cot_all = gather_eight(cot_rows)

    out_sum = 0.0
    d_normed_sum = 0.0
    gate_kept, gate_moved, down_grads = [], [], []
    for chunk in range(CHUNKS):
        gate_up = gather_z(ff_shards[chunk][0]).reshape(width, 2 * chunk_cols)
        down = gather_z(ff_shards[chunk][1]).reshape(chunk_cols, width)
        both = mm(normed_two_all, gate_up)
        gate, upward = both[:, :chunk_cols], both[:, chunk_cols:]
        sigmoid = jax.nn.sigmoid(gate)
        silu = gate * sigmoid
        hidden = (silu * upward).astype(BF16)
        d_hidden = times_transposed(cot_all, down)
        d_gate = (d_hidden * upward * sigmoid * (1.0 + gate * (1.0 - sigmoid))).astype(BF16)
        d_upward = (d_hidden * silu).astype(BF16)
        d_both = jnp.concatenate([d_gate, d_upward], axis=1)
        down_part = outer_sum(hidden, cot_all).astype(BF16)
        down_grads.append(reduce_z(down_part.reshape(z_size, piece, width)))
        both_part = outer_sum(normed_two_all, d_both).astype(BF16)
        both_sum = reduce_z(both_part.reshape(z_size, 2, shard_rows, 2 * chunk_cols))
        gate_kept.append(take(both_sum, here_x))
        gate_moved.append(
            lax.ppermute(take(both_sum, 1 - here_x).astype(BF16), "x", SWAP).astype(F32)
        )
        out_sum = out_sum + mm(hidden, down)
        d_normed_sum = d_normed_sum + times_transposed(d_both, gate_up)
    down_grad = jnp.concatenate(down_grads, axis=0)
    kept = jnp.stack(gate_kept).reshape(CHUNKS, shard_rows, 2, z_size, piece)
    moved = jnp.stack(gate_moved).reshape(CHUNKS, shard_rows, 2, z_size, piece)
    parity = in_order(here_x, kept, moved)
    gate_grad, up_grad = jnp.transpose(parity, (3, 2, 4, 0, 1, 5)).reshape(
        2, shard_rows, hidden_cols
    )

    layer_rows = residual + reduce_eight(out_sum.astype(BF16))
    d_normed_two = reduce_eight(d_normed_sum.astype(BF16))
    d_through, d_gain_two = norm_backward(residual, second_scale, gain_two, d_normed_two)
    d_residual = cot_rows.astype(F32) + d_through

    d_residual_all = gather_tensor(
        d_residual.astype(BF16).reshape(micro, local_rows, width)
    ).reshape(all_rows, width)
    d_heads_all = times_transposed(d_residual_all, output_full).astype(BF16)
    output_part = outer_sum(heads_flat, d_residual_all).astype(BF16)
    d_fused_list = []
    for index in range(micro):
        query, key, value, log_totals, allowed, cosine, sine = saved[index]
        d_heads = d_heads_all[index * group_rows : (index + 1) * group_rows].reshape(query.shape)
        d_query, d_key, d_value = attend_backward(
            query, key, value, d_heads, log_totals, allowed, scale
        )
        d_query = rotate(
            d_query.reshape(group_rows, query_local, HEAD_SIZE), cosine, -sine
        ).reshape(group_rows, query_cols)
        d_key = rotate(d_key, cosine, -sine).reshape(group_rows, kv_cols)
        d_fused_list.append(
            jnp.concatenate([d_query, d_key, d_value.reshape(group_rows, kv_cols)], axis=1).astype(
                BF16
            )
        )
    d_fused = jnp.concatenate(d_fused_list)
    d_normed_one = reduce_tensor(
        times_transposed(d_fused, fused_full).astype(BF16).reshape(micro, 4, local_rows, width)
    ).reshape(flat_rows, width)
    fused_part = outer_sum(normed_all, d_fused).astype(BF16)

    def reduce_data(part):
        part = part.reshape((z_size, 2, part.shape[0] // (2 * z_size), part.shape[1]))
        arrived = lax.ppermute(take(part, 1 - here_x, 1), "x", SWAP)
        return reduce_z((take(part, here_x, 1).astype(F32) + arrived.astype(F32)).astype(BF16))

    output_grad = reduce_data(output_part)
    fused_grad = reduce_data(fused_part)
    d_first, d_gain_one = norm_backward(inputs, first_scale, gain_one, d_normed_one)
    input_grads = (d_residual + d_first).astype(BF16)
    gain_grads = reduce_gains(jnp.stack([d_gain_one, d_gain_two]))

    def send_back(rows):
        returned = exchange(mm(to_place, rows).astype(BF16))
        return outer_sum(to_send, returned).astype(BF16).reshape(micro, local_rows, width)

    return (
        send_back(layer_rows.astype(BF16)),
        send_back(input_grads),
        fused_grad[:, :query_cols],
        fused_grad[:, query_cols : query_cols + kv_cols],
        fused_grad[:, query_cols + kv_cols :],
        output_grad,
        gate_grad,
        up_grad,
        down_grad,
        gain_grads[0],
        gain_grads[1],
    )


def solution(mesh):
    z_size = mesh.shape["dp"] // 2
    fine = Mesh(mesh.devices.reshape(z_size, 2, 2, 2), ("z", "x", "y", "c"))
    dp, tensor = ("z", "x"), ("y", "c")
    rows, columns, stacked = P(None, dp + tensor, None), P(dp, tensor), P(tensor + dp, None)
    return jax.shard_map(
        body,
        mesh=fine,
        in_specs=(
            rows,
            rows,
            P(None, dp + tensor),
            P(None, dp, None),
            columns,
            columns,
            columns,
            stacked,
            columns,
            columns,
            stacked,
            P(dp),
            P(dp),
        ),
        out_specs=(
            rows,
            rows,
            columns,
            columns,
            columns,
            stacked,
            columns,
            columns,
            stacked,
            P(dp),
            P(dp),
        ),
        check_vma=False,
    )
```

time: 1930 us -> 1310 us (0.68)
  waiting for transfers between devices: 1370 us -> 672 us
  starting transfers between devices: 33.5 us -> 168 us
  blocking collectives: 110 us -> 0 us
  local copies, waits for them, and re-layouts: 65.2 us -> 137 us
  matrix products: 248 us -> 216 us
  other arithmetic: 77.1 us -> 100 us
    reduce_scatter x15 -> x0, waiting for transfers between devices: 709 us -> none  [the longest x1 149 us: body(): lax.psum_scatter(gate_acc.astype(jnp.bfloat16), 'dp', scatter_dimension=0...]
    ppermute x0 -> x98, waiting for transfers between devices: none -> 672 us  [the longest x6 146 us: reduce_z(): from_far = lax.ppermute(relay, 'z', Z_FAR)]
    all_gather x15 -> x0, waiting for transfers between devices: 595 us -> none  [the longest x1 127 us: fetch_feedforward(): lax.all_gather(down_weight, 'dp', axis=0, tiled=True)]
    ppermute x0 -> x98, starting transfers between devices: none -> 144 us  [the longest x6 29.7 us: gather_z(): near = lax.ppermute(piece, 'z', Z_NEAR)]
    all_to_all x8 -> x5, waiting for transfers between devices: 63.2 us -> 0.01 us  [exchange(): lax.all_to_all(rows.reshape((devices, micro * sends) + rows.shape[1:]), e...]
    all_gather x2 -> x0, blocking collectives: 43.3 us -> none  [the longest x1 25.3 us: fetch_attention(): lax.all_gather(prenorm_gain, 'dp', axis=0, tiled=True)]
    all_to_all x2 -> x0, blocking collectives: 39.9 us -> none  [body(): lax.all_to_all(cotangent[batch_index][sending], ('dp', 'tensor'), split_a...]
    another operation x1 -> x28, local copies, waits for them, and re-layouts: 0.01 us -> 35 us  [the longest x3 11.4 us: body(): gate_grad, up_grad = jnp.transpose(parity, (3, 2, 4, 0, 1, 5)).reshape(2,...]
  transfers between devices with their start and end apart: 38 -> 103, of which waited for: 32 -> 38; matrix products, arithmetic and copies ran while one was open for 11% -> 31% of each run, Pallas kernels for 0% -> 0%
where the time goes in v1:
time: 1310 us; the launch traced here: 1300 us
  waiting for transfers between devices  672 us (51%)
  matrix products  216 us (16%)
  starting transfers between devices  168 us (13%)
  local copies, waits for them, and re-layouts  137 us (10%)
  other arithmetic  100 us (8%)
    ppermute x6, waiting for transfers between devices, reduce_z(): from_far = lax.ppermute(relay, 'z', Z_FAR)  146 us
    ppermute x6, waiting for transfers between devices, gather_z(): outward = lax.ppermute(far, 'z', Z_OUTWARD)  88.2 us
    ppermute x6, waiting for transfers between devices, gather_z(): far = lax.ppermute(piece, 'z', Z_FAR)  83 us
    dot_general x6, matrix products, times_transposed(): lax.dot_general(left, right, (((1,), (1,)), ((), ())), preferred_element_...  71.2 us
    dot_general x10, matrix products, mm(): return jnp.dot(left, right, preferred_element_type=F32)  66.3 us
    dot_general x10, matrix products, outer_sum(): lax.dot_general(left, right, (((0,), (0,)), ((), ())), preferred_element_...  63.3 us
    ppermute x6, waiting for transfers between devices, reduce_z(): from_near = lax.ppermute(near, 'z', Z_NEAR)  52.7 us
    ppermute x3, waiting for transfers between devices, reduce_gains(): total = total + lax.ppermute(take(parts, here_z ^ step, 1), 'z', pairs)  44.6 us
  transfers between devices with their start and end apart: 103, of which 38 were waited for; matrix products, arithmetic and copies ran while one was open for 31% of the time, Pallas kernels for 0%

profile of v1, /device:TPU:0, one launch (start us, length us, event | category | flops | bytes accessed | tf_op | source)
XLA Modules:
  0.0 1296.3 jit_solution(13799440236387286585)
XLA Ops:
  54.6 22.2 %collective-permute-done.2 = bf16[2,2,256]{2,1,0:T(2,128)(2,1)S(1)} collective-permute-done((bf16[2,2,256]{2,1,0:T(2,128)(2,1)S(1)}, bf16[2,2,256]{2,1,0:T(2,128)(2,1)S(1)}, u32[]{:S(2)}, u32[]{:S(2)}) %collective-permute-start.2) | collective-permute-done | bytes 2080 | tf_op jit(solution)/shard_map/ppermute | solution.py:206
  124.4 22.6 %collective-permute-done.32 = bf16[128,2048]{1,0:T(8,128)(2,1)} collective-permute-done((bf16[128,2048]{1,0:T(8,128)(2,1)}, bf16[128,2048]{1,0:T(8,128)(2,1)}, u32[]{:S(2)}, u32[]{:S(2)}) %collective-permute-start.32) | collective-permute-done | bytes 524320 | tf_op jit(solution)/shard_map/ppermute | solution.py:120
  155.2 14.3 %collective-permute-done.14 = bf16[2,64,2048]{2,1,0:T(8,128)(2,1)} collective-permute-done((bf16[2,64,2048]{2,1,0:T(8,128)(2,1)}, bf16[2,64,2048]{2,1,0:T(8,128)(2,1)}, u32[]{:S(2)}, u32[]{:S(2)}) %collective-permute-start.14) | collective-permute-done | bytes 524320 | tf_op jit(solution)/shard_map/ppermute | solution.py:120
  190.9 46.1 %collective-permute-done.9 = bf16[2,256,1024]{2,1,0:T(8,128)(2,1)} collective-permute-done((bf16[2,256,1024]{2,1,0:T(8,128)(2,1)}, bf16[2,256,1024]{2,1,0:T(8,128)(2,1)}, u32[]{:S(2)}, u32[]{:S(2)}) %collective-permute-start.9) | collective-permute-done | bytes 1048608 | tf_op jit(solution)/shard_map/ppermute | solution.py:120
  247.9 21.2 %collective-permute-start.36 = (bf16[2,256,1024]{2,1,0:T(8,128)(2,1)}, bf16[2,256,1024]{2,1,0:T(8,128)(2,1)}, u32[]{:S(2)}, u32[]{:S(2)}) collective-permute-start(bf16[2,256,1024]{2,1,0:T(8,128)(2,1)} %pad_maximum_fusion.11), channel_id=1, source_target_pairs={{0,8},{8,0},{16,24},{24,16},{1,9},{9,1},{17,25},{25,17},{2,10},{10... | collective-permute-start | bytes 3145736 | tf_op jit(solution)/shard_map/ppermute | solution.py:121
  312.8 56.8 %collective-permute-done.34 = bf16[128,2048]{1,0:T(8,128)(2,1)} collective-permute-done((bf16[128,2048]{1,0:T(8,128)(2,1)}, bf16[128,2048]{1,0:T(8,128)(2,1)}, u32[]{:S(2)}, u32[]{:S(2)}) %collective-permute-start.34) | collective-permute-done | bytes 524320 | tf_op jit(solution)/shard_map/ppermute | solution.py:123
  409.5 13.9 %collective-permute-done.30 = bf16[2,256,1024]{2,1,0:T(8,128)(2,1)} collective-permute-done((bf16[2,256,1024]{2,1,0:T(8,128)(2,1)}, bf16[2,256,1024]{2,1,0:T(8,128)(2,1)}, u32[]{:S(2)}, u32[]{:S(2)}) %collective-permute-start.30) | collective-permute-done | bytes 1048608 | tf_op jit(solution)/shard_map/ppermute | solution.py:123
  427.5 22.4 %collective-permute-done.49 = bf16[256,2048]{1,0:T(8,128)(2,1)S(1)} collective-permute-done((bf16[256,2048]{1,0:T(8,128)(2,1)S(1)}, bf16[256,2048]{1,0:T(8,128)(2,1)S(1)}, u32[]{:S(2)}, u32[]{:S(2)}) %collective-permute-start.49) | collective-permute-done | bytes 1048608 | tf_op jit(solution)/shard_map/ppermute | solution.py:178
  450.7 19.9 %collective-permute-done.18 = bf16[2,128,2048]{2,1,0:T(8,128)(2,1)S(1)} collective-permute-done((bf16[2,128,2048]{2,1,0:T(8,128)(2,1)S(1)}, bf16[2,128,2048]{2,1,0:T(8,128)(2,1)S(1)}, u32[]{:S(2)}, u32[]{:S(2)}) %collective-permute-start.18) | collective-permute-done | bytes 1048608 | tf_op jit(solution)/shard_map/ppermute | solution.py:170
  481.0 17.8 %collective-permute-done.19 = bf16[256,2048]{1,0:T(8,128)(2,1)S(1)} collective-permute-done((bf16[256,2048]{1,0:T(8,128)(2,1)S(1)}, bf16[256,2048]{1,0:T(8,128)(2,1)S(1)}, u32[]{:S(2)}, u32[]{:S(2)}) %collective-permute-start.19) | collective-permute-done | bytes 1048608 | tf_op jit(solution)/shard_map/ppermute | solution.py:177
  499.4 21.5 %collective-permute-done.20 = bf16[256,2048]{1,0:T(8,128)(2,1)S(1)} collective-permute-done((bf16[256,2048]{1,0:T(8,128)(2,1)S(1)}, bf16[256,2048]{1,0:T(8,128)(2,1)S(1)}, u32[]{:S(2)}, u32[]{:S(2)}) %collective-permute-start.20) | collective-permute-done | bytes 1048608 | tf_op jit(solution)/shard_map/ppermute | solution.py:178
  561.1 13.7 %fusion.174 = f32[2048,1024]{0,1:T(8,128)} fusion(bf16[2048,2048]{1,0:T(8,128)(2,1)S(1)} %constant_dynamic-update-slice_fusion.3, bf16[2048,1024]{1,0:T(8,128)(2,1)} %bitcast.107), kind=kOutput, calls=%fused_computation.465 | convolution fusion | flops 8589934592 | bytes 20971520 | tf_op jit(solution)/shard_map/dot_general | solution.py:57
  585.5 15.4 %fusion.3 = f32[2048,2048]{1,0:T(8,128)} fusion(bf16[2048,1024]{1,0:T(8,128)(2,1)} %bitcast.107, bf16[2048,512]{0,1:T(8,128)(2,1)} %get-tuple-element.23, bf16[2048,512]{0,1:T(8,128)(2,1)} %get-tuple-element.22), kind=kOutput, calls=%fused_computation.29 | convolution fusion | flops 8598323200 | bytes 25165824 | tf_op jit(solution)/shard_map/dot_general | solution.py:65
  644.3 16.3 %add_convert_fusion = bf16[2048,2048]{1,0:T(8,128)(2,1)} fusion(f32[2048,2048]{1,0:T(8,128)} %fusion.3, bf16[2048,1024]{1,0:T(8,128)(2,1)} %bitcast.91, bf16[2048,512]{0,1:T(8,128)(2,1)} %get-tuple-element.21, bf16[2048,512]{0,1:T(8,128)(2,1)} %get-tuple-element.20), kind=kOutput, calls=%fused_computation | convolution fusion | flops 8606711808 | bytes 33554432 | tf_op jit(solution)/shard_map/dot_general | solution.py:65
  710.0 52.7 %collective-permute-done.88 = bf16[128,2048]{1,0:T(8,128)(2,1)S(1)} collective-permute-done((bf16[128,2048]{1,0:T(8,128)(2,1)S(1)}, bf16[128,2048]{1,0:T(8,128)(2,1)S(1)}, u32[]{:S(2)}, u32[]{:S(2)}) %collective-permute-start.88) | collective-permute-done | bytes 524320 | tf_op jit(solution)/shard_map/ppermute | solution.py:137
  774.2 49.3 %collective-permute-done.87 = bf16[128,2048]{1,0:T(8,128)(2,1)S(1)} collective-permute-done((bf16[128,2048]{1,0:T(8,128)(2,1)S(1)}, bf16[128,2048]{1,0:T(8,128)(2,1)S(1)}, u32[]{:S(2)}, u32[]{:S(2)}) %collective-permute-start.87) | collective-permute-done | bytes 524320 | tf_op jit(solution)/shard_map/ppermute | solution.py:140
  836.4 43.4 %collective-permute-done.77 = bf16[2,256,1024]{2,1,0:T(8,128)(2,1)S(1)} collective-permute-done((bf16[2,256,1024]{2,1,0:T(8,128)(2,1)S(1)}, bf16[2,256,1024]{2,1,0:T(8,128)(2,1)S(1)}, u32[]{:S(2)}, u32[]{:S(2)}) %collective-permute-start.77) | collective-permute-done | bytes 1048608 | tf_op jit(solution)/shard_map/ppermute | solution.py:140
  882.1 42.4 %collective-permute-done.81 = bf16[2,256,1024]{2,1,0:T(8,128)(2,1)S(1)} collective-permute-done((bf16[2,256,1024]{2,1,0:T(8,128)(2,1)S(1)}, bf16[2,256,1024]{2,1,0:T(8,128)(2,1)S(1)}, u32[]{:S(2)}, u32[]{:S(2)}) %collective-permute-start.81) | collective-permute-done | bytes 1048608 | tf_op jit(solution)/shard_map/ppermute | solution.py:140
  985.5 21.8 %collective-permute-done.57 = bf16[256,2048]{1,0:T(8,128)(2,1)} collective-permute-done((bf16[256,2048]{1,0:T(8,128)(2,1)}, bf16[256,2048]{1,0:T(8,128)(2,1)}, u32[]{:S(2)}, u32[]{:S(2)}) %collective-permute-start.57) | collective-permute-done | bytes 1048608 | tf_op jit(solution)/shard_map/ppermute | solution.py:192
  1029.7 22.7 %collective-permute-done.46 = bf16[256,2048]{1,0:T(8,128)(2,1)} collective-permute-done((bf16[256,2048]{1,0:T(8,128)(2,1)}, bf16[256,2048]{1,0:T(8,128)(2,1)}, u32[]{:S(2)}, u32[]{:S(2)}) %collective-permute-start.46) | collective-permute-done | bytes 1048608 | tf_op jit(solution)/shard_map/ppermute | solution.py:192
  1060.4 21.0 %collective-permute-done.59 = bf16[2,128,2048]{2,1,0:T(8,128)(2,1)} collective-permute-done((bf16[2,128,2048]{2,1,0:T(8,128)(2,1)}, bf16[2,128,2048]{2,1,0:T(8,128)(2,1)}, u32[]{:S(2)}, u32[]{:S(2)}) %collective-permute-start.59) | collective-permute-done | bytes 1048608 | tf_op jit(solution)/shard_map/ppermute | solution.py:151
  1118.1 16.0 %convolution_convert_fusion.2 = bf16[1024,2048]{1,0:T(8,128)(2,1)S(1)} fusion(bf16[2048,1024]{1,0:T(8,128)(2,1)} %bitcast.609, bf16[512,256]{0,1:T(8,128)(2,1)S(1)} %copy-done.86, bf16[512,256]{0,1:T(8,128)(2,1)S(1)} %maximum_bitcast_fusion.4, bf16[512,512]{0,1:T(8,128)(2,1)S(1)} %bitcast.642, bf16[512,256]{0,1:T(8,128)(2,1)S(1)} %copy-done.85, ...), kind=kOutput, calls=%fused_computation.23 | convolution fusion | flops 4309647360 | bytes 10485760 | tf_op jit(solution)/shard_map/dot_general | solution.py:65
  1178.5 28.5 %collective-permute-done.64 = bf16[4,256,1024]{2,1,0:T(8,128)(2,1)} collective-permute-done((bf16[4,256,1024]{2,1,0:T(8,128)(2,1)}, bf16[4,256,1024]{2,1,0:T(8,128)(2,1)}, u32[]{:S(2)}, u32[]{:S(2)}) %collective-permute-start.64) | collective-permute-done | bytes 2097184 | tf_op jit(solution)/shard_map/ppermute | solution.py:439
  1251.7 36.3 %collective-permute-done.94 = f32[2,256]{1,0:T(2,128)S(1)} collective-permute-done((f32[2,256]{1,0:T(2,128)S(1)}, f32[2,256]{1,0:T(2,128)S(1)}, u32[]{:S(2)}, u32[]{:S(2)}) %collective-permute-start.94) | collective-permute-done | bytes 2080 | tf_op jit(solution)/shard_map/ppermute | solution.py:219
  (699 shorter events, 634.7 us)
Async XLA Ops:
  3.1 109.0 %collective-permute-start.40 = (bf16[128,2048]{1,0:T(8,128)(2,1)}, bf16[128,2048]{1,0:T(8,128)(2,1)}, u32[]{:S(2)}, u32[]{:S(2)}) collective-permute-start(bf16[128,2048]{1,0:T(8,128)(2,1)} %get-tuple-element.81), channel_id=1, source_target_pairs={{0,8},{8,0},{16,24},{24,16},{1,9},{9,1},{17,25},{25,17},{2,10},{10... | collective-permute-start | bytes 1572872 | tf_op jit(solution)/shard_map/ppermute | solution.py:121
  6.1 109.8 %collective-permute-start.41 = (bf16[128,2048]{1,0:T(8,128)(2,1)}, bf16[128,2048]{1,0:T(8,128)(2,1)}, u32[]{:S(2)}, u32[]{:S(2)}) collective-permute-start(bf16[128,2048]{1,0:T(8,128)(2,1)} %get-tuple-element.81), channel_id=1, source_target_pairs={{0,16},{16,0},{8,24},{24,8},{1,17},{17,1},{9,25},{25,9},{2,18},{18... | collective-permute-start | bytes 1572872 | tf_op jit(solution)/shard_map/ppermute | solution.py:120
  8.7 161.9 %collective-permute-start.42 = (bf16[128,2048]{1,0:T(8,128)(2,1)}, bf16[128,2048]{1,0:T(8,128)(2,1)}, u32[]{:S(2)}, u32[]{:S(2)}) collective-permute-start(bf16[128,2048]{1,0:T(8,128)(2,1)} %get-tuple-element.81), channel_id=1, source_target_pairs={{8,16},{16,8},{9,17},{17,9},{10,18},{18,10},{11,19},{19,11},{12,20... | collective-permute-start | bytes 1572872 | tf_op jit(solution)/shard_map/ppermute | solution.py:122
  15.1 76.3 %collective-permute-start.35 = (bf16[256,1024]{1,0:T(8,128)(2,1)}, bf16[256,1024]{1,0:T(8,128)(2,1)}, u32[]{:S(2)}, u32[]{:S(2)}) collective-permute-start(bf16[256,1024]{1,0:T(8,128)(2,1)} %broadcast_select_fusion), channel_id=1, source_target_pairs={{0,4},{4,0},{1,5},{5,1},{2,6},{6,2},{3,7},{7,3},{8,12},{12,8},{9,1... | collective-permute-start | bytes 1572872 | tf_op jit(solution)/shard_map/ppermute | solution.py:324
  45.9 133.7 %all-to-all-start.1 = ((bf16[32,8,2048]{2,1,0:T(8,128)(2,1)}), bf16[32,8,2048]{2,1,0:T(8,128)(2,1)S(1)}, u32[]{:S(2)}, u32[]{:S(2)}) async-start(bf16[32,8,2048]{2,1,0:T(8,128)(2,1)} %fusion.4), calls=%async_computation.1 | async-start | bytes 2097152 | tf_op jit(solution)/shard_map/all_to_all | solution.py:277
  112.1 193.9 %collective-permute-start.33 = (bf16[128,2048]{1,0:T(8,128)(2,1)}, bf16[128,2048]{1,0:T(8,128)(2,1)}, u32[]{:S(2)}, u32[]{:S(2)}) collective-permute-start(bf16[128,2048]{1,0:T(8,128)(2,1)} %get-tuple-element.80), channel_id=1, source_target_pairs={{8,16},{16,8},{9,17},{17,9},{10,18},{18,10},{11,19},{19,11},{12,20... | collective-permute-start | bytes 1572872 | tf_op jit(solution)/shard_map/ppermute | solution.py:122
  169.5 75.0 %collective-permute-start.8 = (bf16[2,256,1024]{2,1,0:T(8,128)(2,1)}, bf16[2,256,1024]{2,1,0:T(8,128)(2,1)}, u32[]{:S(2)}, u32[]{:S(2)}) collective-permute-start(bf16[2,256,1024]{2,1,0:T(8,128)(2,1)} %pad_maximum_fusion.8), channel_id=1, source_target_pairs={{0,8},{8,0},{16,24},{24,16},{1,9},{9,1},{17,25},{25,17},{2,10},{10... | collective-permute-start | bytes 3145736 | tf_op jit(solution)/shard_map/ppermute | solution.py:121
  180.5 206.3 %all-to-all-start.3 = ((bf16[32,8,2048]{2,1,0:T(8,128)(2,1)}), bf16[32,8,2048]{2,1,0:T(8,128)(2,1)}, u32[]{:S(2)}, u32[]{:S(2)}) async-start(bf16[32,8,2048]{2,1,0:T(8,128)(2,1)} %fusion.6), calls=%async_computation.3 | async-start | bytes 2097152 | tf_op jit(solution)/shard_map/all_to_all | solution.py:277
  247.9 123.6 %collective-permute-start.36 = (bf16[2,256,1024]{2,1,0:T(8,128)(2,1)}, bf16[2,256,1024]{2,1,0:T(8,128)(2,1)}, u32[]{:S(2)}, u32[]{:S(2)}) collective-permute-start(bf16[2,256,1024]{2,1,0:T(8,128)(2,1)} %pad_maximum_fusion.11), channel_id=1, source_target_pairs={{0,8},{8,0},{16,24},{24,16},{1,9},{9,1},{17,25},{25,17},{2,10},{10... | collective-permute-start | bytes 3145736 | tf_op jit(solution)/shard_map/ppermute | solution.py:121
  269.1 104.1 %collective-permute-start.37 = (bf16[2,256,1024]{2,1,0:T(8,128)(2,1)}, bf16[2,256,1024]{2,1,0:T(8,128)(2,1)}, u32[]{:S(2)}, u32[]{:S(2)}) collective-permute-start(bf16[2,256,1024]{2,1,0:T(8,128)(2,1)} %pad_maximum_fusion.11), channel_id=1, source_target_pairs={{0,16},{16,0},{8,24},{24,8},{1,17},{17,1},{9,25},{25,9},{2,18},{18... | collective-permute-start | bytes 3145736 | tf_op jit(solution)/shard_map/ppermute | solution.py:120
  270.7 108.3 %collective-permute-start.27 = (bf16[2,256,1024]{2,1,0:T(8,128)(2,1)}, bf16[2,256,1024]{2,1,0:T(8,128)(2,1)}, u32[]{:S(2)}, u32[]{:S(2)}) collective-permute-start(bf16[2,256,1024]{2,1,0:T(8,128)(2,1)} %pad_maximum_fusion.10), channel_id=1, source_target_pairs={{0,8},{8,0},{16,24},{24,16},{1,9},{9,1},{17,25},{25,17},{2,10},{10... | collective-permute-start | bytes 3145736 | tf_op jit(solution)/shard_map/ppermute | solution.py:121
  272.9 96.7 %collective-permute-start.34 = (bf16[128,2048]{1,0:T(8,128)(2,1)}, bf16[128,2048]{1,0:T(8,128)(2,1)}, u32[]{:S(2)}, u32[]{:S(2)}) collective-permute-start(bf16[128,2048]{1,0:T(8,128)(2,1)} %collective-permute-done.32), channel_id=1, source_target_pairs={{16,24},{8,0},{17,25},{9,1},{18,26},{10,2},{19,27},{11,3},{20,28},... | collective-permute-start | bytes 1572872 | tf_op jit(solution)/shard_map/ppermute | solution.py:123
  305.9 74.8 %collective-permute-start.28 = (bf16[2,256,1024]{2,1,0:T(8,128)(2,1)}, bf16[2,256,1024]{2,1,0:T(8,128)(2,1)}, u32[]{:S(2)}, u32[]{:S(2)}) collective-permute-start(bf16[2,256,1024]{2,1,0:T(8,128)(2,1)} %pad_maximum_fusion.10), channel_id=1, source_target_pairs={{0,16},{16,0},{8,24},{24,8},{1,17},{17,1},{9,25},{25,9},{2,18},{18... | collective-permute-start | bytes 3145736 | tf_op jit(solution)/shard_map/ppermute | solution.py:120
  556.5 134.0 %collective-permute-start.86 = (bf16[128,2048]{1,0:T(8,128)(2,1)}, bf16[128,2048]{1,0:T(8,128)(2,1)}, u32[]{:S(2)}, u32[]{:S(2)}) collective-permute-start(bf16[128,2048]{1,0:T(8,128)(2,1)} %get-tuple-element.57), channel_id=1, source_target_pairs={{24,16},{0,8},{25,17},{1,9},{26,18},{2,10},{27,19},{3,11},{28,20},... | collective-permute-start | bytes 1572872 | tf_op jit(solution)/shard_map/ppermute | solution.py:136
  559.6 136.2 %collective-permute-start.85 = (bf16[128,2048]{1,0:T(8,128)(2,1)}, bf16[128,2048]{1,0:T(8,128)(2,1)}, u32[]{:S(2)}, u32[]{:S(2)}) collective-permute-start(bf16[128,2048]{1,0:T(8,128)(2,1)} %get-tuple-element.57), channel_id=1, source_target_pairs={{8,16},{16,8},{9,17},{17,9},{10,18},{18,10},{11,19},{19,11},{12,20... | collective-permute-start | bytes 1572872 | tf_op jit(solution)/shard_map/ppermute | solution.py:138
  690.6 75.2 %collective-permute-start.74 = (bf16[2,256,1024]{2,1,0:T(8,128)(2,1)S(1)}, bf16[2,256,1024]{2,1,0:T(8,128)(2,1)S(1)}, u32[]{:S(2)}, u32[]{:S(2)}) collective-permute-start(bf16[2,256,1024]{2,1,0:T(8,128)(2,1)S(1)} %copy-done.53), channel_id=1, source_target_pairs={{0,8},{8,0},{16,24},{24,16},{1,9},{9,1},{17,25},{25,17},{2,10},{10... | collective-permute-start | bytes 3145736 | tf_op jit(solution)/shard_map/ppermute | solution.py:137
  690.7 75.2 %collective-permute-start.80 = (bf16[2,256,1024]{2,1,0:T(8,128)(2,1)S(1)}, bf16[2,256,1024]{2,1,0:T(8,128)(2,1)S(1)}, u32[]{:S(2)}, u32[]{:S(2)}) collective-permute-start(bf16[2,256,1024]{2,1,0:T(8,128)(2,1)S(1)} %get-tuple-element.41), channel_id=1, source_target_pairs={{24,16},{0,8},{25,17},{1,9},{26,18},{2,10},{27,19},{3,11},{28,20},... | collective-permute-start | bytes 3145736 | tf_op jit(solution)/shard_map/ppermute | solution.py:136
  762.7 186.5 %collective-permute-start.55 = (bf16[4,256,2048]{2,1,0:T(8,128)(2,1)}, bf16[4,256,2048]{2,1,0:T(8,128)(2,1)}, u32[]{:S(2)}, u32[]{:S(2)}) collective-permute-start(bf16[4,256,2048]{2,1,0:T(8,128)(2,1)} %bitcast.126), channel_id=1, source_target_pairs={{0,1},{1,0},{2,3},{3,2},{4,5},{5,4},{6,7},{7,6},{8,9},{9,8},{10,11... | collective-permute-start | bytes 12582920 | tf_op jit(solution)/shard_map/ppermute | solution.py:186
  765.9 113.8 %collective-permute-start.77 = (bf16[2,256,1024]{2,1,0:T(8,128)(2,1)S(1)}, bf16[2,256,1024]{2,1,0:T(8,128)(2,1)S(1)}, u32[]{:S(2)}, u32[]{:S(2)}) collective-permute-start(bf16[2,256,1024]{2,1,0:T(8,128)(2,1)S(1)} %fusion.19), channel_id=1, source_target_pairs={{0,16},{16,0},{8,24},{24,8},{1,17},{17,1},{9,25},{25,9},{2,18},{18... | collective-permute-start | bytes 3145736 | tf_op jit(solution)/shard_map/ppermute | solution.py:140
  773.0 109.1 %collective-permute-start.79 = (bf16[2,256,1024]{2,1,0:T(8,128)(2,1)S(1)}, bf16[2,256,1024]{2,1,0:T(8,128)(2,1)S(1)}, u32[]{:S(2)}, u32[]{:S(2)}) collective-permute-start(bf16[2,256,1024]{2,1,0:T(8,128)(2,1)S(1)} %get-tuple-element.41), channel_id=1, source_target_pairs={{8,16},{16,8},{9,17},{17,9},{10,18},{18,10},{11,19},{19,11},{12,20... | collective-permute-start | bytes 3145736 | tf_op jit(solution)/shard_map/ppermute | solution.py:138
  834.8 89.6 %collective-permute-start.81 = (bf16[2,256,1024]{2,1,0:T(8,128)(2,1)S(1)}, bf16[2,256,1024]{2,1,0:T(8,128)(2,1)S(1)}, u32[]{:S(2)}, u32[]{:S(2)}) collective-permute-start(bf16[2,256,1024]{2,1,0:T(8,128)(2,1)S(1)} %fusion.16), channel_id=1, source_target_pairs={{0,16},{16,0},{8,24},{24,8},{1,17},{17,1},{9,25},{25,9},{2,18},{18... | collective-permute-start | bytes 3145736 | tf_op jit(solution)/shard_map/ppermute | solution.py:140
  879.7 82.0 %collective-permute-start.44 = (bf16[4,256,2048]{2,1,0:T(8,128)(2,1)}, bf16[4,256,2048]{2,1,0:T(8,128)(2,1)}, u32[]{:S(2)}, u32[]{:S(2)}) collective-permute-start(bf16[4,256,2048]{2,1,0:T(8,128)(2,1)} %bitcast.114), channel_id=1, source_target_pairs={{0,1},{1,0},{2,3},{3,2},{4,5},{5,4},{6,7},{7,6},{8,9},{9,8},{10,11... | collective-permute-start | bytes 12582920 | tf_op jit(solution)/shard_map/ppermute | solution.py:186
  971.4 81.0 %collective-permute-start.46 = (bf16[256,2048]{1,0:T(8,128)(2,1)}, bf16[256,2048]{1,0:T(8,128)(2,1)}, u32[]{:S(2)}, u32[]{:S(2)}) collective-permute-start(bf16[256,2048]{1,0:T(8,128)(2,1)} %get-tuple-element.49), channel_id=1, source_target_pairs={{0,2},{2,0},{1,3},{3,1},{4,6},{6,4},{5,7},{7,5},{8,10},{10,8},{9,1... | collective-permute-start | bytes 3145736 | tf_op jit(solution)/shard_map/ppermute | solution.py:192
  1056.7 113.8 %all-to-all-start.2 = ((bf16[32,8,2048]{2,1,0:T(8,128)(2,1)}), bf16[32,8,2048]{2,1,0:T(8,128)(2,1)}, u32[]{:S(2)}, u32[]{:S(2)}) async-start(bf16[32,8,2048]{2,1,0:T(8,128)(2,1)} %fusion.5), calls=%async_computation.2 | async-start | bytes 2097152 | tf_op jit(solution)/shard_map/all_to_all | solution.py:277
  (205 other events, 5836.5 us)

commit v2 on v1

v2 whole, which is shorter than its diff:
```python
import functools
import math

import jax
import jax.numpy as jnp
from jax import lax
from jax.experimental import pallas as pl
from jax.experimental.layout import Layout, with_layout_constraint
from jax.experimental.pallas import tpu as pltpu
from jax.sharding import Mesh, PartitionSpec as P

HEAD_SIZE = 256
EPSILON = 1e-06
ROPE_BASE = 1000042.0
NEGATIVE = -1e30
LONGEST = 256
CHUNKS = 2
F32 = jnp.float32
BF16 = jnp.bfloat16

SWAP = [(0, 1), (1, 0)]
DIAGONAL = [(0, 3), (3, 0), (1, 2), (2, 1)]
Z_NEAR = [(0, 1), (1, 0), (2, 3), (3, 2)]
Z_FAR = [(0, 2), (2, 0), (1, 3), (3, 1)]
Z_ACROSS = [(0, 3), (3, 0), (1, 2), (2, 1)]


def rms_scale(values):
    return lax.rsqrt(jnp.mean(values * values, axis=-1, keepdims=True) + EPSILON)


def rope_tables(positions, head):
    half = head // 2
    frequency = jnp.exp(jnp.arange(half, dtype=F32) * (-2.0 * math.log(ROPE_BASE) / head))
    angles = positions.astype(F32)[:, None] * frequency[None, :]
    return (jnp.cos(angles), jnp.sin(angles))


def rotate(head, cosine, sine):
    half = head.shape[-1] // 2
    first, second = head[:, :half], head[:, half:]
    return jnp.concatenate(
        [first * cosine - second * sine, second * cosine + first * sine], axis=-1
    )


def sequence_layout(lens, total):
    rows = jnp.arange(total, dtype=jnp.int32)
    ends = jnp.cumsum(lens)
    segment = jnp.sum((rows[:, None] >= ends[None, :]).astype(jnp.int32), axis=1)
    starts = ends - lens
    which = segment[:, None] == jnp.arange(lens.shape[0], dtype=jnp.int32)[None, :]
    begin = jnp.sum(jnp.where(which, starts[None, :], 0), axis=1)
    return (segment, rows - begin)


def mm(left, right):
    return jnp.dot(left, right, preferred_element_type=F32)


def outer_sum(left, right):
    return lax.dot_general(left, right, (((0,), (0,)), ((), ())), preferred_element_type=F32)


def times_transposed(left, right):
    return lax.dot_general(left, right, (((1,), (1,)), ((), ())), preferred_element_type=F32)


def masked_scores(query, key, seg_query, seg_key, row_start, key_start):
    scores = times_transposed(query, key) * (1.0 / math.sqrt(HEAD_SIZE))
    rows = row_start + lax.broadcasted_iota(jnp.int32, scores.shape, 0)
    keys = key_start + lax.broadcasted_iota(jnp.int32, scores.shape, 1)
    allowed = (seg_query == seg_key) & (rows >= keys)
    scores = jnp.where(allowed, scores, NEGATIVE)
    expo = jnp.exp(scores - jnp.max(scores, axis=-1, keepdims=True))
    return expo / jnp.sum(expo, axis=-1, keepdims=True)


def query_blocks(total):
    size = LONGEST
    return [
        (start, start + size, max(0, start - LONGEST)) for start in range(0, total, size)
    ]


def place_rows(place_ref, piece_refs, rows_ref):
    here = place_ref[0]
    size = piece_refs[0].shape[1]
    for step, piece in enumerate(piece_refs):
        start = pl.multiple_of(jnp.bitwise_xor(here, step) * size, size)
        rows_ref[pl.ds(start, size), :] = piece[0]


def spread_rows(place_ref, rows_ref, kept_ref, sent_ref):
    here = place_ref[0]
    size = kept_ref.shape[2]
    for step in range(4):
        start = pl.multiple_of(jnp.bitwise_xor(here, step) * size, size)
        out_ref = sent_ref if step % 2 else kept_ref
        out_ref[step // 2, 0] = rows_ref[pl.ds(start, size), :]


def attention_forward_kernel(
    query_heads,
    place_ref,
    piece0,
    piece1,
    piece2,
    piece3,
    own_ref,
    other_ref,
    output_ref,
    cosine_ref,
    sine_ref,
    seg_query_ref,
    seg_key_ref,
    normed_ref,
    fused_ref,
    heads_ref,
    kept_ref,
    sent_ref,
    rows_ref,
    sums_ref,
):
    place_rows(place_ref, (piece0, piece1, piece2, piece3), rows_ref)
    normed_ref[...] = rows_ref[...]
    half = own_ref.shape[0]
    fused = mm(rows_ref[:, :half], own_ref[...]) + mm(rows_ref[:, half:], other_ref[...])
    cosine, sine = cosine_ref[0], sine_ref[0]
    total = rows_ref.shape[0]
    kv_heads = fused.shape[1] // HEAD_SIZE - query_heads
    for head in range(query_heads + kv_heads // 2):
        columns = slice(head * HEAD_SIZE, (head + 1) * HEAD_SIZE)
        fused_ref[:, columns] = rotate(fused[:, columns], cosine, sine).astype(BF16)
    first_value = (query_heads + kv_heads // 2) * HEAD_SIZE
    fused_ref[:, first_value:] = fused[:, first_value:].astype(BF16)
    per_group = 2 * query_heads // kv_heads
    for head in range(query_heads):
        group = head // per_group
        columns = slice(head * HEAD_SIZE, (head + 1) * HEAD_SIZE)
        at_key = (query_heads + group) * HEAD_SIZE
        at_value = first_value + group * HEAD_SIZE
        for start, stop, low in query_blocks(total):
            probs = masked_scores(
                fused_ref[start:stop, columns],
                fused_ref[low:stop, at_key : at_key + HEAD_SIZE],
                seg_query_ref[0, start:stop],
                seg_key_ref[0, :, low:stop],
                start,
                low,
            )
            heads_ref[start:stop, columns] = mm(
                probs.astype(BF16), fused_ref[low:stop, at_value : at_value + HEAD_SIZE]
            ).astype(BF16)
    sums_ref[...] = mm(heads_ref[...], output_ref[...]).astype(BF16)
    spread_rows(place_ref, sums_ref, kept_ref, sent_ref)


def attention_backward_kernel(
    query_heads,
    block_rows,
    place_ref,
    piece0,
    piece1,
    piece2,
    piece3,
    own_ref,
    other_ref,
    output_ref,
    cosine_ref,
    sine_ref,
    seg_query_ref,
    seg_key_ref,
    normed_ref,
    fused_ref,
    heads_ref,
    kept_ref,
    sent_ref,
    fused_kept_ref,
    fused_sent_ref,
    output_kept_ref,
    output_sent_ref,
    rows_ref,
    sums_ref,
    d_heads_ref,
    d_fused_ref,
    d_key_ref,
    d_value_ref,
    fused_acc,
    output_acc,
):
    index = pl.program_id(0)
    scale = 1.0 / math.sqrt(HEAD_SIZE)
    place_rows(place_ref, (piece0, piece1, piece2, piece3), rows_ref)
    d_heads_ref[...] = times_transposed(rows_ref[...], output_ref[...]).astype(BF16)
    cosine, sine = cosine_ref[0], sine_ref[0]
    total = rows_ref.shape[0]
    kv_heads = fused_ref.shape[1] // HEAD_SIZE - query_heads
    first_value = (query_heads + kv_heads // 2) * HEAD_SIZE
    per_group = 2 * query_heads // kv_heads
    for group in range(kv_heads // 2):
        at_key = (query_heads + group) * HEAD_SIZE
        at_value = first_value + group * HEAD_SIZE
        d_key_ref[...] = jnp.zeros_like(d_key_ref)
        d_value_ref[...] = jnp.zeros_like(d_value_ref)
        for head in range(group * per_group, (group + 1) * per_group):
            columns = slice(head * HEAD_SIZE, (head + 1) * HEAD_SIZE)
            for start, stop, low in query_blocks(total):
                query = fused_ref[start:stop, columns]
                key = fused_ref[low:stop, at_key : at_key + HEAD_SIZE]
                value = fused_ref[low:stop, at_value : at_value + HEAD_SIZE]
                d_heads = d_heads_ref[start:stop, columns]
                probs = masked_scores(
                    query,
                    key,
                    seg_query_ref[0, start:stop],
                    seg_key_ref[0, :, low:stop],
                    start,
                    low,
                )
                d_probs = times_transposed(d_heads, value)
                delta = jnp.sum(probs * d_probs, axis=-1, keepdims=True)
                d_scores = (probs * (d_probs - delta)).astype(BF16)
                d_query = mm(d_scores, key) * scale
                d_fused_ref[start:stop, columns] = rotate(
                    d_query, cosine[start:stop], -sine[start:stop]
                ).astype(BF16)
                d_key_ref[low:stop] += outer_sum(d_scores, query) * scale
                d_value_ref[low:stop] += outer_sum(probs.astype(BF16), d_heads)
        d_fused_ref[:, at_key : at_key + HEAD_SIZE] = rotate(
            d_key_ref[...], cosine, -sine
        ).astype(BF16)
        d_fused_ref[:, at_value : at_value + HEAD_SIZE] = d_value_ref[...].astype(BF16)
    half = own_ref.shape[0]
    sums_ref[:, :half] = times_transposed(d_fused_ref[...], own_ref[...]).astype(BF16)
    sums_ref[:, half:] = times_transposed(d_fused_ref[...], other_ref[...]).astype(BF16)
    spread_rows(place_ref, sums_ref, kept_ref, sent_ref)
    fused_part = outer_sum(normed_ref[...], d_fused_ref[...])
    output_part = outer_sum(heads_ref[...], rows_ref[...])

    @pl.when(index == 0)
    def _():
        fused_acc[...] = fused_part
        output_acc[...] = output_part

    @pl.when(index > 0)
    def _():
        fused_acc[...] += fused_part
        output_acc[...] += output_part

    @pl.when(index == pl.num_programs(0) - 1)
    def _():
        fused_kept_ref[...] = fused_acc[:half].astype(BF16)
        fused_sent_ref[...] = fused_acc[half:].astype(BF16)
        here_x = place_ref[1]
        size = block_rows
        for step in range(output_acc.shape[0] // (2 * size)):
            kept = pl.multiple_of((2 * step + here_x) * size, size)
            sent = pl.multiple_of((2 * step + 1 - here_x) * size, size)
            rows = slice(step * size, (step + 1) * size)
            output_kept_ref[rows] = output_acc[pl.ds(kept, size), :].astype(BF16)
            output_sent_ref[rows] = output_acc[pl.ds(sent, size), :].astype(BF16)


def whole_spec(shape):
    zeros = (0,) * len(shape)
    return pl.BlockSpec(shape, lambda *_: zeros, pipeline_mode=pl.Buffered(1))


def attention_specs(pieces, own, other, output_full, tables, segments):
    micro, rows, width = pieces[0].shape
    total = 4 * rows
    half = tables[0].shape[-1]
    return (
        [pl.BlockSpec(memory_space=pltpu.SMEM)]
        + [pl.BlockSpec((1, rows, width), lambda m: (m, 0, 0))] * 4
        + [whole_spec(own.shape), whole_spec(other.shape), whole_spec(output_full.shape)]
        + [pl.BlockSpec((1, total, half), lambda m: (m, 0, 0))] * 2
        + [
            pl.BlockSpec((1, total, 1), lambda m: (m, 0, 0)),
            pl.BlockSpec((1, 1, total), lambda m: (m, 0, 0)),
        ]
    )


def attention_forward(place, pieces, own, other, output_full, tables, segments):
    micro, rows, width = pieces[0].shape
    total = 4 * rows
    query_cols, fused_cols = output_full.shape[0], own.shape[1]

    def by_micro(columns):
        return pl.BlockSpec((total, columns), lambda m: (m, 0))

    return pl.pallas_call(
        functools.partial(attention_forward_kernel, query_cols // HEAD_SIZE),
        grid=(micro,),
        in_specs=attention_specs(pieces, own, other, output_full, tables, segments),
        out_specs=[
            by_micro(width),
            by_micro(fused_cols),
            by_micro(query_cols),
            pl.BlockSpec((2, 1, rows, width), lambda m: (0, m, 0, 0)),
            pl.BlockSpec((2, 1, rows, width), lambda m: (0, m, 0, 0)),
        ],
        out_shape=[
            jax.ShapeDtypeStruct((micro * total, width), BF16),
            jax.ShapeDtypeStruct((micro * total, fused_cols), BF16),
            jax.ShapeDtypeStruct((micro * total, query_cols), BF16),
            jax.ShapeDtypeStruct((2, micro, rows, width), BF16),
            jax.ShapeDtypeStruct((2, micro, rows, width), BF16),
        ],
        scratch_shapes=[pltpu.VMEM((total, width), BF16), pltpu.VMEM((total, width), BF16)],
        compiler_params=pltpu.CompilerParams(vmem_limit_bytes=56 << 20),
    )(place, *pieces, own, other, output_full, *tables, *segments)


def attention_backward(
    place, pieces, own, other, output_full, tables, segments, normed, fused, heads, block_rows
):
    micro, rows, width = pieces[0].shape
    total = 4 * rows
    query_cols, fused_cols = output_full.shape[0], own.shape[1]

    def by_micro(columns):
        return pl.BlockSpec((total, columns), lambda m: (m, 0))

    return pl.pallas_call(
        functools.partial(attention_backward_kernel, query_cols // HEAD_SIZE, block_rows),
        grid=(micro,),
        in_specs=attention_specs(pieces, own, other, output_full, tables, segments)
        + [by_micro(width), by_micro(fused_cols), by_micro(query_cols)],
        out_specs=[
            pl.BlockSpec((2, 1, rows, width), lambda m: (0, m, 0, 0)),
            pl.BlockSpec((2, 1, rows, width), lambda m: (0, m, 0, 0)),
            whole_spec((width // 2, fused_cols)),
            whole_spec((width // 2, fused_cols)),
            whole_spec((query_cols // 2, width)),
            whole_spec((query_cols // 2, width)),
        ],
        out_shape=[
            jax.ShapeDtypeStruct((2, micro, rows, width), BF16),
            jax.ShapeDtypeStruct((2, micro, rows, width), BF16),
            jax.ShapeDtypeStruct((width // 2, fused_cols), BF16),
            jax.ShapeDtypeStruct((width // 2, fused_cols), BF16),
            jax.ShapeDtypeStruct((query_cols // 2, width), BF16),
            jax.ShapeDtypeStruct((query_cols // 2, width), BF16),
        ],
        scratch_shapes=[
            pltpu.VMEM((total, width), BF16),
            pltpu.VMEM((total, width), BF16),
            pltpu.VMEM((total, query_cols), BF16),
            pltpu.VMEM((total, fused_cols), BF16),
            pltpu.VMEM((total, HEAD_SIZE), F32),
            pltpu.VMEM((total, HEAD_SIZE), F32),
            pltpu.VMEM((width, fused_cols), F32),
            pltpu.VMEM((query_cols, width), F32),
        ],
        compiler_params=pltpu.CompilerParams(vmem_limit_bytes=60 << 20),
    )(place, *pieces, own, other, output_full, *tables, *segments, normed, fused, heads)


def feedforward_kernel(previous, last, normed_ref, cot_ref, weights_ref, *refs):
    refs = list(refs)
    before = [refs.pop(0) for _ in range(2)] if previous else []
    down_ref = refs.pop()
    hidden_ref, d_both_ref, *sums = refs
    pieces, _, fused = weights_ref.shape
    columns, width = down_ref.shape
    rows, piece = width // pieces, columns // pieces
    index = pl.program_id(0)

    @pl.when(index == 0)
    def _():
        for step in range(pieces):
            for part in range(width // fused):
                start = rows + part * piece
                down_ref[step * piece : (step + 1) * piece, part * fused : (part + 1) * fused] = (
                    weights_ref[step, start : start + piece, :]
                )

    both = mm(normed_ref[:, :rows], weights_ref[0, :rows, :])
    for step in range(1, pieces):
        both = both + mm(normed_ref[:, step * rows : (step + 1) * rows], weights_ref[step, :rows, :])
    gate, upward = both[:, :columns], both[:, columns:]
    sigmoid = 1.0 / (1.0 + jnp.exp(-gate))
    silu = gate * sigmoid
    hidden_ref[...] = (silu * upward).astype(BF16)
    d_hidden = times_transposed(cot_ref[...], down_ref[...])
    d_both_ref[:, :columns] = (
        d_hidden * upward * sigmoid * (1.0 + gate * (1.0 - sigmoid))
    ).astype(BF16)
    d_both_ref[:, columns:] = (d_hidden * silu).astype(BF16)

    def write(out_ref, d_normed_ref):
        out = mm(hidden_ref[...], down_ref[...])
        if previous:
            out = out + before[0][...]
        out_ref[...] = out.astype(out_ref.dtype)
        for step in range(pieces):
            at = slice(step * rows, (step + 1) * rows)
            d_normed = times_transposed(d_both_ref[...], weights_ref[step, :rows, :])
            if previous:
                d_normed = d_normed + before[1][:, at]
            d_normed_ref[:, at] = d_normed.astype(d_normed_ref.dtype)

    if not last:
        write(*sums)
        return

    @pl.when(index < 4)
    def _():
        write(*sums[1::2])

    @pl.when(index >= 4)
    def _():
        write(*sums[0::2])


def feedforward(normed, cot, weights, columns, previous, last):
    rows, width = normed.shape
    size = rows // 8

    def blocks(count):
        return pl.BlockSpec((size, count), lambda i: ((i + 4) % 8, 0))

    if last:
        sums = [
            pl.BlockSpec((size, width), lambda i: (jnp.maximum(i - 4, 0), 0)),
            pl.BlockSpec((size, width), lambda i: (jnp.minimum(i, 3), 0)),
        ] * 2
        shapes = [jax.ShapeDtypeStruct((rows // 2, width), BF16)] * 4
    else:
        sums = [blocks(width)] * 2
        shapes = [jax.ShapeDtypeStruct((rows, width), F32)] * 2
    return pl.pallas_call(
        functools.partial(feedforward_kernel, bool(previous), last),
        grid=(8,),
        in_specs=[blocks(width), blocks(width), whole_spec(weights.shape)]
        + [blocks(width)] * len(previous),
        out_specs=[blocks(columns), blocks(2 * columns)] + sums,
        out_shape=[
            jax.ShapeDtypeStruct((rows, columns), BF16),
            jax.ShapeDtypeStruct((rows, 2 * columns), BF16),
        ]
        + shapes,
        scratch_shapes=[pltpu.VMEM((columns, width), BF16)],
        compiler_params=pltpu.CompilerParams(vmem_limit_bytes=56 << 20),
    )(normed, cot, weights, *previous)


def feedforward_grads_kernel(normed_ref, d_both_ref, hidden_ref, cot_ref, out_ref, down_ref):
    index = pl.program_id(0)
    rows, fused = normed_ref.shape[1], d_both_ref.shape[1]
    piece = down_ref.shape[0] // pl.num_programs(0)

    @pl.when(index == 0)
    def _():
        down_ref[...] = outer_sum(hidden_ref[...], cot_ref[...]).astype(BF16)

    out_ref[0, :rows, :] = outer_sum(normed_ref[...], d_both_ref[...]).astype(BF16)
    mine = down_ref[pl.ds(pl.multiple_of(index * piece, piece), piece), :]
    for part in range(down_ref.shape[1] // fused):
        start = rows + part * piece
        out_ref[0, start : start + piece, :] = mine[:, part * fused : (part + 1) * fused]


def feedforward_grads(normed, d_both, hidden, cot, pieces):
    rows, width = normed.shape
    columns = hidden.shape[1]
    fused = d_both.shape[1]
    out_rows = width // pieces + (columns // pieces) * (width // fused)
    return pl.pallas_call(
        feedforward_grads_kernel,
        grid=(pieces,),
        in_specs=[
            pl.BlockSpec((rows, width // pieces), lambda i: (0, i)),
            whole_spec(d_both.shape),
            whole_spec(hidden.shape),
            whole_spec(cot.shape),
        ],
        out_specs=pl.BlockSpec((1, out_rows, fused), lambda i: (i, 0, 0)),
        out_shape=jax.ShapeDtypeStruct((pieces, out_rows, fused), BF16),
        scratch_shapes=[pltpu.VMEM((columns, width), BF16)],
        compiler_params=pltpu.CompilerParams(vmem_limit_bytes=56 << 20),
    )(normed, d_both, hidden, cot)


def assemble_kernel(pieces, place_ref, *refs):
    inputs, outputs = refs[:-2], refs[-2:]
    here_x = place_ref[1]
    chunks = len(inputs) // 2
    half = inputs[0].shape[1] // 2
    size = half // pieces
    for which, out_ref in enumerate(outputs):
        for step in range(pieces):
            columns = slice(which * half + step * size, which * half + (step + 1) * size)
            own = [inputs[2 * chunk][:, columns].astype(F32) for chunk in range(chunks)]
            moved = [inputs[2 * chunk + 1][:, columns].astype(F32) for chunk in range(chunks)]
            even = [jnp.where(here_x == 0, a, b) for a, b in zip(own, moved)]
            odd = [jnp.where(here_x == 0, b, a) for a, b in zip(own, moved)]
            span = 2 * chunks * size
            out_ref[:, step * span : (step + 1) * span] = jnp.concatenate(even + odd, axis=1)


def assemble(place, inputs, pieces, columns):
    rows, width = inputs[0].shape
    size = min(rows, 64)
    return pl.pallas_call(
        functools.partial(assemble_kernel, pieces),
        grid=(rows // size,),
        in_specs=[pl.BlockSpec(memory_space=pltpu.SMEM)]
        + [pl.BlockSpec((size, width), lambda i: (i, 0))] * len(inputs),
        out_specs=[pl.BlockSpec((size, columns), lambda i: (i, 0))] * 2,
        out_shape=[jax.ShapeDtypeStruct((rows, columns), F32)] * 2,
    )(place, *inputs)


def norm_backward(values, scale, gain, d_normed):
    weighted = d_normed * gain
    d_values = scale * weighted - values * scale * scale * scale * jnp.mean(
        weighted * values, axis=-1, keepdims=True
    )
    return (d_values, jnp.sum(d_normed * values * scale, axis=0))


def take(array, index, axis=0):
    return lax.dynamic_index_in_dim(array, index, axis, keepdims=False)


def choose(position, own, other):
    return [jnp.where(position == 0, own, other), jnp.where(position == 0, other, own)]


def in_order(position, own, other, axis=0):
    return jnp.stack(choose(position, own, other), axis=axis)


def rows_major(array):
    return with_layout_constraint(array, Layout(major_to_minor=tuple(range(array.ndim))))


def gather_z(piece):
    return rows_major(lax.all_gather(rows_major(piece), "z", axis=0))


def reduce_z(parts):
    return lax.psum_scatter(parts, "z", scatter_dimension=0)


def tie(*values):
    return lax.optimization_barrier(values)


def swap_blocks(rows, size, here):
    blocks = []
    for start in range(0, rows.shape[1], 2 * size):
        first, second = rows[:, start : start + size], rows[:, start + size : start + 2 * size]
        blocks += choose(here, first, second)
    return blocks


def gather_tensor(rows):
    beside = lax.ppermute(rows, "y", SWAP)
    return (
        rows,
        lax.ppermute(rows, "c", SWAP),
        beside,
        lax.ppermute(beside, "c", SWAP),
    )


def reduce_tensor(kept, sent):
    arrived = lax.ppermute(sent, "c", SWAP).astype(F32)
    moved = (kept[1].astype(F32) + arrived[1]).astype(BF16)
    return kept[0].astype(F32) + arrived[0] + lax.ppermute(moved, "y", SWAP).astype(F32)


def gather_planes(rows):
    return (
        rows,
        lax.ppermute(rows, "x", SWAP),
        lax.ppermute(rows, "y", SWAP),
        lax.ppermute(rows, ("x", "y"), DIAGONAL),
    )


def join_planes(planes):
    return jnp.concatenate(planes + tuple(lax.ppermute(plane, "c", SWAP) for plane in planes))


def reduce_eight(kept, sent):
    kept = kept.reshape((4, kept.shape[0] // 4) + kept.shape[1:])
    arrived = lax.ppermute(sent.reshape(kept.shape), "c", SWAP)
    sums = [kept[step].astype(F32) + arrived[step].astype(F32) for step in range(4)]
    return sums[0], [part.astype(BF16) for part in sums[1:]]


def finish_eight(total, leaving):
    routes = (("x", SWAP), ("y", SWAP), (("x", "y"), DIAGONAL))
    for part, (axes, pairs) in zip(leaving, routes):
        total = total + lax.ppermute(part, axes, pairs).astype(F32)
    return total


def body(
    tokens,
    cotangent,
    token_slots,
    lengths,
    query_weight,
    key_projection_weight,
    value_projection_weight,
    output_weight,
    gate_weight,
    up_weight,
    down_weight,
    prenorm_gain,
    midnorm_gain,
):
    z_size = lax.axis_size("z")
    here_x = lax.axis_index("x")
    devices = 8 * z_size
    micro, local_rows, width = tokens.shape
    flat_rows = micro * local_rows
    sends = local_rows // devices
    group_rows = 4 * local_rows
    query_cols = query_weight.shape[1]
    kv_cols = key_projection_weight.shape[1]
    fused_cols = query_cols + 2 * kv_cols
    shard_rows = query_weight.shape[0]
    hidden_cols = gate_weight.shape[1]
    block = hidden_cols // (2 * z_size)
    piece = block // CHUNKS
    chunk_cols = z_size * piece
    everywhere = ("z", "x", "y", "c")

    rank = jnp.sum(
        (token_slots[:, None, :] < token_slots[:, :, None]).astype(jnp.int32), axis=2
    )
    order = (
        (rank // sends) * (micro * sends)
        + jnp.arange(micro, dtype=jnp.int32)[:, None] * sends
        + rank % sends
    ).reshape(flat_rows)
    places = jnp.arange(flat_rows, dtype=jnp.int32)
    to_send = (places[:, None] == order[None, :]).astype(BF16)
    local_slot = (token_slots % local_rows).reshape(flat_rows)

    def exchange(rows):
        return lax.all_to_all(
            rows.reshape((devices, micro * sends) + rows.shape[1:]),
            everywhere,
            split_axis=0,
            concat_axis=0,
            tiled=True,
        ).reshape(rows.shape)

    gains = jnp.stack([prenorm_gain, midnorm_gain]).reshape(micro * sends, -1)
    leaving = jnp.concatenate(
        [
            tokens.reshape(flat_rows, width),
            jnp.broadcast_to(local_slot[:, None], (flat_rows, gains.shape[1])).astype(BF16),
        ],
        axis=1,
    )
    leaving = jnp.concatenate(
        [mm(to_send, leaving).astype(BF16), jnp.tile(gains, (devices, 1))], axis=1
    )
    fused_shard = jnp.concatenate(
        [query_weight, key_projection_weight, value_projection_weight], axis=1
    )
    leaving, gate_weight, up_weight, down_weight, cotangent = tie(
        leaving, gate_weight, up_weight, down_weight, cotangent
    )
    arrived = exchange(leaving)
    cot_leaving = mm(to_send, cotangent.reshape(flat_rows, width)).astype(BF16)
    cot_leaving, arrived = tie(cot_leaving, arrived)
    arrived_cot = exchange(cot_leaving)
    arrived_tokens = arrived[:, :width]
    arrived_slots = arrived[:, width].astype(jnp.int32)
    arrived_gains = arrived[:, width + gains.shape[1] :].reshape(
        2 * z_size, 4, 2, -1, gains.shape[1]
    )[:, 0]
    gains = jnp.swapaxes(arrived_gains, 0, 1).reshape(2, width).astype(F32)
    gain_one, gain_two = gains[0:1], gains[1:2]
    arrived_micro = (places // sends) % micro
    to_place = (
        (arrived_slots + arrived_micro * local_rows)[:, None] == places[None, :]
    ).astype(BF16)

    def by_parity(weight):
        blocks = weight.reshape(shard_rows, z_size, 2, CHUNKS, piece)
        return (blocks[:, :, 0], blocks[:, :, 1])

    gate_parts, up_parts = by_parity(gate_weight), by_parity(up_weight)
    ff_shards = []
    for chunk in range(CHUNKS):
        even, odd = [
            jnp.concatenate(
                [
                    parts[parity][:, :, chunk].reshape(shard_rows, chunk_cols)
                    for parts in (gate_parts, up_parts)
                ],
                axis=1,
            )
            for parity in range(2)
        ]
        kept = jnp.where(here_x == 0, even, odd)
        leaving = jnp.where(here_x == 0, odd, even)
        down = down_weight[chunk * piece : (chunk + 1) * piece]
        down_parts = [
            down[:, start : start + 2 * chunk_cols] for start in range(0, width, 2 * chunk_cols)
        ]
        ff_shards.append(
            jnp.concatenate(
                choose(here_x, kept, lax.ppermute(leaving, "x", SWAP)) + down_parts
            )
        )

    fused_own = gather_z(fused_shard).reshape(width // 2, fused_cols)
    fused_own, output_weight, arrived_tokens, *ff_shards = tie(
        fused_own, output_weight, arrived_tokens, *ff_shards
    )
    output_own = gather_z(output_weight)
    fused_other = lax.ppermute(fused_own, "x", SWAP)

    inputs = outer_sum(to_place, arrived_tokens)
    first_scale = rms_scale(inputs)
    first_normed = (inputs * first_scale * gain_one).astype(BF16)
    blocks = swap_blocks(first_normed, shard_rows, here_x)
    first_normed = jnp.concatenate(blocks[0::2] + blocks[1::2], axis=1)
    first_shard, first_normed = tie(ff_shards[0], first_normed)
    ff_weights = [gather_z(first_shard)]
    place = jnp.stack([2 * lax.axis_index("y") + lax.axis_index("c"), here_x]).astype(jnp.int32)
    segments, tables = [], []
    for index in range(micro):
        segment, positions = sequence_layout(lengths[index, 0], group_rows)
        segments.append(segment)
        tables.append(rope_tables(positions, HEAD_SIZE))
    segments = jnp.stack(segments)
    segments = (segments[:, :, None], segments[:, None, :])
    tables = tuple(jnp.stack(table) for table in zip(*tables))
    rows_own = first_normed.reshape(micro, local_rows, width)
    rows_beside = lax.ppermute(rows_own, "y", SWAP)
    output_other = lax.ppermute(output_own, "x", SWAP)
    rows_own, rows_beside, fused_other = tie(rows_own, rows_beside, fused_other)
    output_full = in_order(here_x, output_own, output_other, axis=1).reshape(query_cols, width)
    shared = (fused_own, fused_other, output_full, tables, segments)
    pieces = (
        rows_own,
        lax.ppermute(rows_own, "c", SWAP),
        rows_beside,
        lax.ppermute(rows_beside, "c", SWAP),
    )
    normed_all, fused, heads, kept, sent = attention_forward(place, pieces, *shared)
    cot_rows = outer_sum(to_place, arrived_cot).astype(BF16)
    cot_planes = gather_planes(cot_rows)
    kept, sent, *cot_planes = tie(kept, sent, *cot_planes)
    for shard in ff_shards[1:]:
        shard, sent = tie(shard, sent)
        ff_weights.append(gather_z(shard))
    attended = reduce_tensor(kept, sent).reshape(flat_rows, width)
    cot_all = join_planes(tuple(cot_planes))
    residual = inputs + attended

    second_scale = rms_scale(residual)
    normed_two = (residual * second_scale * gain_two).astype(BF16)
    normed_two_all = join_planes(gather_planes(normed_two))

    previous = ()
    gate_kept, gate_moved, down_grads = [], [], []
    for chunk in range(CHUNKS):
        hidden, d_both, *previous = feedforward(
            normed_two_all, cot_all, ff_weights[chunk], chunk_cols, previous, chunk == CHUNKS - 1
        )
        part = feedforward_grads(normed_two_all, d_both, hidden, cot_all, z_size)
        if chunk == CHUNKS - 1:
            d_own, d_leaving = reduce_eight(*previous[2:])
            part, d_own = tie(part, d_own)
        total = reduce_z(part)
        own, other = choose(here_x, total[:shard_rows], total[shard_rows : 2 * shard_rows])
        gate_kept.append(own)
        gate_moved.append(other)
        down_grads.append(
            jnp.concatenate(
                [
                    total[start : start + piece]
                    for start in range(2 * shard_rows, total.shape[0], piece)
                ],
                axis=1,
            )
        )
    down_grad = jnp.concatenate(down_grads, axis=0).astype(F32)

    d_normed_two = finish_eight(d_own, d_leaving)
    d_through, d_gain_two = norm_backward(residual, second_scale, gain_two, d_normed_two)
    d_residual = cot_rows.astype(F32) + d_through

    pieces = gather_tensor(d_residual.astype(BF16).reshape(micro, local_rows, width))
    out_own, out_leaving = reduce_eight(*previous[:2])
    *pieces, out_own = tie(*pieces, out_own)
    out_over_x = lax.ppermute(jnp.stack([out_leaving[0], out_leaving[2]]), "x", SWAP)
    kept, sent, *weight_parts = attention_backward(
        place, pieces, *shared, normed_all, fused, heads, output_weight.shape[0]
    )
    kept, sent, out_over_x = tie(kept, sent, out_over_x)
    out_over_y = (out_leaving[1].astype(F32) + out_over_x[1].astype(F32)).astype(BF16)
    layer_rows = (
        residual
        + (out_own + out_over_x[0].astype(F32))
        + lax.ppermute(out_over_y, "y", SWAP).astype(F32)
    )
    d_normed_one = reduce_tensor(kept, sent).reshape(flat_rows, width)
    swapped = swap_blocks(
        jnp.concatenate(
            [
                d_normed_one[:, side * (width // 2) + start : side * (width // 2) + start + shard_rows]
                for start in range(0, width // 2, shard_rows)
                for side in range(2)
            ],
            axis=1,
        ),
        shard_rows,
        here_x,
    )
    d_normed_one = jnp.concatenate(swapped, axis=1)

    def reduce_x(kept, leaving):
        return (kept.astype(F32) + lax.ppermute(leaving, "x", SWAP).astype(F32)).astype(BF16)

    def reduce_data(total):
        return reduce_z(total.reshape(z_size, -1, total.shape[-1])).astype(F32)

    output_total, fused_sent = tie(reduce_x(*weight_parts[2:]), weight_parts[1])
    fused_total, *gate_moved = tie(reduce_x(weight_parts[0], fused_sent), *gate_moved)
    gate_moved = [lax.ppermute(part, "x", SWAP) for part in gate_moved]
    output_grad = reduce_data(output_total)
    fused_grad = reduce_data(fused_total)
    d_first, d_gain_one = norm_backward(inputs, first_scale, gain_one, d_normed_one)
    input_grads = (d_residual + d_first).astype(BF16)

    gain_grads = jnp.stack([d_gain_one, d_gain_two])
    high = gain_grads.astype(BF16)
    low = (gain_grads - high.astype(F32)).astype(BF16)
    riders = jnp.stack([high, low]).reshape(2, 2, 2 * z_size, 1, shard_rows)
    riders = jnp.broadcast_to(
        jnp.transpose(riders, (2, 3, 0, 1, 4)), (2 * z_size, 4, 2, 2, shard_rows)
    ).reshape(flat_rows, -1)

    back = jnp.concatenate([layer_rows.astype(BF16), input_grads], axis=1)
    returned = exchange(jnp.concatenate([mm(to_place, back).astype(BF16), riders], axis=1))
    returned, *gate_moved = tie(returned, *gate_moved)
    gate_up_grads = assemble(
        place, [part for pair in zip(gate_kept, gate_moved) for part in pair], z_size, hidden_cols
    )
    outputs = outer_sum(to_send, returned[:, : 2 * width]).astype(BF16)
    outputs = outputs.reshape(micro, local_rows, 2 * width)
    gain_grads = jnp.sum(
        returned[:, 2 * width :].astype(F32).reshape(devices, 2, 2, shard_rows), axis=(0, 1)
    )

    return (
        outputs[:, :, :width],
        outputs[:, :, width:],
        fused_grad[:, :query_cols],
        fused_grad[:, query_cols : query_cols + kv_cols],
        fused_grad[:, query_cols + kv_cols :],
        output_grad,
        *gate_up_grads,
        down_grad,
        gain_grads[0],
        gain_grads[1],
    )


def solution(mesh):
    z_size = mesh.shape["dp"] // 2
    fine = Mesh(mesh.devices.reshape(z_size, 2, 2, 2), ("z", "x", "y", "c"))
    dp, tensor = ("z", "x"), ("y", "c")
    rows, columns, stacked = P(None, dp + tensor, None), P(dp, tensor), P(tensor + dp, None)
    return jax.shard_map(
        body,
        mesh=fine,
        in_specs=(
            rows,
            rows,
            P(None, dp + tensor),
            P(None, dp, None),
            columns,
            columns,
            columns,
            stacked,
            columns,
            columns,
            stacked,
            P(dp),
            P(dp),
        ),
        out_specs=(
            rows,
            rows,
            columns,
            columns,
            columns,
            stacked,
            columns,
            columns,
            stacked,
            P(dp),
            P(dp),
        ),
        check_vma=False,
    )
```

time: 1310 us -> 744 us (0.57)
  waiting for transfers between devices: 672 us -> 374 us
  matrix products: 216 us -> 9.99 us
  Pallas kernels: 0 us -> 167 us
  starting transfers between devices: 168 us -> 47.9 us
  local copies, waits for them, and re-layouts: 137 us -> 45.4 us
  other arithmetic: 100 us -> 76.8 us
    ppermute x90 -> x34, waiting for transfers between devices: 646 us -> 215 us  [the longest x3 38 us: finish_eight(): total = total + lax.ppermute(part, axes, pairs).astype(F32)]
    pallas_call x0 -> x7, Pallas kernels: none -> 167 us  [the longest x2 73.3 us: feedforward(): pl.pallas_call(functools.partial(feedforward_kernel, bool(previous), last...]
    ppermute x90 -> x34, starting transfers between devices: 139 us -> 27.1 us  [the longest x2 3.71 us: gather_planes(): lax.ppermute(rows, ('x', 'y'), DIAGONAL)]
    dot_general x18 -> x0, matrix products: 86.2 us -> none  [the longest x6 71.2 us: times_transposed(): lax.dot_general(left, right, (((1,), (1,)), ((), ())), preferred_element_...]
    all_to_all x5 -> x3, waiting for transfers between devices: 0.01 us -> 78.8 us  [exchange(): lax.all_to_all(rows.reshape((devices, micro * sends) + rows.shape[1:]), e...]
    dot_general x10 -> x3, matrix products: 66.3 us -> 3.96 us  [mm(): return jnp.dot(left, right, preferred_element_type=F32)]
    dot_general x10 -> x3, matrix products: 63.3 us -> 6.04 us  [outer_sum(): lax.dot_general(left, right, (((0,), (0,)), ((), ())), preferred_element_...]
    all_gather x0 -> x4, waiting for transfers between devices: none -> 42.4 us  [gather_z(): return rows_major(lax.all_gather(rows_major(piece), 'z', axis=0))]
  transfers between devices with their start and end apart: 103 -> 50, of which waited for: 38 -> 22; matrix products, arithmetic and copies ran while one was open for 31% -> 14% of each run, Pallas kernels for 0% -> 23%
where the time goes in v2:
time: 744 us; the launch traced here: 737 us
  waiting for transfers between devices  374 us (50%)
  Pallas kernels  167 us (22%)
  other arithmetic  76.8 us (10%)
  starting transfers between devices  47.9 us (6%)
  local copies, waits for them, and re-layouts  45.4 us (6%)
  between operations  15.5 us (2%)
  matrix products  9.99 us (1%)
    all_to_all x3, waiting for transfers between devices, exchange(): lax.all_to_all(rows.reshape((devices, micro * sends) + rows.shape[1:]), e...  78.8 us
    pallas_call x2, Pallas kernels, feedforward(): pl.pallas_call(functools.partial(feedforward_kernel, bool(previous), last...  73.3 us
    all_gather x4, waiting for transfers between devices, gather_z(): return rows_major(lax.all_gather(rows_major(piece), 'z', axis=0))  42.4 us
    pallas_call x2, Pallas kernels, feedforward_grads(): pl.pallas_call(feedforward_grads_kernel, grid=(pieces,), in_specs=[pl.Blo...  42.1 us
    ppermute x3, waiting for transfers between devices, finish_eight(): total = total + lax.ppermute(part, axes, pairs).astype(F32)  38 us
    pallas_call x1, Pallas kernels, attention_backward(): pl.pallas_call(functools.partial(attention_backward_kernel, query_cols //...  30.7 us
    ppermute x2, waiting for transfers between devices, reduce_tensor(): lax.ppermute(moved, 'y', SWAP).astype(F32)  27.3 us
    ppermute x1, waiting for transfers between devices, body(): output_other = lax.ppermute(output_own, 'x', SWAP)  22.5 us
  transfers between devices with their start and end apart: 50, of which 22 were waited for; matrix products, arithmetic and copies ran while one was open for 14% of the time, Pallas kernels for 23%

profile of v2, /device:TPU:0, one launch (start us, length us, event | category | flops | bytes accessed | tf_op | source)
XLA Modules:
  0.0 737.0 jit_solution(15814476122276573923)
XLA Ops:
  46.6 16.0 %collective-permute-done = bf16[256,1024]{1,0:T(8,128)(2,1)S(1)} collective-permute-done((bf16[256,1024]{1,0:T(8,128)(2,1)S(1)}, bf16[256,1024]{1,0:T(8,128)(2,1)S(1)}, u32[]{:S(2)}, u32[]{:S(2)}) %collective-permute-start) | collective-permute-done | bytes 524320 | tf_op jit(solution)/shard_map/ppermute | solution.py:716
  64.7 17.9 %all-to-all-done = bf16[32,8,2176]{2,1,0:T(8,128)(2,1)S(1)} async-done(((bf16[32,8,2176]{2,1,0:T(8,128)(2,1)}), bf16[32,8,2176]{2,1,0:T(8,128)(2,1)S(1)}, u32[]{:S(2)}, u32[]{:S(2)}) %all-to-all-start) | async-done | bytes 1114144 | tf_op jit(solution)/shard_map/all_to_all | solution.py:650
  83.9 12.7 %all-gather.9.cloned.1.call-done.own_ref = bf16[1024,1024]{1,0:T(8,128)(2,1)} async-done(((bf16[256,1024]{1,0:T(8,128)(2,1)}), bf16[1024,1024]{1,0:T(8,128)(2,1)}) %all-gather.9.cloned.1.call-update) | async-done | bytes 2097168 | tf_op jit(solution)/shard_map/all_gather | solution.py:543
  114.0 29.7 %all-gather.11.cloned.1.call-done = bf16[256,2048]{1,0:T(8,128)(2,1)} async-done(((bf16[64,2048]{1,0:T(8,128)(2,1)}), bf16[256,2048]{1,0:T(8,128)(2,1)}) %all-gather.11.cloned.1.call-update) | async-done | bytes 1048592 | tf_op jit(solution)/shard_map/all_gather | solution.py:543
  154.1 13.6 %collective-permute-done.3.other_ref = bf16[1024,1024]{1,0:T(8,128)(2,1)} collective-permute-done((bf16[1024,1024]{1,0:T(8,128)(2,1)}, bf16[1024,1024]{1,0:T(8,128)(2,1)}, u32[]{:S(2)}, u32[]{:S(2)}) %collective-permute-start.3) | collective-permute-done | bytes 2097184 | tf_op jit(solution)/shard_map/ppermute | solution.py:725
  167.6 22.5 %collective-permute-done.6 = bf16[4,64,2048]{2,1,0:T(8,128)(2,1)} collective-permute-done((bf16[4,64,2048]{2,1,0:T(8,128)(2,1)}, bf16[4,64,2048]{2,1,0:T(8,128)(2,1)}, u32[]{:S(2)}, u32[]{:S(2)}) %collective-permute-start.6) | collective-permute-done | bytes 1048608 | tf_op jit(solution)/shard_map/ppermute | solution.py:745
  195.9 17.1 %shard_map.212 = (bf16[1024,2048]{1,0:T(8,128)(2,1)}, bf16[1024,1024]{1,0:T(8,128)(2,1)}, bf16[1024,512]{1,0:T(8,128)(2,1)}, bf16[2,2,128,2048]{3,2,1,0:T(8,128)(2,1)}, bf16[2,2,128,2048]{3,2,1,0:T(8,128)(2,1)}) custom-call(s32[2]{0:T(128)} %pad_add_fusion.1.place_ref, bf16[2,128,2048]{2,1,0:T(8,128)(2,1)} %bitcast.19.piece0, ...), custom_call_target="tpu_custom_call" | custom-call | tf_op jit(solution)/shard_map/pallas_call | solution.py:294
  213.1 22.3 %collective-permute-done.9 = bf16[256,2048]{1,0:T(8,128)(2,1)S(1)} collective-permute-done((bf16[256,2048]{1,0:T(8,128)(2,1)S(1)}, bf16[256,2048]{1,0:T(8,128)(2,1)S(1)}, u32[]{:S(2)}, u32[]{:S(2)}) %collective-permute-start.9) | collective-permute-done | bytes 1048608 | tf_op jit(solution)/shard_map/ppermute | solution.py:583
  247.3 22.4 %collective-permute-done.11 = bf16[2,128,2048]{2,1,0:T(8,128)(2,1)} collective-permute-done((bf16[2,128,2048]{2,1,0:T(8,128)(2,1)}, bf16[2,128,2048]{2,1,0:T(8,128)(2,1)}, u32[]{:S(2)}, u32[]{:S(2)}) %collective-permute-start.11) | collective-permute-done | bytes 1048608 | tf_op jit(solution)/shard_map/ppermute | solution.py:575
  278.6 21.8 %collective-permute-done.12 = bf16[256,2048]{1,0:T(8,128)(2,1)S(1)} collective-permute-done((bf16[256,2048]{1,0:T(8,128)(2,1)S(1)}, bf16[256,2048]{1,0:T(8,128)(2,1)S(1)}, u32[]{:S(2)}, u32[]{:S(2)}) %collective-permute-start.12) | collective-permute-done | bytes 1048608 | tf_op jit(solution)/shard_map/ppermute | solution.py:581
  300.5 21.1 %collective-permute-done.13 = bf16[256,2048]{1,0:T(8,128)(2,1)S(1)} collective-permute-done((bf16[256,2048]{1,0:T(8,128)(2,1)S(1)}, bf16[256,2048]{1,0:T(8,128)(2,1)S(1)}, u32[]{:S(2)}, u32[]{:S(2)}) %collective-permute-start.13) | collective-permute-done | bytes 1048608 | tf_op jit(solution)/shard_map/ppermute | solution.py:582
  329.5 34.8 %shard_map.213 = (bf16[2048,512]{1,0:T(8,128)(2,1)}, bf16[2048,1024]{1,0:T(8,128)(2,1)}, f32[2048,2048]{1,0:T(8,128)}, f32[2048,2048]{1,0:T(8,128)}) custom-call(bf16[2048,2048]{1,0:T(8,128)(2,1)} %constant_dynamic-update-slice_fusion.normed_ref, bf16[2048,2048]{1,0:T(8,128)(2,1)} %copy-done.2, bf16[4,768,1024]{2,1,0:T(8,128)(2,1)} %bitcast.237), custom_call_target="tpu_custom_call" | custom-call | tf_op jit(solution)/shard_map/pallas_call | solution.py:435
  364.3 21.1 %shard_map.217 = bf16[4,768,1024]{2,1,0:T(8,128)(2,1)} custom-call(bf16[2048,2048]{1,0:T(8,128)(2,1)} %constant_dynamic-update-slice_fusion.normed_ref, bf16[2048,1024]{1,0:T(8,128)(2,1)} %get-tuple-element.131.d_both_ref, bf16[2048,512]{1,0:T(8,128)(2,1)} %get-tuple-element.132.hidden_ref, bf16[2048,2048]{1,0:T(8,128)(2,1)} %copy-done.2), custom_call_target="tpu_custom_call" | custom-call | tf_op jit(solution)/shard_map/pallas_call | solution.py:472
  385.6 38.6 %shard_map.214 = (bf16[2048,512]{1,0:T(8,128)(2,1)}, bf16[2048,1024]{1,0:T(8,128)(2,1)}, bf16[1024,2048]{1,0:T(8,128)(2,1)}, bf16[1024,2048]{1,0:T(8,128)(2,1)},...) custom-call(bf16[2048,2048]{1,0:T(8,128)(2,1)} %constant_dynamic-update-slice_fusion.normed_ref, ...), custom_call_target="tpu_custom_call" | custom-call | tf_op jit(solution)/shard_map/pallas_call | solution.py:435
  424.3 21.1 %shard_map.215 = bf16[4,768,1024]{2,1,0:T(8,128)(2,1)} custom-call(bf16[2048,2048]{1,0:T(8,128)(2,1)} %constant_dynamic-update-slice_fusion.normed_ref, bf16[2048,1024]{1,0:T(8,128)(2,1)} %get-tuple-element.106.d_both_ref, bf16[2048,512]{1,0:T(8,128)(2,1)} %get-tuple-element.107.hidden_ref, bf16[2048,2048]{1,0:T(8,128)(2,1)} %copy-done.2), custom_call_target="tpu_custom_call" | custom-call | tf_op jit(solution)/shard_map/pallas_call | solution.py:472
  445.4 7.3 fusion.19
  464.4 15.3 %collective-permute-done.24 = bf16[256,2048]{1,0:T(8,128)(2,1)S(1)} collective-permute-done((bf16[256,2048]{1,0:T(8,128)(2,1)}, bf16[256,2048]{1,0:T(8,128)(2,1)S(1)}, u32[]{:S(2)}, u32[]{:S(2)}) %collective-permute-start.24) | collective-permute-done | bytes 1048608 | tf_op jit(solution)/shard_map/ppermute | solution.py:601
  479.8 22.7 %collective-permute-done.25 = bf16[256,2048]{1,0:T(8,128)(2,1)S(1)} collective-permute-done((bf16[256,2048]{1,0:T(8,128)(2,1)}, bf16[256,2048]{1,0:T(8,128)(2,1)S(1)}, u32[]{:S(2)}, u32[]{:S(2)}) %collective-permute-start.25) | collective-permute-done | bytes 1048608 | tf_op jit(solution)/shard_map/ppermute | solution.py:601
  508.4 20.1 %collective-permute-done.28.piece2 = bf16[2,128,2048]{2,1,0:T(8,128)(2,1)S(1)} collective-permute-done((bf16[2,128,2048]{2,1,0:T(8,128)(2,1)S(1)}, bf16[2,128,2048]{2,1,0:T(8,128)(2,1)S(1)}, u32[]{:S(2)}, u32[]{:S(2)}) %collective-permute-start.28) | collective-permute-done | bytes 1048608 | tf_op jit(solution)/shard_map/ppermute | solution.py:563
  533.8 30.7 %shard_map.216 = (bf16[2,2,128,2048]{3,2,1,0:T(8,128)(2,1)}, bf16[2,2,128,2048]{3,2,1,0:T(8,128)(2,1)}, bf16[1024,1024]{1,0:T(8,128)(2,1)}, bf16[1024,1024]{1,0:...) custom-call(s32[2]{0:T(128)} %pad_add_fusion.1.place_ref, bf16[2,128,2048]{2,1,0:T(8,128)(2,1)} %bitcast.245, ...), custom_call_target="tpu_custom_call" | custom-call | tf_op jit(solution)/shard_map/pallas_call | solution.py:327
  577.2 13.1 %collective-permute-done.35 = bf16[256,2048]{1,0:T(8,128)(2,1)S(1)} collective-permute-done((bf16[256,2048]{1,0:T(8,128)(2,1)}, bf16[256,2048]{1,0:T(8,128)(2,1)S(1)}, u32[]{:S(2)}, u32[]{:S(2)}) %collective-permute-start.35) | collective-permute-done | bytes 1048608 | tf_op jit(solution)/shard_map/ppermute | solution.py:829
  602.7 17.1 %collective-permute-done.32 = bf16[256,2048]{1,0:T(8,128)(2,1)} collective-permute-done((bf16[256,2048]{1,0:T(8,128)(2,1)}, bf16[256,2048]{1,0:T(8,128)(2,1)}, u32[]{:S(2)}, u32[]{:S(2)}) %collective-permute-start.32) | collective-permute-done | bytes 1048608 | tf_op jit(solution)/shard_map/ppermute | solution.py:811
  634.7 7.0 collective-permute-done.36
  656.2 60.9 %all-to-all-done.2 = bf16[32,8,4224]{2,1,0:T(8,128)(2,1)} async-done(((bf16[32,8,4224]{2,1,0:T(8,128)(2,1)}), bf16[32,8,4224]{2,1,0:T(8,128)(2,1)}, u32[]{:S(2)}, u32[]{:S(2)}) %all-to-all-start.2) | async-done | bytes 2162720 | tf_op jit(solution)/shard_map/all_to_all | solution.py:650
  (305 shorter events, 194.8 us)
Async XLA Ops:
  29.9 52.6 %all-to-all-start = ((bf16[32,8,2176]{2,1,0:T(8,128)(2,1)}), bf16[32,8,2176]{2,1,0:T(8,128)(2,1)S(1)}, u32[]{:S(2)}, u32[]{:S(2)}) async-start(bf16[32,8,2176]{2,1,0:T(8,128)(2,1)} %bitcast.241), calls=%async_computation | async-start | bytes 2228224 | tf_op jit(solution)/shard_map/all_to_all | solution.py:650
  34.9 61.8 %all-gather.9.cloned.1.call-start = ((), (), s32[]{:S(2)}) async-start(), calls=%async_computation.11 | async-start | bytes 2621440 | tf_op jit(solution)/shard_map/all_gather | solution.py:543
  36.9 106.8 %all-gather.11.cloned.1.call-start = ((), (), s32[]{:S(2)}) async-start(), calls=%async_computation.12 | async-start | bytes 1310720 | tf_op jit(solution)/shard_map/all_gather | solution.py:543
  96.7 232.9 %all-gather.15.cloned.1.call-start = ((), (), s32[]{:S(2)}) async-start(), calls=%async_computation.14 | async-start | bytes 7864320 | tf_op jit(solution)/shard_map/all_gather | solution.py:543
  108.1 277.5 %all-gather.13.cloned.1.call-start = ((), (), s32[]{:S(2)}) async-start(), calls=%async_computation.13 | async-start | bytes 7864320 | tf_op jit(solution)/shard_map/all_gather | solution.py:543
  108.4 59.2 %collective-permute-start.3 = (bf16[1024,1024]{1,0:T(8,128)(2,1)}, bf16[1024,1024]{1,0:T(8,128)(2,1)}, u32[]{:S(2)}, u32[]{:S(2)}) collective-permute-start(bf16[1024,1024]{1,0:T(8,128)(2,1)} %all-gather.9.cloned.1.call-done.own_ref), channel_id=1, source_target_pairs={{0,4},{4,0},{1,5},{5,1},{2,6},{6,2},{3,7},{7,3},{8,12},{12,8},{9,1... | collective-permute-start | bytes 6291464 | tf_op jit(solution)/shard_map/ppermute | solution.py:725
  150.5 62.5 %collective-permute-start.7 = (bf16[256,2048]{1,0:T(8,128)(2,1)S(1)}, bf16[256,2048]{1,0:T(8,128)(2,1)S(1)}, u32[]{:S(2)}, u32[]{:S(2)}) collective-permute-start(bf16[256,2048]{1,0:T(8,128)(2,1)S(1)} %convolution_convert_fusion.3), channel_id=1, source_target_pairs={{0,4},{4,0},{1,5},{5,1},{2,6},{6,2},{3,7},{7,3},{8,12},{12,8},{9,1... | collective-permute-start | bytes 3145736 | tf_op jit(solution)/shard_map/ppermute | solution.py:581
  151.3 61.7 %collective-permute-start.8 = (bf16[256,2048]{1,0:T(8,128)(2,1)S(1)}, bf16[256,2048]{1,0:T(8,128)(2,1)S(1)}, u32[]{:S(2)}, u32[]{:S(2)}) collective-permute-start(bf16[256,2048]{1,0:T(8,128)(2,1)S(1)} %convolution_convert_fusion.3), channel_id=1, source_target_pairs={{0,2},{2,0},{1,3},{3,1},{4,6},{6,4},{5,7},{7,5},{8,10},{10,8},{9,1... | collective-permute-start | bytes 3145736 | tf_op jit(solution)/shard_map/ppermute | solution.py:582
  152.8 82.6 %collective-permute-start.9 = (bf16[256,2048]{1,0:T(8,128)(2,1)S(1)}, bf16[256,2048]{1,0:T(8,128)(2,1)S(1)}, u32[]{:S(2)}, u32[]{:S(2)}) collective-permute-start(bf16[256,2048]{1,0:T(8,128)(2,1)S(1)} %convolution_convert_fusion.3), channel_id=1, source_target_pairs={{0,6},{6,0},{2,4},{4,2},{1,7},{7,1},{3,5},{5,3},{8,14},{14,8},{10,... | collective-permute-start | bytes 3145736 | tf_op jit(solution)/shard_map/ppermute | solution.py:583
  236.4 396.0 %reduce-scatter.5.cloned.1.call-start = ((), (), s32[]{:S(2)}) async-start(), calls=%async_computation.7 | async-start | bytes 7864320 | tf_op jit(solution)/shard_map/reduce_scatter | solution.py:547
  245.4 55.0 %collective-permute-start.22 = (bf16[256,2048]{1,0:T(8,128)(2,1)}, bf16[256,2048]{1,0:T(8,128)(2,1)S(1)}, u32[]{:S(2)}, u32[]{:S(2)}) collective-permute-start(bf16[256,2048]{1,0:T(8,128)(2,1)} %copy-done.23), channel_id=1, source_target_pairs={{0,1},{1,0},{2,3},{3,2},{4,5},{5,4},{6,7},{7,6},{8,9},{9,8},{10,11... | collective-permute-start | bytes 3145736 | tf_op jit(solution)/shard_map/ppermute | solution.py:588
  274.9 46.7 %collective-permute-start.13 = (bf16[256,2048]{1,0:T(8,128)(2,1)S(1)}, bf16[256,2048]{1,0:T(8,128)(2,1)S(1)}, u32[]{:S(2)}, u32[]{:S(2)}) collective-permute-start(bf16[256,2048]{1,0:T(8,128)(2,1)S(1)} %get-tuple-element.149), channel_id=1, source_target_pairs={{0,2},{2,0},{1,3},{3,1},{4,6},{6,4},{5,7},{7,5},{8,10},{10,8},{9,1... | collective-permute-start | bytes 3145736 | tf_op jit(solution)/shard_map/ppermute | solution.py:582
  275.7 46.9 %collective-permute-start.14 = (bf16[256,2048]{1,0:T(8,128)(2,1)S(1)}, bf16[256,2048]{1,0:T(8,128)(2,1)S(1)}, u32[]{:S(2)}, u32[]{:S(2)}) collective-permute-start(bf16[256,2048]{1,0:T(8,128)(2,1)S(1)} %get-tuple-element.149), channel_id=1, source_target_pairs={{0,6},{6,0},{2,4},{4,2},{1,7},{7,1},{3,5},{5,3},{8,14},{14,8},{10,... | collective-permute-start | bytes 3145736 | tf_op jit(solution)/shard_map/ppermute | solution.py:583
  278.4 46.9 %collective-permute-start.15 = (bf16[256,2048]{1,0:T(8,128)(2,1)S(1)}, bf16[256,2048]{1,0:T(8,128)(2,1)S(1)}, u32[]{:S(2)}, u32[]{:S(2)}) collective-permute-start(bf16[256,2048]{1,0:T(8,128)(2,1)S(1)} %get-tuple-element.149), channel_id=1, source_target_pairs={{0,1},{1,0},{2,3},{3,2},{4,5},{5,4},{6,7},{7,6},{8,9},{9,8},{10,11... | collective-permute-start | bytes 3145736 | tf_op jit(solution)/shard_map/ppermute | solution.py:588
  385.4 260.3 %reduce-scatter.7.cloned.1.call-start = ((), (), s32[]{:S(2)}) async-start(), calls=%async_computation.8 | async-start | bytes 7864320 | tf_op jit(solution)/shard_map/reduce_scatter | solution.py:547
  452.7 199.0 %reduce-scatter.11.cloned.1.call-start = ((), (), s32[]{:S(2)}) async-start(), calls=%async_computation.10 | async-start | bytes 1310720 | tf_op jit(solution)/shard_map/reduce_scatter | solution.py:547
  454.9 47.5 %collective-permute-start.25 = (bf16[256,2048]{1,0:T(8,128)(2,1)}, bf16[256,2048]{1,0:T(8,128)(2,1)S(1)}, u32[]{:S(2)}, u32[]{:S(2)}) collective-permute-start(bf16[256,2048]{1,0:T(8,128)(2,1)} %get-tuple-element.156), channel_id=1, source_target_pairs={{0,2},{2,0},{1,3},{3,1},{4,6},{6,4},{5,7},{7,5},{8,10},{10,8},{9,1... | collective-permute-start | bytes 3145736 | tf_op jit(solution)/shard_map/ppermute | solution.py:601
  455.6 46.8 %collective-permute-start.26 = (bf16[256,2048]{1,0:T(8,128)(2,1)}, bf16[256,2048]{1,0:T(8,128)(2,1)S(1)}, u32[]{:S(2)}, u32[]{:S(2)}) collective-permute-start(bf16[256,2048]{1,0:T(8,128)(2,1)} %get-tuple-element.155), channel_id=1, source_target_pairs={{0,6},{6,0},{2,4},{4,2},{1,7},{7,1},{3,5},{5,3},{8,14},{14,8},{10,... | collective-permute-start | bytes 3145736 | tf_op jit(solution)/shard_map/ppermute | solution.py:601
  507.5 57.0 %collective-permute-start.31 = (bf16[2,256,2048]{2,1,0:T(8,128)(2,1)}, bf16[2,256,2048]{2,1,0:T(8,128)(2,1)}, u32[]{:S(2)}, u32[]{:S(2)}) collective-permute-start(bf16[2,256,2048]{2,1,0:T(8,128)(2,1)} %pad_maximum_fusion.2), channel_id=1, source_target_pairs={{0,4},{4,0},{1,5},{5,1},{2,6},{6,2},{3,7},{7,3},{8,12},{12,8},{9,1... | collective-permute-start | bytes 6291464 | tf_op jit(solution)/shard_map/ppermute | solution.py:802
  591.7 49.9 %collective-permute-start.36 = (bf16[1024,1024]{1,0:T(8,128)(2,1)}, bf16[1024,1024]{1,0:T(8,128)(2,1)}, u32[]{:S(2)}, u32[]{:S(2)}) collective-permute-start(bf16[1024,1024]{1,0:T(8,128)(2,1)} %get-tuple-element.130), channel_id=1, source_target_pairs={{0,4},{4,0},{1,5},{5,1},{2,6},{6,2},{3,7},{7,3},{8,12},{12,8},{9,1... | collective-permute-start | bytes 6291464 | tf_op jit(solution)/shard_map/ppermute | solution.py:829
  627.0 90.0 %all-to-all-start.2 = ((bf16[32,8,4224]{2,1,0:T(8,128)(2,1)}), bf16[32,8,4224]{2,1,0:T(8,128)(2,1)}, u32[]{:S(2)}, u32[]{:S(2)}) async-start(bf16[32,8,4224]{2,1,0:T(8,128)(2,1)} %pad_maximum_fusion), calls=%async_computation.2 | async-start | bytes 4325376 | tf_op jit(solution)/shard_map/all_to_all | solution.py:650
  632.4 94.5 %reduce-scatter.9.cloned.1.call-start = ((), (), s32[]{:S(2)}) async-start(), calls=%async_computation.9 | async-start | bytes 2621440 | tf_op jit(solution)/shard_map/reduce_scatter | solution.py:547
  648.8 68.3 %collective-permute-start.37 = (bf16[256,1024]{1,0:T(8,128)(2,1)S(1)}, bf16[256,1024]{1,0:T(8,128)(2,1)S(1)}, u32[]{:S(2)}, u32[]{:S(2)}) collective-permute-start(bf16[256,1024]{1,0:T(8,128)(2,1)S(1)} %get-tuple-element.134), channel_id=1, source_target_pairs={{0,4},{4,0},{1,5},{5,1},{2,6},{6,2},{3,7},{7,3},{8,12},{12,8},{9,1... | collective-permute-start | bytes 1572872 | tf_op jit(solution)/shard_map/ppermute | solution.py:836
  651.7 65.4 %collective-permute-start.38 = (bf16[256,1024]{1,0:T(8,128)(2,1)S(1)}, bf16[256,1024]{1,0:T(8,128)(2,1)S(1)}, u32[]{:S(2)}, u32[]{:S(2)}) collective-permute-start(bf16[256,1024]{1,0:T(8,128)(2,1)S(1)} %get-tuple-element.135), channel_id=1, source_target_pairs={{0,4},{4,0},{1,5},{5,1},{2,6},{6,2},{3,7},{7,3},{8,12},{12,8},{9,1... | collective-permute-start | bytes 1572872 | tf_op jit(solution)/shard_map/ppermute | solution.py:836
  (59 other events, 1008.0 us)
Sparse Core Ops, SparseCore 0:
  37.8 58.7 all-gather.8
  98.2 45.4 all-gather.10
  145.3 114.4 all-gather.14
  261.1 113.5 all-gather.12
  385.5 110.7 reduce-scatter.4
  498.4 111.2 reduce-scatter.6
  612.6 29.7 reduce-scatter.10
  647.9 67.7 reduce-scatter.8

commit v3 on v2

--- a/solution.py
+++ b/solution.py
@@ -485,6 +485,37 @@
     )(normed, d_both, hidden, cot)
 
 
+def split_kernel(pieces, place_ref, gate_ref, up_ref, *refs):
+    here_x = place_ref[1]
+    chunks = len(refs) // 2
+    size = gate_ref.shape[1] // (2 * chunks * pieces)
+    for chunk in range(chunks):
+        sides = []
+        for side in range(2):
+            starts = [(2 * chunks * step + side * chunks + chunk) * size for step in range(pieces)]
+            sides.append(
+                jnp.concatenate(
+                    [ref[:, at : at + size] for ref in (gate_ref, up_ref) for at in starts], axis=1
+                )
+            )
+        refs[2 * chunk][...] = jnp.where(here_x == 0, sides[0], sides[1])
+        refs[2 * chunk + 1][...] = jnp.where(here_x == 0, sides[1], sides[0])
+
+
+def split(place, gate, up, pieces):
+    rows, columns = gate.shape
+    size = min(rows, 64)
+    fused = 2 * columns // (2 * CHUNKS)
+    return pl.pallas_call(
+        functools.partial(split_kernel, pieces),
+        grid=(rows // size,),
+        in_specs=[pl.BlockSpec(memory_space=pltpu.SMEM)]
+        + [pl.BlockSpec((size, columns), lambda i: (i, 0))] * 2,
+        out_specs=[pl.BlockSpec((size, fused), lambda i: (i, 0))] * (2 * CHUNKS),
+        out_shape=[jax.ShapeDtypeStruct((rows, fused), BF16)] * (2 * CHUNKS),
+    )(place, gate, up)
+
+
 def assemble_kernel(pieces, place_ref, *refs):
     inputs, outputs = refs[:-2], refs[-2:]
     here_x = place_ref[1]
@@ -595,11 +626,9 @@
     return sums[0], [part.astype(BF16) for part in sums[1:]]
 
 
-def finish_eight(total, leaving):
+def send_eight(leaving):
     routes = (("x", SWAP), ("y", SWAP), (("x", "y"), DIAGONAL))
-    for part, (axes, pairs) in zip(leaving, routes):
-        total = total + lax.ppermute(part, axes, pairs).astype(F32)
-    return total
+    return [lax.ppermute(part, axes, pairs) for part, (axes, pairs) in zip(leaving, routes)]
 
 
 def body(
@@ -633,6 +662,7 @@
     piece = block // CHUNKS
     chunk_cols = z_size * piece
     everywhere = ("z", "x", "y", "c")
+    place = jnp.stack([2 * lax.axis_index("y") + lax.axis_index("c"), here_x]).astype(jnp.int32)
 
     rank = jnp.sum(
         (token_slots[:, None, :] < token_slots[:, :, None]).astype(jnp.int32), axis=2
@@ -646,14 +676,13 @@
     to_send = (places[:, None] == order[None, :]).astype(BF16)
     local_slot = (token_slots % local_rows).reshape(flat_rows)
 
-    def exchange(rows):
+    def by_device(rows):
+        return rows.reshape((devices, micro * sends) + rows.shape[1:])
+
+    def exchange(blocks):
         return lax.all_to_all(
-            rows.reshape((devices, micro * sends) + rows.shape[1:]),
-            everywhere,
-            split_axis=0,
-            concat_axis=0,
-            tiled=True,
-        ).reshape(rows.shape)
+            blocks, everywhere, split_axis=0, concat_axis=0, tiled=True
+        ).reshape((flat_rows,) + blocks.shape[2:])
 
     gains = jnp.stack([prenorm_gain, midnorm_gain]).reshape(micro * sends, -1)
     leaving = jnp.concatenate(
@@ -669,13 +698,13 @@
     fused_shard = jnp.concatenate(
         [query_weight, key_projection_weight, value_projection_weight], axis=1
     )
-    leaving, gate_weight, up_weight, down_weight, cotangent = tie(
-        leaving, gate_weight, up_weight, down_weight, cotangent
+    leaving, fused_shard, gate_weight, down_weight, cotangent = tie(
+        by_device(leaving), fused_shard, gate_weight, down_weight, cotangent
     )
     arrived = exchange(leaving)
     cot_leaving = mm(to_send, cotangent.reshape(flat_rows, width)).astype(BF16)
     cot_leaving, arrived = tie(cot_leaving, arrived)
-    arrived_cot = exchange(cot_leaving)
+    arrived_cot = exchange(by_device(cot_leaving))
     arrived_tokens = arrived[:, :width]
     arrived_slots = arrived[:, width].astype(jnp.int32)
     arrived_gains = arrived[:, width + gains.shape[1] :].reshape(
@@ -688,25 +717,10 @@
         (arrived_slots + arrived_micro * local_rows)[:, None] == places[None, :]
     ).astype(BF16)
 
-    def by_parity(weight):
-        blocks = weight.reshape(shard_rows, z_size, 2, CHUNKS, piece)
-        return (blocks[:, :, 0], blocks[:, :, 1])
-
-    gate_parts, up_parts = by_parity(gate_weight), by_parity(up_weight)
+    halves = split(place, gate_weight, up_weight, z_size)
     ff_shards = []
     for chunk in range(CHUNKS):
-        even, odd = [
-            jnp.concatenate(
-                [
-                    parts[parity][:, :, chunk].reshape(shard_rows, chunk_cols)
-                    for parts in (gate_parts, up_parts)
-                ],
-                axis=1,
-            )
-            for parity in range(2)
-        ]
-        kept = jnp.where(here_x == 0, even, odd)
-        leaving = jnp.where(here_x == 0, odd, even)
+        kept, leaving = halves[2 * chunk : 2 * chunk + 2]
         down = down_weight[chunk * piece : (chunk + 1) * piece]
         down_parts = [
             down[:, start : start + 2 * chunk_cols] for start in range(0, width, 2 * chunk_cols)
@@ -731,7 +745,6 @@
     first_normed = jnp.concatenate(blocks[0::2] + blocks[1::2], axis=1)
     first_shard, first_normed = tie(ff_shards[0], first_normed)
     ff_weights = [gather_z(first_shard)]
-    place = jnp.stack([2 * lax.axis_index("y") + lax.axis_index("c"), here_x]).astype(jnp.int32)
     segments, tables = [], []
     for index in range(micro):
         segment, positions = sequence_layout(lengths[index, 0], group_rows)
@@ -745,22 +758,24 @@
     output_other = lax.ppermute(output_own, "x", SWAP)
     rows_own, rows_beside, fused_other = tie(rows_own, rows_beside, fused_other)
     output_full = in_order(here_x, output_own, output_other, axis=1).reshape(query_cols, width)
-    shared = (fused_own, fused_other, output_full, tables, segments)
     pieces = (
         rows_own,
         lax.ppermute(rows_own, "c", SWAP),
         rows_beside,
         lax.ppermute(rows_beside, "c", SWAP),
     )
+    cot_rows = outer_sum(to_place, arrived_cot).astype(BF16)
+    cot_beside = lax.ppermute(cot_rows, "y", SWAP)
+    cot_pair, output_full = tie(jnp.stack([cot_rows, cot_beside]), output_full)
+    cot_over_x = lax.ppermute(cot_pair, "x", SWAP)
+    shared = (fused_own, fused_other, output_full, tables, segments)
     normed_all, fused, heads, kept, sent = attention_forward(place, pieces, *shared)
-    cot_rows = outer_sum(to_place, arrived_cot).astype(BF16)
-    cot_planes = gather_planes(cot_rows)
-    kept, sent, *cot_planes = tie(kept, sent, *cot_planes)
     for shard in ff_shards[1:]:
         shard, sent = tie(shard, sent)
         ff_weights.append(gather_z(shard))
     attended = reduce_tensor(kept, sent).reshape(flat_rows, width)
-    cot_all = join_planes(tuple(cot_planes))
+    cot_over_x, attended = tie(cot_over_x, attended)
+    cot_all = join_planes((cot_pair[0], cot_over_x[0], cot_pair[1], cot_over_x[1]))
     residual = inputs + attended
 
     second_scale = rms_scale(residual)
@@ -773,10 +788,12 @@
         hidden, d_both, *previous = feedforward(
             normed_two_all, cot_all, ff_weights[chunk], chunk_cols, previous, chunk == CHUNKS - 1
         )
+        if chunk == CHUNKS - 1:
+            d_own, d_leaving = reduce_eight(*previous[2:])
+            d_both, *d_leaving = tie(d_both, *d_leaving)
         part = feedforward_grads(normed_two_all, d_both, hidden, cot_all, z_size)
         if chunk == CHUNKS - 1:
-            d_own, d_leaving = reduce_eight(*previous[2:])
-            part, d_own = tie(part, d_own)
+            part, *d_arrived = tie(part, *send_eight(d_leaving))
         total = reduce_z(part)
         own, other = choose(here_x, total[:shard_rows], total[shard_rows : 2 * shard_rows])
         gate_kept.append(own)
@@ -792,13 +809,13 @@
         )
     down_grad = jnp.concatenate(down_grads, axis=0).astype(F32)
 
-    d_normed_two = finish_eight(d_own, d_leaving)
+    d_normed_two = d_own + sum(part.astype(F32) for part in d_arrived)
     d_through, d_gain_two = norm_backward(residual, second_scale, gain_two, d_normed_two)
     d_residual = cot_rows.astype(F32) + d_through
 
+    d_residual, *out_parts = tie(d_residual, *previous[:2])
+    out_own, out_leaving = reduce_eight(*out_parts)
     pieces = gather_tensor(d_residual.astype(BF16).reshape(micro, local_rows, width))
-    out_own, out_leaving = reduce_eight(*previous[:2])
-    *pieces, out_own = tie(*pieces, out_own)
     out_over_x = lax.ppermute(jnp.stack([out_leaving[0], out_leaving[2]]), "x", SWAP)
     kept, sent, *weight_parts = attention_backward(
         place, pieces, *shared, normed_all, fused, heads, output_weight.shape[0]
@@ -848,11 +865,13 @@
     ).reshape(flat_rows, -1)
 
     back = jnp.concatenate([layer_rows.astype(BF16), input_grads], axis=1)
-    returned = exchange(jnp.concatenate([mm(to_place, back).astype(BF16), riders], axis=1))
-    returned, *gate_moved = tie(returned, *gate_moved)
+    returned = exchange(
+        by_device(jnp.concatenate([mm(to_place, back).astype(BF16), riders], axis=1))
+    )
     gate_up_grads = assemble(
         place, [part for pair in zip(gate_kept, gate_moved) for part in pair], z_size, hidden_cols
     )
+    returned, *gate_up_grads = tie(returned, *gate_up_grads)
     outputs = outer_sum(to_send, returned[:, : 2 * width]).astype(BF16)
     outputs = outputs.reshape(micro, local_rows, 2 * width)
     gain_grads = jnp.sum(

time: 744 us -> 716 us (0.962)
  waiting for transfers between devices: 374 us -> 338 us
  starting transfers between devices: 47.9 us -> 56 us
    all_gather x4, waiting for transfers between devices: 42.4 us -> 7.27 us  [gather_z(): return rows_major(lax.all_gather(rows_major(piece), 'z', axis=0))]
    ppermute x2, waiting for transfers between devices: 0.01 us -> 26.1 us  [body(): gate_moved = [lax.ppermute(part, 'x', SWAP) for part in gate_moved]]
    ppermute x2 -> x1, waiting for transfers between devices: 21.1 us -> 0.01 us  [gather_planes(): lax.ppermute(rows, 'y', SWAP)]
    ppermute x1, waiting for transfers between devices: 17.1 us -> 1.54 us  [body(): lax.ppermute(out_over_y, 'y', SWAP).astype(F32)]
    ppermute x1, waiting for transfers between devices: 22.5 us -> 10.4 us  [body(): output_other = lax.ppermute(output_own, 'x', SWAP)]
    ppermute x2, waiting for transfers between devices: 27.3 us -> 38.1 us  [reduce_tensor(): lax.ppermute(moved, 'y', SWAP).astype(F32)]
    reduce_scatter x4, starting transfers between devices: 0.95 us -> 10.5 us  [reduce_z(): return lax.psum_scatter(parts, 'z', scatter_dimension=0)]
    ppermute x2 -> x1, waiting for transfers between devices: 21.8 us -> 12.4 us  [gather_planes(): lax.ppermute(rows, 'x', SWAP)]
  transfers between devices with their start and end apart: 50 -> 49, of which waited for: 22 -> 27; matrix products, arithmetic and copies ran while one was open for 14% -> 15% of each run, Pallas kernels for 23% -> 24%
where the time goes in v3:
time: 716 us; the launch traced here: 711 us
  waiting for transfers between devices  338 us (47%)
  Pallas kernels  172 us (24%)
  other arithmetic  74.8 us (10%)
  starting transfers between devices  56 us (8%)
  local copies, waits for them, and re-layouts  43.8 us (6%)
  between operations  15.3 us (2%)
  matrix products  10.9 us (2%)
    all_to_all x3, waiting for transfers between devices, exchange(): lax.all_to_all(blocks, everywhere, split_axis=0, concat_axis=0, tiled=True)  81.5 us
    pallas_call x2, Pallas kernels, feedforward(): pl.pallas_call(functools.partial(feedforward_kernel, bool(previous), last...  73.5 us
    pallas_call x2, Pallas kernels, feedforward_grads(): pl.pallas_call(feedforward_grads_kernel, grid=(pieces,), in_specs=[pl.Blo...  42.2 us
    ppermute x2, waiting for transfers between devices, reduce_tensor(): lax.ppermute(moved, 'y', SWAP).astype(F32)  38.1 us
    pallas_call x1, Pallas kernels, attention_backward(): pl.pallas_call(functools.partial(attention_backward_kernel, query_cols //...  30.8 us
    ppermute x2, waiting for transfers between devices, body(): lax.ppermute(leaving, 'x', SWAP)  27.4 us
    ppermute x2, waiting for transfers between devices, reduce_x(): lax.ppermute(leaving, 'x', SWAP).astype(F32)  26.8 us
    ppermute x2, waiting for transfers between devices, body(): gate_moved = [lax.ppermute(part, 'x', SWAP) for part in gate_moved]  26.1 us
  transfers between devices with their start and end apart: 49, of which 27 were waited for; matrix products, arithmetic and copies ran while one was open for 15% of the time, Pallas kernels for 24%

profile of v3, /device:TPU:0, one launch (start us, length us, event | category | flops | bytes accessed | tf_op | source)
XLA Modules:
  0.0 710.8 jit_solution(305262602826481820)
XLA Ops:
  31.2 15.6 %collective-permute-done.1 = bf16[256,1024]{1,0:T(8,128)(2,1)} collective-permute-done((bf16[256,1024]{1,0:T(8,128)(2,1)}, bf16[256,1024]{1,0:T(8,128)(2,1)}, u32[]{:S(2)}, u32[]{:S(2)}) %collective-permute-start.1) | collective-permute-done | bytes 524320 | tf_op jit(solution)/shard_map/ppermute | solution.py:730
  47.9 11.8 %collective-permute-done = bf16[256,1024]{1,0:T(8,128)(2,1)} collective-permute-done((bf16[256,1024]{1,0:T(8,128)(2,1)}, bf16[256,1024]{1,0:T(8,128)(2,1)}, u32[]{:S(2)}, u32[]{:S(2)}) %collective-permute-start) | collective-permute-done | bytes 524320 | tf_op jit(solution)/shard_map/ppermute | solution.py:730
  62.7 13.4 %all-to-all-done = bf16[32,8,2176]{2,1,0:T(8,128)(2,1)S(1)} async-done(((bf16[32,8,2176]{2,1,0:T(8,128)(2,1)}), bf16[32,8,2176]{2,1,0:T(8,128)(2,1)S(1)}, u32[]{:S(2)}, u32[]{:S(2)}) %all-to-all-start) | async-done | bytes 1114144 | tf_op jit(solution)/shard_map/all_to_all | solution.py:683
  100.6 37.0 %all-to-all-done.1 = bf16[32,8,2048]{2,1,0:T(8,128)(2,1)} async-done(((bf16[32,8,2048]{2,1,0:T(8,128)(2,1)}), bf16[32,8,2048]{2,1,0:T(8,128)(2,1)}, u32[]{:S(2)}, u32[]{:S(2)}) %all-to-all-start.1) | async-done | bytes 1048608 | tf_op jit(solution)/shard_map/all_to_all | solution.py:683
  167.4 10.4 %collective-permute-done.3 = bf16[4,64,2048]{2,1,0:T(8,128)(2,1)} collective-permute-done((bf16[4,64,2048]{2,1,0:T(8,128)(2,1)}, bf16[4,64,2048]{2,1,0:T(8,128)(2,1)}, u32[]{:S(2)}, u32[]{:S(2)}) %collective-permute-start.3) | collective-permute-done | bytes 1048608 | tf_op jit(solution)/shard_map/ppermute | solution.py:758
  182.8 17.2 %shard_map.213 = (bf16[1024,2048]{1,0:T(8,128)(2,1)}, bf16[1024,1024]{1,0:T(8,128)(2,1)}, bf16[1024,512]{1,0:T(8,128)(2,1)}, bf16[2,2,128,2048]{3,2,1,0:T(8,128)(2,1)}, bf16[2,2,128,2048]{3,2,1,0:T(8,128)(2,1)}) custom-call(s32[2]{0:T(128)} %pad_add_fusion.1.place_ref, bf16[2,128,2048]{2,1,0:T(8,128)(2,1)} %bitcast.22.piece0, ...), custom_call_target="tpu_custom_call" | custom-call | tf_op jit(solution)/shard_map/pallas_call | solution.py:294
  213.9 20.6 %collective-permute-done.10 = bf16[2,128,2048]{2,1,0:T(8,128)(2,1)} collective-permute-done((bf16[2,128,2048]{2,1,0:T(8,128)(2,1)}, bf16[2,128,2048]{2,1,0:T(8,128)(2,1)}, u32[]{:S(2)}, u32[]{:S(2)}) %collective-permute-start.10) | collective-permute-done | bytes 1048608 | tf_op jit(solution)/shard_map/ppermute | solution.py:606
  236.6 12.3 %collective-permute-done.4 = bf16[2,256,2048]{2,1,0:T(8,128)(2,1)} collective-permute-done((bf16[2,256,2048]{2,1,0:T(8,128)(2,1)}, bf16[2,256,2048]{2,1,0:T(8,128)(2,1)}, u32[]{:S(2)}, u32[]{:S(2)}) %collective-permute-start.4) | collective-permute-done | bytes 2097184 | tf_op jit(solution)/shard_map/ppermute | solution.py:770
  264.7 12.4 %collective-permute-done.11 = bf16[256,2048]{1,0:T(8,128)(2,1)S(1)} collective-permute-done((bf16[256,2048]{1,0:T(8,128)(2,1)S(1)}, bf16[256,2048]{1,0:T(8,128)(2,1)S(1)}, u32[]{:S(2)}, u32[]{:S(2)}) %collective-permute-start.11) | collective-permute-done | bytes 1048608 | tf_op jit(solution)/shard_map/ppermute | solution.py:612
  279.7 19.4 %collective-permute-done.13 = bf16[256,2048]{1,0:T(8,128)(2,1)S(1)} collective-permute-done((bf16[256,2048]{1,0:T(8,128)(2,1)S(1)}, bf16[256,2048]{1,0:T(8,128)(2,1)S(1)}, u32[]{:S(2)}, u32[]{:S(2)}) %collective-permute-start.13) | collective-permute-done | bytes 1048608 | tf_op jit(solution)/shard_map/ppermute | solution.py:614
  307.1 34.8 %shard_map.214 = (bf16[2048,512]{1,0:T(8,128)(2,1)}, bf16[2048,1024]{1,0:T(8,128)(2,1)}, f32[2048,2048]{1,0:T(8,128)}, f32[2048,2048]{1,0:T(8,128)}) custom-call(bf16[2048,2048]{1,0:T(8,128)(2,1)} %constant_dynamic-update-slice_fusion.normed_ref, bf16[2048,2048]{1,0:T(8,128)(2,1)} %constant_dynamic-update-slice_fusion.8.cot_ref, bf16[4,768,1024]{2,1,0:T(8,128)(2,1)} %bitcast.202), custom_call_target="tpu_custom_call" | custom-call | tf_op jit(solution)/shard_map/pallas_call | solution.py:435
  341.9 21.1 %shard_map.218 = bf16[4,768,1024]{2,1,0:T(8,128)(2,1)} custom-call(bf16[2048,2048]{1,0:T(8,128)(2,1)} %constant_dynamic-update-slice_fusion.normed_ref, bf16[2048,1024]{1,0:T(8,128)(2,1)} %get-tuple-element.138.d_both_ref, bf16[2048,512]{1,0:T(8,128)(2,1)} %get-tuple-element.139.hidden_ref, bf16[2048,2048]{1,0:T(8,128)(2,1)} %constant_dynamic-update-slice_fusion.8.cot_ref), custom_call_target="tpu_custom_call" | custom-call | tf_op jit(solution)/shard_map/pallas_call | solution.py:472
  363.0 10.1 %reduce-scatter.7.cloned.1.call-start = ((), (), s32[]{:S(2)}) async-start(), calls=%async_computation.8 | async-start | bytes 7864320 | tf_op jit(solution)/shard_map/reduce_scatter | solution.py:578
  373.1 38.7 %shard_map.215 = (bf16[2048,512]{1,0:T(8,128)(2,1)}, bf16[2048,1024]{1,0:T(8,128)(2,1)}, bf16[1024,2048]{1,0:T(8,128)(2,1)}, bf16[1024,2048]{1,0:T(8,128)(2,1)},...) custom-call(bf16[2048,2048]{1,0:T(8,128)(2,1)} %constant_dynamic-update-slice_fusion.normed_ref, ...), custom_call_target="tpu_custom_call" | custom-call | tf_op jit(solution)/shard_map/pallas_call | solution.py:435
  428.6 21.2 %shard_map.216 = bf16[4,768,1024]{2,1,0:T(8,128)(2,1)} custom-call(bf16[2048,2048]{1,0:T(8,128)(2,1)} %constant_dynamic-update-slice_fusion.normed_ref, bf16[2048,1024]{1,0:T(8,128)(2,1)} %get-tuple-element.117.d_both_ref, bf16[2048,512]{1,0:T(8,128)(2,1)} %get-tuple-element.118.hidden_ref, bf16[2048,2048]{1,0:T(8,128)(2,1)} %constant_dynamic-update-slice_fusion.8.cot_ref), custom_call_target="tpu_custom_call" | custom-call | tf_op jit(solution)/shard_map/pallas_call | solution.py:472
  451.4 23.7 %collective-permute-done.24 = bf16[256,2048]{1,0:T(8,128)(2,1)} collective-permute-done((bf16[256,2048]{1,0:T(8,128)(2,1)}, bf16[256,2048]{1,0:T(8,128)(2,1)}, u32[]{:S(2)}, u32[]{:S(2)}) %collective-permute-start.24) | collective-permute-done | bytes 1048608 | tf_op jit(solution)/shard_map/ppermute | solution.py:631
  492.6 13.9 %collective-permute-done.28.piece2 = bf16[2,128,2048]{2,1,0:T(8,128)(2,1)S(1)} collective-permute-done((bf16[2,128,2048]{2,1,0:T(8,128)(2,1)S(1)}, bf16[2,128,2048]{2,1,0:T(8,128)(2,1)S(1)}, u32[]{:S(2)}, u32[]{:S(2)}) %collective-permute-start.28) | collective-permute-done | bytes 1048608 | tf_op jit(solution)/shard_map/ppermute | solution.py:594
  510.1 30.8 %shard_map.217 = (bf16[2,2,128,2048]{3,2,1,0:T(8,128)(2,1)}, bf16[2,2,128,2048]{3,2,1,0:T(8,128)(2,1)}, bf16[1024,1024]{1,0:T(8,128)(2,1)}, bf16[1024,1024]{1,0:...) custom-call(s32[2]{0:T(128)} %pad_add_fusion.1.place_ref, bf16[2,128,2048]{2,1,0:T(8,128)(2,1)} %bitcast.209, ...), custom_call_target="tpu_custom_call" | custom-call | tf_op jit(solution)/shard_map/pallas_call | solution.py:327
  549.7 17.1 %collective-permute-done.34 = bf16[256,2048]{1,0:T(8,128)(2,1)S(1)} collective-permute-done((bf16[256,2048]{1,0:T(8,128)(2,1)}, bf16[256,2048]{1,0:T(8,128)(2,1)S(1)}, u32[]{:S(2)}, u32[]{:S(2)}) %collective-permute-start.34) | collective-permute-done | bytes 1048608 | tf_op jit(solution)/shard_map/ppermute | solution.py:846
  575.0 17.5 %collective-permute-done.33 = bf16[2,128,2048]{2,1,0:T(8,128)(2,1)} collective-permute-done((bf16[2,128,2048]{2,1,0:T(8,128)(2,1)}, bf16[2,128,2048]{2,1,0:T(8,128)(2,1)}, u32[]{:S(2)}, u32[]{:S(2)}) %collective-permute-start.33) | collective-permute-done | bytes 1048608 | tf_op jit(solution)/shard_map/ppermute | solution.py:606
  608.4 9.7 %collective-permute-done.35 = bf16[1024,1024]{1,0:T(8,128)(2,1)} collective-permute-done((bf16[1024,1024]{1,0:T(8,128)(2,1)}, bf16[1024,1024]{1,0:T(8,128)(2,1)}, u32[]{:S(2)}, u32[]{:S(2)}) %collective-permute-start.35) | collective-permute-done | bytes 2097184 | tf_op jit(solution)/shard_map/ppermute | solution.py:846
  633.0 16.8 %collective-permute-done.36.refs_1_ = bf16[256,1024]{1,0:T(8,128)(2,1)S(1)} collective-permute-done((bf16[256,1024]{1,0:T(8,128)(2,1)S(1)}, bf16[256,1024]{1,0:T(8,128)(2,1)S(1)}, u32[]{:S(2)}, u32[]{:S(2)}) %collective-permute-start.36) | collective-permute-done | bytes 524320 | tf_op jit(solution)/shard_map/ppermute | solution.py:853
  649.8 9.3 %collective-permute-done.37.refs_3_ = bf16[256,1024]{1,0:T(8,128)(2,1)S(1)} collective-permute-done((bf16[256,1024]{1,0:T(8,128)(2,1)S(1)}, bf16[256,1024]{1,0:T(8,128)(2,1)S(1)}, u32[]{:S(2)}, u32[]{:S(2)}) %collective-permute-start.37) | collective-permute-done | bytes 524320 | tf_op jit(solution)/shard_map/ppermute | solution.py:853
  664.1 31.2 %all-to-all-done.2 = bf16[32,8,4224]{2,1,0:T(8,128)(2,1)} async-done(((bf16[32,8,4224]{2,1,0:T(8,128)(2,1)}), bf16[32,8,4224]{2,1,0:T(8,128)(2,1)}, u32[]{:S(2)}, u32[]{:S(2)}) %all-to-all-start.2) | async-done | bytes 2162720 | tf_op jit(solution)/shard_map/all_to_all | solution.py:683
  (295 shorter events, 229.7 us)
Async XLA Ops:
  7.2 77.6 %all-gather.9.cloned.1.call-start = ((), (), s32[]{:S(2)}) async-start(), calls=%async_computation.11 | async-start | bytes 2621440 | tf_op jit(solution)/shard_map/all_gather | solution.py:574
  15.8 60.4 %all-to-all-start = ((bf16[32,8,2176]{2,1,0:T(8,128)(2,1)}), bf16[32,8,2176]{2,1,0:T(8,128)(2,1)S(1)}, u32[]{:S(2)}, u32[]{:S(2)}) async-start(bf16[32,8,2176]{2,1,0:T(8,128)(2,1)} %pad_maximum_fusion.6), calls=%async_computation | async-start | bytes 2228224 | tf_op jit(solution)/shard_map/all_to_all | solution.py:683
  23.1 117.8 %all-gather.11.cloned.1.call-start = ((), (), s32[]{:S(2)}) async-start(), calls=%async_computation.12 | async-start | bytes 1310720 | tf_op jit(solution)/shard_map/all_gather | solution.py:574
  87.6 219.4 %all-gather.15.cloned.1.call-start = ((), (), s32[]{:S(2)}) async-start(), calls=%async_computation.14 | async-start | bytes 7864320 | tf_op jit(solution)/shard_map/all_gather | solution.py:574
  92.5 45.0 %all-to-all-start.1 = ((bf16[32,8,2048]{2,1,0:T(8,128)(2,1)}), bf16[32,8,2048]{2,1,0:T(8,128)(2,1)}, u32[]{:S(2)}, u32[]{:S(2)}) async-start(bf16[32,8,2048]{2,1,0:T(8,128)(2,1)} %bitcast.211), calls=%async_computation.1 | async-start | bytes 2097152 | tf_op jit(solution)/shard_map/all_to_all | solution.py:683
  96.4 276.7 %all-gather.13.cloned.1.call-start = ((), (), s32[]{:S(2)}) async-start(), calls=%async_computation.13 | async-start | bytes 7864320 | tf_op jit(solution)/shard_map/all_gather | solution.py:574
  96.6 59.2 %collective-permute-start.6 = (bf16[1024,1024]{1,0:T(8,128)(2,1)}, bf16[1024,1024]{1,0:T(8,128)(2,1)}, u32[]{:S(2)}, u32[]{:S(2)}) collective-permute-start(bf16[1024,1024]{1,0:T(8,128)(2,1)} %all-gather.9.cloned.1.call-done.own_ref), channel_id=1, source_target_pairs={{0,4},{4,0},{1,5},{5,1},{2,6},{6,2},{3,7},{7,3},{8,12},{12,8},{9,1... | collective-permute-start | bytes 6291464 | tf_op jit(solution)/shard_map/ppermute | solution.py:739
  99.0 48.5 %collective-permute-start.5 = (bf16[2,128,2048]{2,1,0:T(8,128)(2,1)}, bf16[2,128,2048]{2,1,0:T(8,128)(2,1)}, u32[]{:S(2)}, u32[]{:S(2)}) collective-permute-start(bf16[2,128,2048]{2,1,0:T(8,128)(2,1)} %bitcast.22.piece0), channel_id=1, source_target_pairs={{0,2},{2,0},{1,3},{3,1},{4,6},{6,4},{5,7},{7,5},{8,10},{10,8},{9,1... | collective-permute-start | bytes 3145736 | tf_op jit(solution)/shard_map/ppermute | solution.py:757
  140.9 37.0 %collective-permute-start.3 = (bf16[4,64,2048]{2,1,0:T(8,128)(2,1)}, bf16[4,64,2048]{2,1,0:T(8,128)(2,1)}, u32[]{:S(2)}, u32[]{:S(2)}) collective-permute-start(bf16[4,64,2048]{2,1,0:T(8,128)(2,1)} %bitcast.212), channel_id=1, source_target_pairs={{0,4},{4,0},{1,5},{5,1},{2,6},{6,2},{3,7},{7,3},{8,12},{12,8},{9,1... | collective-permute-start | bytes 3145736 | tf_op jit(solution)/shard_map/ppermute | solution.py:758
  200.1 406.1 %reduce-scatter.5.cloned.1.call-start = ((), (), s32[]{:S(2)}) async-start(), calls=%async_computation.7 | async-start | bytes 7864320 | tf_op jit(solution)/shard_map/reduce_scatter | solution.py:578
  200.5 48.4 %collective-permute-start.4 = (bf16[2,256,2048]{2,1,0:T(8,128)(2,1)}, bf16[2,256,2048]{2,1,0:T(8,128)(2,1)}, u32[]{:S(2)}, u32[]{:S(2)}) collective-permute-start(bf16[2,256,2048]{2,1,0:T(8,128)(2,1)} %pad_maximum_fusion.1), channel_id=1, source_target_pairs={{0,4},{4,0},{1,5},{5,1},{2,6},{6,2},{3,7},{7,3},{8,12},{12,8},{9,1... | collective-permute-start | bytes 6291464 | tf_op jit(solution)/shard_map/ppermute | solution.py:770
  212.4 49.6 %collective-permute-start.18 = (bf16[256,2048]{1,0:T(8,128)(2,1)S(1)}, bf16[256,2048]{1,0:T(8,128)(2,1)S(1)}, u32[]{:S(2)}, u32[]{:S(2)}) collective-permute-start(bf16[256,2048]{1,0:T(8,128)(2,1)S(1)} %get-tuple-element.174), channel_id=1, source_target_pairs={{0,1},{1,0},{2,3},{3,2},{4,5},{5,4},{6,7},{7,6},{8,9},{9,8},{10,11... | collective-permute-start | bytes 3145736 | tf_op jit(solution)/shard_map/ppermute | solution.py:619
  253.0 46.1 %collective-permute-start.13 = (bf16[256,2048]{1,0:T(8,128)(2,1)S(1)}, bf16[256,2048]{1,0:T(8,128)(2,1)S(1)}, u32[]{:S(2)}, u32[]{:S(2)}) collective-permute-start(bf16[256,2048]{1,0:T(8,128)(2,1)S(1)} %get-tuple-element.161), channel_id=1, source_target_pairs={{0,6},{6,0},{2,4},{4,2},{1,7},{7,1},{3,5},{5,3},{8,14},{14,8},{10,... | collective-permute-start | bytes 3145736 | tf_op jit(solution)/shard_map/ppermute | solution.py:614
  262.0 38.2 %collective-permute-start.20 = (bf16[256,2048]{1,0:T(8,128)(2,1)S(1)}, bf16[256,2048]{1,0:T(8,128)(2,1)S(1)}, u32[]{:S(2)}, u32[]{:S(2)}) collective-permute-start(bf16[256,2048]{1,0:T(8,128)(2,1)S(1)} %get-tuple-element.173), channel_id=1, source_target_pairs={{0,1},{1,0},{2,3},{3,2},{4,5},{5,4},{6,7},{7,6},{8,9},{9,8},{10,11... | collective-permute-start | bytes 3145736 | tf_op jit(solution)/shard_map/ppermute | solution.py:619
  263.6 38.2 %collective-permute-start.21 = (bf16[256,2048]{1,0:T(8,128)(2,1)S(1)}, bf16[256,2048]{1,0:T(8,128)(2,1)S(1)}, u32[]{:S(2)}, u32[]{:S(2)}) collective-permute-start(bf16[256,2048]{1,0:T(8,128)(2,1)S(1)} %get-tuple-element.171), channel_id=1, source_target_pairs={{0,1},{1,0},{2,3},{3,2},{4,5},{5,4},{6,7},{7,6},{8,9},{9,8},{10,11... | collective-permute-start | bytes 3145736 | tf_op jit(solution)/shard_map/ppermute | solution.py:619
  363.0 259.1 %reduce-scatter.7.cloned.1.call-start = ((), (), s32[]{:S(2)}) async-start(), calls=%async_computation.8 | async-start | bytes 7864320 | tf_op jit(solution)/shard_map/reduce_scatter | solution.py:578
  427.1 48.0 %collective-permute-start.24 = (bf16[256,2048]{1,0:T(8,128)(2,1)}, bf16[256,2048]{1,0:T(8,128)(2,1)}, u32[]{:S(2)}, u32[]{:S(2)}) collective-permute-start(bf16[256,2048]{1,0:T(8,128)(2,1)} %get-tuple-element.120), channel_id=1, source_target_pairs={{0,2},{2,0},{1,3},{3,1},{4,6},{6,4},{5,7},{7,5},{8,10},{10,8},{9,1... | collective-permute-start | bytes 3145736 | tf_op jit(solution)/shard_map/ppermute | solution.py:631
  428.5 46.5 %collective-permute-start.25 = (bf16[256,2048]{1,0:T(8,128)(2,1)}, bf16[256,2048]{1,0:T(8,128)(2,1)}, u32[]{:S(2)}, u32[]{:S(2)}) collective-permute-start(bf16[256,2048]{1,0:T(8,128)(2,1)} %get-tuple-element.121), channel_id=1, source_target_pairs={{0,6},{6,0},{2,4},{4,2},{1,7},{7,1},{3,5},{5,3},{8,14},{14,8},{10,... | collective-permute-start | bytes 3145736 | tf_op jit(solution)/shard_map/ppermute | solution.py:631
  475.1 153.5 %reduce-scatter.11.cloned.1.call-start = ((), (), s32[]{:S(2)}) async-start(), calls=%async_computation.10 | async-start | bytes 1310720 | tf_op jit(solution)/shard_map/reduce_scatter | solution.py:578
  491.3 49.6 %collective-permute-start.30 = (bf16[2,256,2048]{2,1,0:T(8,128)(2,1)}, bf16[2,256,2048]{2,1,0:T(8,128)(2,1)}, u32[]{:S(2)}, u32[]{:S(2)}) collective-permute-start(bf16[2,256,2048]{2,1,0:T(8,128)(2,1)} %pad_maximum_fusion.3), channel_id=1, source_target_pairs={{0,4},{4,0},{1,5},{5,1},{2,6},{6,2},{3,7},{7,3},{8,12},{12,8},{9,1... | collective-permute-start | bytes 6291464 | tf_op jit(solution)/shard_map/ppermute | solution.py:819
  548.7 43.8 %collective-permute-start.33 = (bf16[2,128,2048]{2,1,0:T(8,128)(2,1)}, bf16[2,128,2048]{2,1,0:T(8,128)(2,1)}, u32[]{:S(2)}, u32[]{:S(2)}) collective-permute-start(bf16[2,128,2048]{2,1,0:T(8,128)(2,1)} %fusion.26), channel_id=1, source_target_pairs={{0,2},{2,0},{1,3},{3,1},{4,6},{6,4},{5,7},{7,5},{8,10},{10,8},{9,1... | collective-permute-start | bytes 3145736 | tf_op jit(solution)/shard_map/ppermute | solution.py:606
  568.2 49.9 %collective-permute-start.35 = (bf16[1024,1024]{1,0:T(8,128)(2,1)}, bf16[1024,1024]{1,0:T(8,128)(2,1)}, u32[]{:S(2)}, u32[]{:S(2)}) collective-permute-start(bf16[1024,1024]{1,0:T(8,128)(2,1)} %get-tuple-element.144), channel_id=1, source_target_pairs={{0,4},{4,0},{1,5},{5,1},{2,6},{6,2},{3,7},{7,3},{8,12},{12,8},{9,1... | collective-permute-start | bytes 6291464 | tf_op jit(solution)/shard_map/ppermute | solution.py:846
  601.4 93.9 %all-to-all-start.2 = ((bf16[32,8,4224]{2,1,0:T(8,128)(2,1)}), bf16[32,8,4224]{2,1,0:T(8,128)(2,1)}, u32[]{:S(2)}, u32[]{:S(2)}) async-start(bf16[32,8,4224]{2,1,0:T(8,128)(2,1)} %pad_maximum_fusion), calls=%async_computation.2 | async-start | bytes 4325376 | tf_op jit(solution)/shard_map/all_to_all | solution.py:683
  606.1 94.6 %reduce-scatter.9.cloned.1.call-start = ((), (), s32[]{:S(2)}) async-start(), calls=%async_computation.9 | async-start | bytes 2621440 | tf_op jit(solution)/shard_map/reduce_scatter | solution.py:578
  (63 other events, 771.3 us)
Sparse Core Ops, SparseCore 0:
  15.9 68.8 all-gather.8
  87.8 46.2 all-gather.10
  135.6 114.4 all-gather.14
  251.5 113.5 all-gather.12
  367.2 108.9 reduce-scatter.4
  478.4 111.2 reduce-scatter.6
  592.6 35.9 reduce-scatter.10
  631.0 65.7 reduce-scatter.8

commit v4 on v3

--- a/solution.py
+++ b/solution.py
@@ -664,6 +664,11 @@
     everywhere = ("z", "x", "y", "c")
     place = jnp.stack([2 * lax.axis_index("y") + lax.axis_index("c"), here_x]).astype(jnp.int32)
 
+    fused_shard = jnp.concatenate(
+        [query_weight, key_projection_weight, value_projection_weight], axis=1
+    )
+    fused_shard, token_slots = tie(fused_shard, token_slots)
+
     rank = jnp.sum(
         (token_slots[:, None, :] < token_slots[:, :, None]).astype(jnp.int32), axis=2
     )
@@ -695,11 +700,8 @@
     leaving = jnp.concatenate(
         [mm(to_send, leaving).astype(BF16), jnp.tile(gains, (devices, 1))], axis=1
     )
-    fused_shard = jnp.concatenate(
-        [query_weight, key_projection_weight, value_projection_weight], axis=1
-    )
-    leaving, fused_shard, gate_weight, down_weight, cotangent = tie(
-        by_device(leaving), fused_shard, gate_weight, down_weight, cotangent
+    leaving, gate_weight, down_weight, cotangent = tie(
+        by_device(leaving), gate_weight, down_weight, cotangent
     )
     arrived = exchange(leaving)
     cot_leaving = mm(to_send, cotangent.reshape(flat_rows, width)).astype(BF16)
@@ -766,21 +768,25 @@
     )
     cot_rows = outer_sum(to_place, arrived_cot).astype(BF16)
     cot_beside = lax.ppermute(cot_rows, "y", SWAP)
-    cot_pair, output_full = tie(jnp.stack([cot_rows, cot_beside]), output_full)
-    cot_over_x = lax.ppermute(cot_pair, "x", SWAP)
+    cot_rows, cot_beside, output_full = tie(cot_rows, cot_beside, output_full)
+    cot_over_x = lax.ppermute(cot_rows, "x", SWAP)
+    cot_across = lax.ppermute(cot_beside, "x", SWAP)
     shared = (fused_own, fused_other, output_full, tables, segments)
     normed_all, fused, heads, kept, sent = attention_forward(place, pieces, *shared)
+    kept, sent, cot_over_x = tie(kept, sent, cot_over_x)
     for shard in ff_shards[1:]:
         shard, sent = tie(shard, sent)
         ff_weights.append(gather_z(shard))
     attended = reduce_tensor(kept, sent).reshape(flat_rows, width)
-    cot_over_x, attended = tie(cot_over_x, attended)
-    cot_all = join_planes((cot_pair[0], cot_over_x[0], cot_pair[1], cot_over_x[1]))
+    cot_across, attended = tie(cot_across, attended)
+    cot_all = join_planes((cot_rows, cot_over_x, cot_beside, cot_across))
     residual = inputs + attended
 
     second_scale = rms_scale(residual)
     normed_two = (residual * second_scale * gain_two).astype(BF16)
-    normed_two_all = join_planes(gather_planes(normed_two))
+    planes = list(gather_planes(normed_two))
+    planes[1], cot_all = tie(planes[1], cot_all)
+    normed_two_all = join_planes(tuple(planes))
 
     previous = ()
     gate_kept, gate_moved, down_grads = [], [], []

time: 716 us -> 709 us (level)
  waiting for transfers between devices: 338 us -> 351 us
  local copies, waits for them, and re-layouts: 43.8 us -> 30.8 us
    all_gather x4, waiting for transfers between devices: 7.27 us -> 37.4 us  [gather_z(): return rows_major(lax.all_gather(rows_major(piece), 'z', axis=0))]
    all_to_all x3, waiting for transfers between devices: 81.5 us -> 53.1 us  [exchange(): lax.all_to_all(blocks, everywhere, split_axis=0, concat_axis=0, tiled=True)]
    ppermute x1, waiting for transfers between devices: 0.01 us -> 21.6 us  [gather_planes(): lax.ppermute(rows, 'y', SWAP)]
    ppermute x1, waiting for transfers between devices: 19.4 us -> 0.38 us  [gather_planes(): lax.ppermute(rows, ('x', 'y'), DIAGONAL)]
    reduce_scatter x4, waiting for transfers between devices: 0.89 us -> 16.1 us  [reduce_z(): return lax.psum_scatter(parts, 'z', scatter_dimension=0)]
    ppermute x2, waiting for transfers between devices: 26.1 us -> 13.1 us  [body(): gate_moved = [lax.ppermute(part, 'x', SWAP) for part in gate_moved]]
    ppermute x1, waiting for transfers between devices: 10.4 us -> 21.5 us  [body(): output_other = lax.ppermute(output_own, 'x', SWAP)]
    ppermute x1 -> x2, waiting for transfers between devices: 12.3 us -> 1.73 us  [the longest x1 1.72 us: body(): cot_over_x = lax.ppermute(cot_rows, 'x', SWAP)]
  transfers between devices with their start and end apart: 49 -> 50, of which waited for: 27 -> 29; matrix products, arithmetic and copies ran while one was open for 15% -> 13% of each run, Pallas kernels for 24% -> 24%
where the time goes in v4:
time: 709 us; the launch traced here: 704 us
  waiting for transfers between devices  351 us (50%)
  Pallas kernels  172 us (24%)
  other arithmetic  71.8 us (10%)
  starting transfers between devices  55.9 us (8%)
  local copies, waits for them, and re-layouts  30.8 us (4%)
  between operations  15.4 us (2%)
  matrix products  7.13 us (1%)
    pallas_call x2, Pallas kernels, feedforward(): pl.pallas_call(functools.partial(feedforward_kernel, bool(previous), last...  73.4 us
    all_to_all x3, waiting for transfers between devices, exchange(): lax.all_to_all(blocks, everywhere, split_axis=0, concat_axis=0, tiled=True)  53.1 us
    pallas_call x2, Pallas kernels, feedforward_grads(): pl.pallas_call(feedforward_grads_kernel, grid=(pieces,), in_specs=[pl.Blo...  42.2 us
    ppermute x2, waiting for transfers between devices, reduce_tensor(): lax.ppermute(moved, 'y', SWAP).astype(F32)  38.9 us
    all_gather x4, waiting for transfers between devices, gather_z(): return rows_major(lax.all_gather(rows_major(piece), 'z', axis=0))  37.4 us
    pallas_call x1, Pallas kernels, attention_backward(): pl.pallas_call(functools.partial(attention_backward_kernel, query_cols //...  30.8 us
    ppermute x2, waiting for transfers between devices, body(): lax.ppermute(leaving, 'x', SWAP)  28 us
    ppermute x3, waiting for transfers between devices, send_eight(): lax.ppermute(part, axes, pairs)  25.1 us
  transfers between devices with their start and end apart: 50, of which 29 were waited for; matrix products, arithmetic and copies ran while one was open for 13% of the time, Pallas kernels for 24%

profile of v4, /device:TPU:0, one launch (start us, length us, event | category | flops | bytes accessed | tf_op | source)
XLA Modules:
  0.0 703.9 jit_solution(2831246885994688521)
XLA Ops:
  31.6 15.9 %collective-permute-done.1 = bf16[256,1024]{1,0:T(8,128)(2,1)} collective-permute-done((bf16[256,1024]{1,0:T(8,128)(2,1)}, bf16[256,1024]{1,0:T(8,128)(2,1)}, u32[]{:S(2)}, u32[]{:S(2)}) %collective-permute-start.1) | collective-permute-done | bytes 524320 | tf_op jit(solution)/shard_map/ppermute | solution.py:732
  48.6 12.1 %collective-permute-done = bf16[256,1024]{1,0:T(8,128)(2,1)} collective-permute-done((bf16[256,1024]{1,0:T(8,128)(2,1)}, bf16[256,1024]{1,0:T(8,128)(2,1)}, u32[]{:S(2)}, u32[]{:S(2)}) %collective-permute-start) | collective-permute-done | bytes 524320 | tf_op jit(solution)/shard_map/ppermute | solution.py:732
  63.8 15.1 %all-to-all-done = bf16[32,8,2176]{2,1,0:T(8,128)(2,1)S(1)} async-done(((bf16[32,8,2176]{2,1,0:T(8,128)(2,1)}), bf16[32,8,2176]{2,1,0:T(8,128)(2,1)S(1)}, u32[]{:S(2)}, u32[]{:S(2)}) %all-to-all-start) | async-done | bytes 1114144 | tf_op jit(solution)/shard_map/all_to_all | solution.py:688
  96.0 34.2 %all-gather.11.cloned.1.call-done = bf16[256,2048]{1,0:T(8,128)(2,1)} async-done(((bf16[64,2048]{1,0:T(8,128)(2,1)}), bf16[256,2048]{1,0:T(8,128)(2,1)}) %all-gather.11.cloned.1.call-update) | async-done | bytes 1048592 | tf_op jit(solution)/shard_map/all_gather | solution.py:574
  138.7 13.2 %collective-permute-done.6.other_ref = bf16[1024,1024]{1,0:T(8,128)(2,1)} collective-permute-done((bf16[1024,1024]{1,0:T(8,128)(2,1)}, bf16[1024,1024]{1,0:T(8,128)(2,1)}, u32[]{:S(2)}, u32[]{:S(2)}) %collective-permute-start.6) | collective-permute-done | bytes 2097184 | tf_op jit(solution)/shard_map/ppermute | solution.py:741
  152.5 21.5 %collective-permute-done.3 = bf16[4,64,2048]{2,1,0:T(8,128)(2,1)} collective-permute-done((bf16[4,64,2048]{2,1,0:T(8,128)(2,1)}, bf16[4,64,2048]{2,1,0:T(8,128)(2,1)}, u32[]{:S(2)}, u32[]{:S(2)}) %collective-permute-start.3) | collective-permute-done | bytes 1048608 | tf_op jit(solution)/shard_map/ppermute | solution.py:760
  183.3 17.1 %shard_map.213 = (bf16[1024,2048]{1,0:T(8,128)(2,1)}, bf16[1024,1024]{1,0:T(8,128)(2,1)}, bf16[1024,512]{1,0:T(8,128)(2,1)}, bf16[2,2,128,2048]{3,2,1,0:T(8,128)(2,1)}, bf16[2,2,128,2048]{3,2,1,0:T(8,128)(2,1)}) custom-call(s32[2]{0:T(128)} %pad_add_fusion.1.place_ref, bf16[2,128,2048]{2,1,0:T(8,128)(2,1)} %bitcast.20.piece0, ...), custom_call_target="tpu_custom_call" | custom-call | tf_op jit(solution)/shard_map/pallas_call | solution.py:294
  215.3 20.9 %collective-permute-done.11 = bf16[2,128,2048]{2,1,0:T(8,128)(2,1)} collective-permute-done((bf16[2,128,2048]{2,1,0:T(8,128)(2,1)}, bf16[2,128,2048]{2,1,0:T(8,128)(2,1)}, u32[]{:S(2)}, u32[]{:S(2)}) %collective-permute-start.11) | collective-permute-done | bytes 1048608 | tf_op jit(solution)/shard_map/ppermute | solution.py:606
  244.7 21.7 %collective-permute-done.12 = bf16[256,2048]{1,0:T(8,128)(2,1)S(1)} collective-permute-done((bf16[256,2048]{1,0:T(8,128)(2,1)S(1)}, bf16[256,2048]{1,0:T(8,128)(2,1)S(1)}, u32[]{:S(2)}, u32[]{:S(2)}) %collective-permute-start.12) | collective-permute-done | bytes 1048608 | tf_op jit(solution)/shard_map/ppermute | solution.py:612
  266.4 21.6 %collective-permute-done.17 = bf16[256,2048]{1,0:T(8,128)(2,1)S(1)} collective-permute-done((bf16[256,2048]{1,0:T(8,128)(2,1)S(1)}, bf16[256,2048]{1,0:T(8,128)(2,1)S(1)}, u32[]{:S(2)}, u32[]{:S(2)}) %collective-permute-start.17) | collective-permute-done | bytes 1048608 | tf_op jit(solution)/shard_map/ppermute | solution.py:613
  295.9 34.8 %shard_map.214 = (bf16[2048,512]{1,0:T(8,128)(2,1)}, bf16[2048,1024]{1,0:T(8,128)(2,1)}, f32[2048,2048]{1,0:T(8,128)}, f32[2048,2048]{1,0:T(8,128)}) custom-call(bf16[2048,2048]{1,0:T(8,128)(2,1)} %constant_dynamic-update-slice_fusion.8.normed_ref, bf16[2048,2048]{1,0:T(8,128)(2,1)} %copy-done.2, bf16[4,768,1024]{2,1,0:T(8,128)(2,1)} %bitcast.185), custom_call_target="tpu_custom_call" | custom-call | tf_op jit(solution)/shard_map/pallas_call | solution.py:435
  330.7 21.1 %shard_map.218 = bf16[4,768,1024]{2,1,0:T(8,128)(2,1)} custom-call(bf16[2048,2048]{1,0:T(8,128)(2,1)} %constant_dynamic-update-slice_fusion.8.normed_ref, bf16[2048,1024]{1,0:T(8,128)(2,1)} %get-tuple-element.152.d_both_ref, bf16[2048,512]{1,0:T(8,128)(2,1)} %get-tuple-element.153.hidden_ref, bf16[2048,2048]{1,0:T(8,128)(2,1)} %copy-done.2), custom_call_target="tpu_custom_call" | custom-call | tf_op jit(solution)/shard_map/pallas_call | solution.py:472
  351.8 10.1 %reduce-scatter.7.cloned.1.call-start = ((), (), s32[]{:S(2)}) async-start(), calls=%async_computation.8 | async-start | bytes 7864320 | tf_op jit(solution)/shard_map/reduce_scatter | solution.py:578
  361.9 38.5 %shard_map.215 = (bf16[2048,512]{1,0:T(8,128)(2,1)}, bf16[2048,1024]{1,0:T(8,128)(2,1)}, bf16[1024,2048]{1,0:T(8,128)(2,1)}, bf16[1024,2048]{1,0:T(8,128)(2,1)},...) custom-call(bf16[2048,2048]{1,0:T(8,128)(2,1)} %constant_dynamic-update-slice_fusion.8.normed_ref, ...), custom_call_target="tpu_custom_call" | custom-call | tf_op jit(solution)/shard_map/pallas_call | solution.py:435
  417.9 21.2 %shard_map.216 = bf16[4,768,1024]{2,1,0:T(8,128)(2,1)} custom-call(bf16[2048,2048]{1,0:T(8,128)(2,1)} %constant_dynamic-update-slice_fusion.8.normed_ref, bf16[2048,1024]{1,0:T(8,128)(2,1)} %get-tuple-element.131.d_both_ref, bf16[2048,512]{1,0:T(8,128)(2,1)} %get-tuple-element.132.hidden_ref, bf16[2048,2048]{1,0:T(8,128)(2,1)} %copy-done.2), custom_call_target="tpu_custom_call" | custom-call | tf_op jit(solution)/shard_map/pallas_call | solution.py:472
  440.7 23.4 %collective-permute-done.25 = bf16[256,2048]{1,0:T(8,128)(2,1)} collective-permute-done((bf16[256,2048]{1,0:T(8,128)(2,1)}, bf16[256,2048]{1,0:T(8,128)(2,1)}, u32[]{:S(2)}, u32[]{:S(2)}) %collective-permute-start.25) | collective-permute-done | bytes 1048608 | tf_op jit(solution)/shard_map/ppermute | solution.py:631
  481.4 14.0 %collective-permute-done.29.piece2 = bf16[2,128,2048]{2,1,0:T(8,128)(2,1)S(1)} collective-permute-done((bf16[2,128,2048]{2,1,0:T(8,128)(2,1)S(1)}, bf16[2,128,2048]{2,1,0:T(8,128)(2,1)S(1)}, u32[]{:S(2)}, u32[]{:S(2)}) %collective-permute-start.29) | collective-permute-done | bytes 1048608 | tf_op jit(solution)/shard_map/ppermute | solution.py:594
  499.0 30.8 %shard_map.217 = (bf16[2,2,128,2048]{3,2,1,0:T(8,128)(2,1)}, bf16[2,2,128,2048]{3,2,1,0:T(8,128)(2,1)}, bf16[1024,1024]{1,0:T(8,128)(2,1)}, bf16[1024,1024]{1,0:...) custom-call(s32[2]{0:T(128)} %pad_add_fusion.1.place_ref, bf16[2,128,2048]{2,1,0:T(8,128)(2,1)} %bitcast.192, ...), custom_call_target="tpu_custom_call" | custom-call | tf_op jit(solution)/shard_map/pallas_call | solution.py:327
  539.5 16.2 %collective-permute-done.35 = bf16[256,2048]{1,0:T(8,128)(2,1)S(1)} collective-permute-done((bf16[256,2048]{1,0:T(8,128)(2,1)}, bf16[256,2048]{1,0:T(8,128)(2,1)S(1)}, u32[]{:S(2)}, u32[]{:S(2)}) %collective-permute-start.35) | collective-permute-done | bytes 1048608 | tf_op jit(solution)/shard_map/ppermute | solution.py:852
  564.6 17.9 %collective-permute-done.34 = bf16[2,128,2048]{2,1,0:T(8,128)(2,1)} collective-permute-done((bf16[2,128,2048]{2,1,0:T(8,128)(2,1)}, bf16[2,128,2048]{2,1,0:T(8,128)(2,1)}, u32[]{:S(2)}, u32[]{:S(2)}) %collective-permute-start.34) | collective-permute-done | bytes 1048608 | tf_op jit(solution)/shard_map/ppermute | solution.py:606
  598.9 7.8 %collective-permute-done.36 = bf16[1024,1024]{1,0:T(8,128)(2,1)} collective-permute-done((bf16[1024,1024]{1,0:T(8,128)(2,1)}, bf16[1024,1024]{1,0:T(8,128)(2,1)}, u32[]{:S(2)}, u32[]{:S(2)}) %collective-permute-start.36) | collective-permute-done | bytes 2097184 | tf_op jit(solution)/shard_map/ppermute | solution.py:852
  616.6 14.1 %reduce-scatter.11.cloned.1.call-done = bf16[1,64,2048]{2,1,0:T(8,128)(2,1)} async-done(((bf16[4,64,2048]{2,1,0:T(8,128)(2,1)}), bf16[1,64,2048]{2,1,0:T(8,128)(2,1)}) %reduce-scatter.11.cloned.1.call-update) | async-done | bytes 262160 | tf_op jit(solution)/shard_map/reduce_scatter | solution.py:578
  636.7 11.4 %collective-permute-done.38.refs_3_ = bf16[256,1024]{1,0:T(8,128)(2,1)} collective-permute-done((bf16[256,1024]{1,0:T(8,128)(2,1)}, bf16[256,1024]{1,0:T(8,128)(2,1)}, u32[]{:S(2)}, u32[]{:S(2)}) %collective-permute-start.38) | collective-permute-done | bytes 524320 | tf_op jit(solution)/shard_map/ppermute | solution.py:859
  652.4 36.4 %all-to-all-done.2 = bf16[32,8,4224]{2,1,0:T(8,128)(2,1)S(1)} async-done(((bf16[32,8,4224]{2,1,0:T(8,128)(2,1)}), bf16[32,8,4224]{2,1,0:T(8,128)(2,1)S(1)}, u32[]{:S(2)}, u32[]{:S(2)}) %all-to-all-start.2) | async-done | bytes 2162720 | tf_op jit(solution)/shard_map/all_to_all | solution.py:688
  (282 shorter events, 197.4 us)
Async XLA Ops:
  7.2 75.3 %all-gather.9.cloned.1.call-start = ((), (), s32[]{:S(2)}) async-start(), calls=%async_computation.11 | async-start | bytes 2621440 | tf_op jit(solution)/shard_map/all_gather | solution.py:574
  16.3 62.6 %all-to-all-start = ((bf16[32,8,2176]{2,1,0:T(8,128)(2,1)}), bf16[32,8,2176]{2,1,0:T(8,128)(2,1)S(1)}, u32[]{:S(2)}, u32[]{:S(2)}) async-start(bf16[32,8,2176]{2,1,0:T(8,128)(2,1)} %pad_maximum_fusion.5), calls=%async_computation | async-start | bytes 2228224 | tf_op jit(solution)/shard_map/all_to_all | solution.py:688
  23.6 106.6 %all-gather.11.cloned.1.call-start = ((), (), s32[]{:S(2)}) async-start(), calls=%async_computation.12 | async-start | bytes 1310720 | tf_op jit(solution)/shard_map/all_gather | solution.py:574
  84.1 211.7 %all-gather.15.cloned.1.call-start = ((), (), s32[]{:S(2)}) async-start(), calls=%async_computation.14 | async-start | bytes 7864320 | tf_op jit(solution)/shard_map/all_gather | solution.py:574
  89.0 44.7 %all-to-all-start.1 = ((bf16[32,8,2048]{2,1,0:T(8,128)(2,1)}), bf16[32,8,2048]{2,1,0:T(8,128)(2,1)}, u32[]{:S(2)}, u32[]{:S(2)}) async-start(bf16[32,8,2048]{2,1,0:T(8,128)(2,1)} %bitcast.194), calls=%async_computation.1 | async-start | bytes 2097152 | tf_op jit(solution)/shard_map/all_to_all | solution.py:688
  92.5 269.4 %all-gather.13.cloned.1.call-start = ((), (), s32[]{:S(2)}) async-start(), calls=%async_computation.13 | async-start | bytes 7864320 | tf_op jit(solution)/shard_map/all_gather | solution.py:574
  92.8 59.2 %collective-permute-start.6 = (bf16[1024,1024]{1,0:T(8,128)(2,1)}, bf16[1024,1024]{1,0:T(8,128)(2,1)}, u32[]{:S(2)}, u32[]{:S(2)}) collective-permute-start(bf16[1024,1024]{1,0:T(8,128)(2,1)} %all-gather.9.cloned.1.call-done.own_ref), channel_id=1, source_target_pairs={{0,4},{4,0},{1,5},{5,1},{2,6},{6,2},{3,7},{7,3},{8,12},{12,8},{9,1... | collective-permute-start | bytes 6291464 | tf_op jit(solution)/shard_map/ppermute | solution.py:741
  94.5 44.2 %collective-permute-start.5 = (bf16[2,128,2048]{2,1,0:T(8,128)(2,1)}, bf16[2,128,2048]{2,1,0:T(8,128)(2,1)}, u32[]{:S(2)}, u32[]{:S(2)}) collective-permute-start(bf16[2,128,2048]{2,1,0:T(8,128)(2,1)} %bitcast.20.piece0), channel_id=1, source_target_pairs={{0,2},{2,0},{1,3},{3,1},{4,6},{6,4},{5,7},{7,5},{8,10},{10,8},{9,1... | collective-permute-start | bytes 3145736 | tf_op jit(solution)/shard_map/ppermute | solution.py:759
  130.2 43.8 %collective-permute-start.3 = (bf16[4,64,2048]{2,1,0:T(8,128)(2,1)}, bf16[4,64,2048]{2,1,0:T(8,128)(2,1)}, u32[]{:S(2)}, u32[]{:S(2)}) collective-permute-start(bf16[4,64,2048]{2,1,0:T(8,128)(2,1)} %bitcast.195), channel_id=1, source_target_pairs={{0,4},{4,0},{1,5},{5,1},{2,6},{6,2},{3,7},{7,3},{8,12},{12,8},{9,1... | collective-permute-start | bytes 3145736 | tf_op jit(solution)/shard_map/ppermute | solution.py:760
  135.5 41.9 %collective-permute-start.2 = (bf16[256,2048]{1,0:T(8,128)(2,1)S(1)}, bf16[256,2048]{1,0:T(8,128)(2,1)}, u32[]{:S(2)}, u32[]{:S(2)}) collective-permute-start(bf16[256,2048]{1,0:T(8,128)(2,1)S(1)} %convolution_convert_fusion.3), channel_id=1, source_target_pairs={{0,2},{2,0},{1,3},{3,1},{4,6},{6,4},{5,7},{7,5},{8,10},{10,8},{9,1... | collective-permute-start | bytes 3145736 | tf_op jit(solution)/shard_map/ppermute | solution.py:770
  203.0 393.4 %reduce-scatter.5.cloned.1.call-start = ((), (), s32[]{:S(2)}) async-start(), calls=%async_computation.7 | async-start | bytes 7864320 | tf_op jit(solution)/shard_map/reduce_scatter | solution.py:578
  241.1 46.8 %collective-permute-start.17 = (bf16[256,2048]{1,0:T(8,128)(2,1)S(1)}, bf16[256,2048]{1,0:T(8,128)(2,1)S(1)}, u32[]{:S(2)}, u32[]{:S(2)}) collective-permute-start(bf16[256,2048]{1,0:T(8,128)(2,1)S(1)} %get-tuple-element.175), channel_id=1, source_target_pairs={{0,2},{2,0},{1,3},{3,1},{4,6},{6,4},{5,7},{7,5},{8,10},{10,8},{9,1... | collective-permute-start | bytes 3145736 | tf_op jit(solution)/shard_map/ppermute | solution.py:613
  242.8 46.6 %collective-permute-start.18 = (bf16[256,2048]{1,0:T(8,128)(2,1)S(1)}, bf16[256,2048]{1,0:T(8,128)(2,1)S(1)}, u32[]{:S(2)}, u32[]{:S(2)}) collective-permute-start(bf16[256,2048]{1,0:T(8,128)(2,1)S(1)} %get-tuple-element.175), channel_id=1, source_target_pairs={{0,6},{6,0},{2,4},{4,2},{1,7},{7,1},{3,5},{5,3},{8,14},{14,8},{10,... | collective-permute-start | bytes 3145736 | tf_op jit(solution)/shard_map/ppermute | solution.py:614
  244.4 47.2 %collective-permute-start.19 = (bf16[256,2048]{1,0:T(8,128)(2,1)S(1)}, bf16[256,2048]{1,0:T(8,128)(2,1)S(1)}, u32[]{:S(2)}, u32[]{:S(2)}) collective-permute-start(bf16[256,2048]{1,0:T(8,128)(2,1)S(1)} %get-tuple-element.175), channel_id=1, source_target_pairs={{0,1},{1,0},{2,3},{3,2},{4,5},{5,4},{6,7},{7,6},{8,9},{9,8},{10,11... | collective-permute-start | bytes 3145736 | tf_op jit(solution)/shard_map/ppermute | solution.py:619
  351.8 258.8 %reduce-scatter.7.cloned.1.call-start = ((), (), s32[]{:S(2)}) async-start(), calls=%async_computation.8 | async-start | bytes 7864320 | tf_op jit(solution)/shard_map/reduce_scatter | solution.py:578
  416.4 47.7 %collective-permute-start.25 = (bf16[256,2048]{1,0:T(8,128)(2,1)}, bf16[256,2048]{1,0:T(8,128)(2,1)}, u32[]{:S(2)}, u32[]{:S(2)}) collective-permute-start(bf16[256,2048]{1,0:T(8,128)(2,1)} %get-tuple-element.134), channel_id=1, source_target_pairs={{0,2},{2,0},{1,3},{3,1},{4,6},{6,4},{5,7},{7,5},{8,10},{10,8},{9,1... | collective-permute-start | bytes 3145736 | tf_op jit(solution)/shard_map/ppermute | solution.py:631
  417.8 46.3 %collective-permute-start.26 = (bf16[256,2048]{1,0:T(8,128)(2,1)}, bf16[256,2048]{1,0:T(8,128)(2,1)}, u32[]{:S(2)}, u32[]{:S(2)}) collective-permute-start(bf16[256,2048]{1,0:T(8,128)(2,1)} %get-tuple-element.135), channel_id=1, source_target_pairs={{0,6},{6,0},{2,4},{4,2},{1,7},{7,1},{3,5},{5,3},{8,14},{14,8},{10,... | collective-permute-start | bytes 3145736 | tf_op jit(solution)/shard_map/ppermute | solution.py:631
  464.1 166.5 %reduce-scatter.11.cloned.1.call-start = ((), (), s32[]{:S(2)}) async-start(), calls=%async_computation.10 | async-start | bytes 1310720 | tf_op jit(solution)/shard_map/reduce_scatter | solution.py:578
  480.3 49.6 %collective-permute-start.31 = (bf16[2,256,2048]{2,1,0:T(8,128)(2,1)}, bf16[2,256,2048]{2,1,0:T(8,128)(2,1)}, u32[]{:S(2)}, u32[]{:S(2)}) collective-permute-start(bf16[2,256,2048]{2,1,0:T(8,128)(2,1)} %pad_maximum_fusion.2), channel_id=1, source_target_pairs={{0,4},{4,0},{1,5},{5,1},{2,6},{6,2},{3,7},{7,3},{8,12},{12,8},{9,1... | collective-permute-start | bytes 6291464 | tf_op jit(solution)/shard_map/ppermute | solution.py:825
  538.5 44.0 %collective-permute-start.34 = (bf16[2,128,2048]{2,1,0:T(8,128)(2,1)}, bf16[2,128,2048]{2,1,0:T(8,128)(2,1)}, u32[]{:S(2)}, u32[]{:S(2)}) collective-permute-start(bf16[2,128,2048]{2,1,0:T(8,128)(2,1)} %fusion.26), channel_id=1, source_target_pairs={{0,2},{2,0},{1,3},{3,1},{4,6},{6,4},{5,7},{7,5},{8,10},{10,8},{9,1... | collective-permute-start | bytes 3145736 | tf_op jit(solution)/shard_map/ppermute | solution.py:606
  557.1 49.6 %collective-permute-start.36 = (bf16[1024,1024]{1,0:T(8,128)(2,1)}, bf16[1024,1024]{1,0:T(8,128)(2,1)}, u32[]{:S(2)}, u32[]{:S(2)}) collective-permute-start(bf16[1024,1024]{1,0:T(8,128)(2,1)} %get-tuple-element.158), channel_id=1, source_target_pairs={{0,4},{4,0},{1,5},{5,1},{2,6},{6,2},{3,7},{7,3},{8,12},{12,8},{9,1... | collective-permute-start | bytes 6291464 | tf_op jit(solution)/shard_map/ppermute | solution.py:852
  591.4 97.3 %all-to-all-start.2 = ((bf16[32,8,4224]{2,1,0:T(8,128)(2,1)}), bf16[32,8,4224]{2,1,0:T(8,128)(2,1)S(1)}, u32[]{:S(2)}, u32[]{:S(2)}) async-start(bf16[32,8,4224]{2,1,0:T(8,128)(2,1)} %pad_maximum_fusion), calls=%async_computation.2 | async-start | bytes 4325376 | tf_op jit(solution)/shard_map/all_to_all | solution.py:688
  596.4 97.4 %reduce-scatter.9.cloned.1.call-start = ((), (), s32[]{:S(2)}) async-start(), calls=%async_computation.9 | async-start | bytes 2621440 | tf_op jit(solution)/shard_map/reduce_scatter | solution.py:578
  616.5 31.7 %collective-permute-start.38 = (bf16[256,1024]{1,0:T(8,128)(2,1)}, bf16[256,1024]{1,0:T(8,128)(2,1)}, u32[]{:S(2)}, u32[]{:S(2)}) collective-permute-start(bf16[256,1024]{1,0:T(8,128)(2,1)} %get-tuple-element.161), channel_id=1, source_target_pairs={{0,4},{4,0},{1,5},{5,1},{2,6},{6,2},{3,7},{7,3},{8,12},{12,8},{9,1... | collective-permute-start | bytes 1572872 | tf_op jit(solution)/shard_map/ppermute | solution.py:859
  (58 other events, 858.9 us)
Sparse Core Ops, SparseCore 0:
  10.2 72.2 all-gather.8
  84.2 45.8 all-gather.10
  131.7 114.4 all-gather.14
  247.6 113.5 all-gather.12
  363.4 108.9 reduce-scatter.4
  474.5 111.2 reduce-scatter.6
  588.7 41.8 reduce-scatter.10
  633.0 60.6 reduce-scatter.8

commit v5 on v4

--- a/solution.py
+++ b/solution.py
@@ -359,9 +359,9 @@
     )(place, *pieces, own, other, output_full, *tables, *segments, normed, fused, heads)
 
 
-def feedforward_kernel(previous, last, normed_ref, cot_ref, weights_ref, *refs):
+def feedforward_kernel(count, last, normed_ref, cot_ref, weights_ref, *refs):
     refs = list(refs)
-    before = [refs.pop(0) for _ in range(2)] if previous else []
+    earlier = [[refs.pop(0) for _ in range(3)] for _ in range(count)]
     down_ref = refs.pop()
     hidden_ref, d_both_ref, *sums = refs
     pieces, _, fused = weights_ref.shape
@@ -391,21 +391,29 @@
     ).astype(BF16)
     d_both_ref[:, columns:] = (d_hidden * silu).astype(BF16)
 
+    if not last:
+        return
+
     def write(out_ref, d_normed_ref):
-        out = mm(hidden_ref[...], down_ref[...])
-        if previous:
-            out = out + before[0][...]
-        out_ref[...] = out.astype(out_ref.dtype)
+        for part in range(width // fused):
+            at = slice(part * fused, (part + 1) * fused)
+            start = rows + part * piece
+            out = mm(hidden_ref[...], down_ref[:, at])
+            for hidden_before, _, weights_before in earlier:
+                for step in range(pieces):
+                    out = out + mm(
+                        hidden_before[:, step * piece : (step + 1) * piece],
+                        weights_before[step, start : start + piece, :],
+                    )
+            out_ref[:, at] = out.astype(BF16)
         for step in range(pieces):
             at = slice(step * rows, (step + 1) * rows)
             d_normed = times_transposed(d_both_ref[...], weights_ref[step, :rows, :])
-            if previous:
-                d_normed = d_normed + before[1][:, at]
-            d_normed_ref[:, at] = d_normed.astype(d_normed_ref.dtype)
-
-    if not last:
-        write(*sums)
-        return
+            for _, d_both_before, weights_before in earlier:
+                d_normed = d_normed + times_transposed(
+                    d_both_before[...], weights_before[step, :rows, :]
+                )
+            d_normed_ref[:, at] = d_normed.astype(BF16)
 
     @pl.when(index < 4)
     def _():
@@ -416,27 +424,29 @@
         write(*sums[0::2])
 
 
-def feedforward(normed, cot, weights, columns, previous, last):
+def feedforward(normed, cot, weights, columns, earlier, last):
     rows, width = normed.shape
     size = rows // 8
 
     def blocks(count):
         return pl.BlockSpec((size, count), lambda i: ((i + 4) % 8, 0))
 
+    sums, shapes = [], []
     if last:
         sums = [
             pl.BlockSpec((size, width), lambda i: (jnp.maximum(i - 4, 0), 0)),
             pl.BlockSpec((size, width), lambda i: (jnp.minimum(i, 3), 0)),
         ] * 2
         shapes = [jax.ShapeDtypeStruct((rows // 2, width), BF16)] * 4
-    else:
-        sums = [blocks(width)] * 2
-        shapes = [jax.ShapeDtypeStruct((rows, width), F32)] * 2
+    earlier_specs = [
+        spec
+        for _, _, before in earlier
+        for spec in (blocks(columns), blocks(2 * columns), whole_spec(before.shape))
+    ]
     return pl.pallas_call(
-        functools.partial(feedforward_kernel, bool(previous), last),
+        functools.partial(feedforward_kernel, len(earlier), last),
         grid=(8,),
-        in_specs=[blocks(width), blocks(width), whole_spec(weights.shape)]
-        + [blocks(width)] * len(previous),
+        in_specs=[blocks(width), blocks(width), whole_spec(weights.shape)] + earlier_specs,
         out_specs=[blocks(columns), blocks(2 * columns)] + sums,
         out_shape=[
             jax.ShapeDtypeStruct((rows, columns), BF16),
@@ -445,7 +455,7 @@
         + shapes,
         scratch_shapes=[pltpu.VMEM((columns, width), BF16)],
         compiler_params=pltpu.CompilerParams(vmem_limit_bytes=56 << 20),
-    )(normed, cot, weights, *previous)
+    )(normed, cot, weights, *[array for before in earlier for array in before])
 
 
 def feedforward_grads_kernel(normed_ref, d_both_ref, hidden_ref, cot_ref, out_ref, down_ref):
@@ -572,6 +582,23 @@
 
 def gather_z(piece):
     return rows_major(lax.all_gather(rows_major(piece), "z", axis=0))
+
+
+def gather_z_small(piece):
+    size, here = lax.axis_size("z"), lax.axis_index("z")
+    if size != 4:
+        return [gather_z(piece)]
+    return [piece] + [lax.ppermute(piece, "z", pairs) for pairs in (Z_NEAR, Z_FAR, Z_ACROSS)]
+
+
+def join_pieces(pieces):
+    if len(pieces) == 1:
+        return pieces[0]
+    here = lax.axis_index("z")
+    whole = jnp.zeros((len(pieces),) + pieces[0].shape, pieces[0].dtype)
+    for step, part in enumerate(pieces):
+        whole = lax.dynamic_update_index_in_dim(whole, part, here ^ step, 0)
+    return whole
 
 
 def reduce_z(parts):
@@ -734,10 +761,17 @@
         )
 
     fused_own = gather_z(fused_shard).reshape(width // 2, fused_cols)
-    fused_own, output_weight, arrived_tokens, *ff_shards = tie(
-        fused_own, output_weight, arrived_tokens, *ff_shards
-    )
-    output_own = gather_z(output_weight)
+    output_pieces = gather_z_small(output_weight)
+    crossed = lax.ppermute(output_pieces[0], "x", SWAP)
+    count = len(output_pieces)
+    fused_own, arrived_tokens, crossed, *rest = tie(
+        fused_own, arrived_tokens, crossed, *output_pieces, *ff_shards
+    )
+    output_pieces, ff_shards = rest[:count], rest[count:]
+    crossed = [crossed] + [lax.ppermute(part, "x", SWAP) for part in output_pieces[1:]]
+    *crossed, fused_own = tie(*crossed, fused_own)
+    output_own, output_other = join_pieces(output_pieces), join_pieces(crossed)
+    ff_weights = [gather_z(ff_shards[0])]
     fused_other = lax.ppermute(fused_own, "x", SWAP)
 
     inputs = outer_sum(to_place, arrived_tokens)
@@ -745,8 +779,6 @@
     first_normed = (inputs * first_scale * gain_one).astype(BF16)
     blocks = swap_blocks(first_normed, shard_rows, here_x)
     first_normed = jnp.concatenate(blocks[0::2] + blocks[1::2], axis=1)
-    first_shard, first_normed = tie(ff_shards[0], first_normed)
-    ff_weights = [gather_z(first_shard)]
     segments, tables = [], []
     for index in range(micro):
         segment, positions = sequence_layout(lengths[index, 0], group_rows)
@@ -757,7 +789,6 @@
     tables = tuple(jnp.stack(table) for table in zip(*tables))
     rows_own = first_normed.reshape(micro, local_rows, width)
     rows_beside = lax.ppermute(rows_own, "y", SWAP)
-    output_other = lax.ppermute(output_own, "x", SWAP)
     rows_own, rows_beside, fused_other = tie(rows_own, rows_beside, fused_other)
     output_full = in_order(here_x, output_own, output_other, axis=1).reshape(query_cols, width)
     pieces = (
@@ -788,17 +819,24 @@
     planes[1], cot_all = tie(planes[1], cot_all)
     normed_two_all = join_planes(tuple(planes))
 
-    previous = ()
+    earlier = []
     gate_kept, gate_moved, down_grads = [], [], []
     for chunk in range(CHUNKS):
-        hidden, d_both, *previous = feedforward(
-            normed_two_all, cot_all, ff_weights[chunk], chunk_cols, previous, chunk == CHUNKS - 1
+        last = chunk == CHUNKS - 1
+        hidden, d_both, *sums = feedforward(
+            normed_two_all,
+            cot_all,
+            ff_weights[chunk],
+            chunk_cols,
+            earlier if last else [],
+            last,
         )
-        if chunk == CHUNKS - 1:
-            d_own, d_leaving = reduce_eight(*previous[2:])
+        earlier.append((hidden, d_both, ff_weights[chunk]))
+        if last:
+            d_own, d_leaving = reduce_eight(*sums[2:])
             d_both, *d_leaving = tie(d_both, *d_leaving)
         part = feedforward_grads(normed_two_all, d_both, hidden, cot_all, z_size)
-        if chunk == CHUNKS - 1:
+        if last:
             part, *d_arrived = tie(part, *send_eight(d_leaving))
         total = reduce_z(part)
         own, other = choose(here_x, total[:shard_rows], total[shard_rows : 2 * shard_rows])
@@ -819,7 +857,7 @@
     d_through, d_gain_two = norm_backward(residual, second_scale, gain_two, d_normed_two)
     d_residual = cot_rows.astype(F32) + d_through
 
-    d_residual, *out_parts = tie(d_residual, *previous[:2])
+    d_residual, *out_parts = tie(d_residual, *sums[:2])
     out_own, out_leaving = reduce_eight(*out_parts)
     pieces = gather_tensor(d_residual.astype(BF16).reshape(micro, local_rows, width))
     out_over_x = lax.ppermute(jnp.stack([out_leaving[0], out_leaving[2]]), "x", SWAP)

time: 709 us -> 692 us (0.976)
  waiting for transfers between devices: 351 us -> 326 us
    all_gather x4 -> x3, waiting for transfers between devices: 37.4 us -> 11.7 us  [gather_z(): return rows_major(lax.all_gather(rows_major(piece), 'z', axis=0))]
    reduce_scatter x4, waiting for transfers between devices: 16.1 us -> 0.02 us  [reduce_z(): return lax.psum_scatter(parts, 'z', scatter_dimension=0)]
    ppermute x1, waiting for transfers between devices: 0.01 us -> 16 us  [body(): cot_beside = lax.ppermute(cot_rows, 'y', SWAP)]
    ppermute x1 -> x7, starting transfers between devices: 1.47 us -> 14.7 us  [the longest x3 7.93 us: gather_z_small(): lax.ppermute(piece, 'z', pairs)]
    ppermute x1, waiting for transfers between devices: 13.2 us -> 0.01 us  [body(): fused_other = lax.ppermute(fused_own, 'x', SWAP)]
    all_to_all x3, waiting for transfers between devices: 53.1 us -> 63.7 us  [exchange(): lax.all_to_all(blocks, everywhere, split_axis=0, concat_axis=0, tiled=True)]
    ppermute x2, waiting for transfers between devices: 13.1 us -> 23.5 us  [body(): gate_moved = [lax.ppermute(part, 'x', SWAP) for part in gate_moved]]
    reduce_scatter x4, starting transfers between devices: 10.5 us -> 0.78 us  [reduce_z(): return lax.psum_scatter(parts, 'z', scatter_dimension=0)]
  transfers between devices with their start and end apart: 50 -> 55, of which waited for: 29 -> 29; matrix products, arithmetic and copies ran while one was open for 13% -> 14% of each run, Pallas kernels for 24% -> 25%
where the time goes in v5:
time: 692 us; the launch traced here: 688 us
  waiting for transfers between devices  326 us (47%)
  Pallas kernels  175 us (25%)
  other arithmetic  71.8 us (10%)
  starting transfers between devices  57.1 us (8%)
  local copies, waits for them, and re-layouts  35.7 us (5%)
  between operations  15.3 us (2%)
  matrix products  7.36 us (1%)
    pallas_call x2, Pallas kernels, feedforward(): pl.pallas_call(functools.partial(feedforward_kernel, len(earlier), last),...  76.5 us
    all_to_all x3, waiting for transfers between devices, exchange(): lax.all_to_all(blocks, everywhere, split_axis=0, concat_axis=0, tiled=True)  63.7 us
    pallas_call x2, Pallas kernels, feedforward_grads(): pl.pallas_call(feedforward_grads_kernel, grid=(pieces,), in_specs=[pl.Blo...  42.5 us
    ppermute x2, waiting for transfers between devices, reduce_tensor(): lax.ppermute(moved, 'y', SWAP).astype(F32)  39.9 us
    ppermute x2, waiting for transfers between devices, reduce_x(): lax.ppermute(leaving, 'x', SWAP).astype(F32)  30.9 us
    pallas_call x1, Pallas kernels, attention_backward(): pl.pallas_call(functools.partial(attention_backward_kernel, query_cols //...  30.8 us
    ppermute x3, waiting for transfers between devices, send_eight(): lax.ppermute(part, axes, pairs)  24.3 us
    ppermute x2, waiting for transfers between devices, body(): gate_moved = [lax.ppermute(part, 'x', SWAP) for part in gate_moved]  23.5 us
  transfers between devices with their start and end apart: 55, of which 29 were waited for; matrix products, arithmetic and copies ran while one was open for 14% of the time, Pallas kernels for 25%

profile of v5, /device:TPU:0, one launch (start us, length us, event | category | flops | bytes accessed | tf_op | source)
XLA Modules:
  0.0 687.6 jit_solution(1401409373807882845)
XLA Ops:
  36.5 13.6 %collective-permute-done.4 = bf16[256,1024]{1,0:T(8,128)(2,1)} collective-permute-done((bf16[256,1024]{1,0:T(8,128)(2,1)}, bf16[256,1024]{1,0:T(8,128)(2,1)}, u32[]{:S(2)}, u32[]{:S(2)}) %collective-permute-start.4) | collective-permute-done | bytes 524320 | tf_op jit(solution)/shard_map/ppermute | solution.py:759
  55.0 8.1 %collective-permute-done.5 = bf16[256,1024]{1,0:T(8,128)(2,1)} collective-permute-done((bf16[256,1024]{1,0:T(8,128)(2,1)}, bf16[256,1024]{1,0:T(8,128)(2,1)}, u32[]{:S(2)}, u32[]{:S(2)}) %collective-permute-start.5) | collective-permute-done | bytes 524320 | tf_op jit(solution)/shard_map/ppermute | solution.py:759
  66.2 19.7 %all-to-all-done = bf16[32,8,2176]{2,1,0:T(8,128)(2,1)S(1)} async-done(((bf16[32,8,2176]{2,1,0:T(8,128)(2,1)}), bf16[32,8,2176]{2,1,0:T(8,128)(2,1)S(1)}, u32[]{:S(2)}, u32[]{:S(2)}) %all-to-all-start) | async-done | bytes 1114144 | tf_op jit(solution)/shard_map/all_to_all | solution.py:715
  86.1 7.1 %all-gather.7.cloned.1.call-done.own_ref = bf16[1024,1024]{1,0:T(8,128)(2,1)} async-done(((bf16[256,1024]{1,0:T(8,128)(2,1)}), bf16[1024,1024]{1,0:T(8,128)(2,1)}) %all-gather.7.cloned.1.call-update) | async-done | bytes 2097168 | tf_op jit(solution)/shard_map/all_gather | solution.py:584
  130.3 19.8 %all-to-all-done.1 = bf16[32,8,2048]{2,1,0:T(8,128)(2,1)} async-done(((bf16[32,8,2048]{2,1,0:T(8,128)(2,1)}), bf16[32,8,2048]{2,1,0:T(8,128)(2,1)}, u32[]{:S(2)}, u32[]{:S(2)}) %all-to-all-start.1) | async-done | bytes 1048608 | tf_op jit(solution)/shard_map/all_to_all | solution.py:715
  155.8 16.0 %collective-permute-done.6 = bf16[256,2048]{1,0:T(8,128)(2,1)S(1)} collective-permute-done((bf16[256,2048]{1,0:T(8,128)(2,1)S(1)}, bf16[256,2048]{1,0:T(8,128)(2,1)S(1)}, u32[]{:S(2)}, u32[]{:S(2)}) %collective-permute-start.6) | collective-permute-done | bytes 1048608 | tf_op jit(solution)/shard_map/ppermute | solution.py:801
  184.7 17.1 %shard_map.213 = (bf16[1024,2048]{1,0:T(8,128)(2,1)}, bf16[1024,1024]{1,0:T(8,128)(2,1)}, bf16[1024,512]{1,0:T(8,128)(2,1)}, bf16[2,2,128,2048]{3,2,1,0:T(8,128)(2,1)}, bf16[2,2,128,2048]{3,2,1,0:T(8,128)(2,1)}) custom-call(s32[2]{0:T(128)} %pad_add_fusion.1.place_ref, bf16[2,128,2048]{2,1,0:T(8,128)(2,1)} %bitcast.28.piece0, ...), custom_call_target="tpu_custom_call" | custom-call | tf_op jit(solution)/shard_map/pallas_call | solution.py:294
  213.9 22.1 %collective-permute-done.17 = bf16[2,128,2048]{2,1,0:T(8,128)(2,1)} collective-permute-done((bf16[2,128,2048]{2,1,0:T(8,128)(2,1)}, bf16[2,128,2048]{2,1,0:T(8,128)(2,1)}, u32[]{:S(2)}, u32[]{:S(2)}) %collective-permute-start.17) | collective-permute-done | bytes 1048608 | tf_op jit(solution)/shard_map/ppermute | solution.py:633
  244.6 21.7 %collective-permute-done.18 = bf16[256,2048]{1,0:T(8,128)(2,1)S(1)} collective-permute-done((bf16[256,2048]{1,0:T(8,128)(2,1)S(1)}, bf16[256,2048]{1,0:T(8,128)(2,1)S(1)}, u32[]{:S(2)}, u32[]{:S(2)}) %collective-permute-start.18) | collective-permute-done | bytes 1048608 | tf_op jit(solution)/shard_map/ppermute | solution.py:639
  266.3 21.2 %collective-permute-done.23 = bf16[256,2048]{1,0:T(8,128)(2,1)S(1)} collective-permute-done((bf16[256,2048]{1,0:T(8,128)(2,1)S(1)}, bf16[256,2048]{1,0:T(8,128)(2,1)S(1)}, u32[]{:S(2)}, u32[]{:S(2)}) %collective-permute-start.23) | collective-permute-done | bytes 1048608 | tf_op jit(solution)/shard_map/ppermute | solution.py:640
  295.6 20.4 %shard_map.214 = (bf16[2048,512]{1,0:T(8,128)(2,1)}, bf16[2048,1024]{1,0:T(8,128)(2,1)}) custom-call(bf16[2048,2048]{1,0:T(8,128)(2,1)} %constant_dynamic-update-slice_fusion.8.normed_ref, bf16[2048,2048]{1,0:T(8,128)(2,1)} %copy-done.2, bf16[4,768,1024]{2,1,0:T(8,128)(2,1)} %bitcast.186), custom_call_target="tpu_custom_call" | custom-call | tf_op jit(solution)/shard_map/pallas_call | solution.py:446
  316.0 21.0 %shard_map.218 = bf16[4,768,1024]{2,1,0:T(8,128)(2,1)} custom-call(bf16[2048,2048]{1,0:T(8,128)(2,1)} %constant_dynamic-update-slice_fusion.8.normed_ref, bf16[2048,1024]{1,0:T(8,128)(2,1)} %get-tuple-element.139.refs_1_.d_both_ref, bf16[2048,512]{1,0:T(8,128)(2,1)} %get-tuple-element.138.refs_0_.hidden_ref, bf16[2048,2048]{1,0:T(8,128)(2,1)} %copy-done.2), custom_call_target="tpu_custom_call" | custom-call | tf_op jit(solution)/shard_map/pallas_call | solution.py:482
  342.1 56.1 %shard_map.215 = (bf16[2048,512]{1,0:T(8,128)(2,1)}, bf16[2048,1024]{1,0:T(8,128)(2,1)}, bf16[1024,2048]{1,0:T(8,128)(2,1)}, bf16[1024,2048]{1,0:T(8,128)(2,1)},...) custom-call(bf16[2048,2048]{1,0:T(8,128)(2,1)} %constant_dynamic-update-slice_fusion.8.normed_ref, ...), custom_call_target="tpu_custom_call" | custom-call | tf_op jit(solution)/shard_map/pallas_call | solution.py:446
  398.3 7.3 %collective-permute-done.29 = bf16[4,256,2048]{2,1,0:T(8,128)(2,1)S(1)} collective-permute-done((bf16[4,256,2048]{2,1,0:T(8,128)(2,1)}, bf16[4,256,2048]{2,1,0:T(8,128)(2,1)S(1)}, u32[]{:S(2)}, u32[]{:S(2)}) %collective-permute-start.29) | collective-permute-done | bytes 4194336 | tf_op jit(solution)/shard_map/ppermute | solution.py:651
  415.1 21.4 %shard_map.216 = bf16[4,768,1024]{2,1,0:T(8,128)(2,1)} custom-call(bf16[2048,2048]{1,0:T(8,128)(2,1)} %constant_dynamic-update-slice_fusion.8.normed_ref, bf16[2048,1024]{1,0:T(8,128)(2,1)} %get-tuple-element.143.d_both_ref, bf16[2048,512]{1,0:T(8,128)(2,1)} %get-tuple-element.144.hidden_ref, bf16[2048,2048]{1,0:T(8,128)(2,1)} %copy-done.2), custom_call_target="tpu_custom_call" | custom-call | tf_op jit(solution)/shard_map/pallas_call | solution.py:482
  437.9 22.9 %collective-permute-done.31 = bf16[256,2048]{1,0:T(8,128)(2,1)} collective-permute-done((bf16[256,2048]{1,0:T(8,128)(2,1)}, bf16[256,2048]{1,0:T(8,128)(2,1)}, u32[]{:S(2)}, u32[]{:S(2)}) %collective-permute-start.31) | collective-permute-done | bytes 1048608 | tf_op jit(solution)/shard_map/ppermute | solution.py:658
  478.7 14.1 %collective-permute-done.35.piece2 = bf16[2,128,2048]{2,1,0:T(8,128)(2,1)S(1)} collective-permute-done((bf16[2,128,2048]{2,1,0:T(8,128)(2,1)S(1)}, bf16[2,128,2048]{2,1,0:T(8,128)(2,1)S(1)}, u32[]{:S(2)}, u32[]{:S(2)}) %collective-permute-start.35) | collective-permute-done | bytes 1048608 | tf_op jit(solution)/shard_map/ppermute | solution.py:621
  496.5 30.8 %shard_map.217 = (bf16[2,2,128,2048]{3,2,1,0:T(8,128)(2,1)}, bf16[2,2,128,2048]{3,2,1,0:T(8,128)(2,1)}, bf16[1024,1024]{1,0:T(8,128)(2,1)}, bf16[1024,1024]{1,0:...) custom-call(s32[2]{0:T(128)} %pad_add_fusion.1.place_ref, bf16[2,128,2048]{2,1,0:T(8,128)(2,1)} %bitcast.210, ...), custom_call_target="tpu_custom_call" | custom-call | tf_op jit(solution)/shard_map/pallas_call | solution.py:327
  536.9 16.3 %collective-permute-done.41 = bf16[256,2048]{1,0:T(8,128)(2,1)S(1)} collective-permute-done((bf16[256,2048]{1,0:T(8,128)(2,1)}, bf16[256,2048]{1,0:T(8,128)(2,1)S(1)}, u32[]{:S(2)}, u32[]{:S(2)}) %collective-permute-start.41) | collective-permute-done | bytes 1048608 | tf_op jit(solution)/shard_map/ppermute | solution.py:890
  562.1 17.8 %collective-permute-done.40 = bf16[2,128,2048]{2,1,0:T(8,128)(2,1)} collective-permute-done((bf16[2,128,2048]{2,1,0:T(8,128)(2,1)}, bf16[2,128,2048]{2,1,0:T(8,128)(2,1)}, u32[]{:S(2)}, u32[]{:S(2)}) %collective-permute-start.40) | collective-permute-done | bytes 1048608 | tf_op jit(solution)/shard_map/ppermute | solution.py:633
  594.0 14.6 %collective-permute-done.42 = bf16[1024,1024]{1,0:T(8,128)(2,1)} collective-permute-done((bf16[1024,1024]{1,0:T(8,128)(2,1)}, bf16[1024,1024]{1,0:T(8,128)(2,1)}, u32[]{:S(2)}, u32[]{:S(2)}) %collective-permute-start.42) | collective-permute-done | bytes 2097184 | tf_op jit(solution)/shard_map/ppermute | solution.py:890
  622.8 12.5 %collective-permute-done.43.refs_1_ = bf16[256,1024]{1,0:T(8,128)(2,1)} collective-permute-done((bf16[256,1024]{1,0:T(8,128)(2,1)}, bf16[256,1024]{1,0:T(8,128)(2,1)}, u32[]{:S(2)}, u32[]{:S(2)}) %collective-permute-start.43) | collective-permute-done | bytes 524320 | tf_op jit(solution)/shard_map/ppermute | solution.py:897
  635.4 10.9 %collective-permute-done.44.refs_3_ = bf16[256,1024]{1,0:T(8,128)(2,1)} collective-permute-done((bf16[256,1024]{1,0:T(8,128)(2,1)}, bf16[256,1024]{1,0:T(8,128)(2,1)}, u32[]{:S(2)}, u32[]{:S(2)}) %collective-permute-start.44) | collective-permute-done | bytes 524320 | tf_op jit(solution)/shard_map/ppermute | solution.py:897
  650.5 24.2 %all-to-all-done.2 = bf16[32,8,4224]{2,1,0:T(8,128)(2,1)S(1)} async-done(((bf16[32,8,4224]{2,1,0:T(8,128)(2,1)}), bf16[32,8,4224]{2,1,0:T(8,128)(2,1)S(1)}, u32[]{:S(2)}, u32[]{:S(2)}) %all-to-all-start.2) | async-done | bytes 2162720 | tf_op jit(solution)/shard_map/all_to_all | solution.py:715
  (318 shorter events, 215.5 us)
Async XLA Ops:
  7.2 86.0 %all-gather.7.cloned.1.call-start = ((), (), s32[]{:S(2)}) async-start(), calls=%async_computation.11 | async-start | bytes 2621440 | tf_op jit(solution)/shard_map/all_gather | solution.py:584
  7.2 78.8 %collective-permute-start = (bf16[64,2048]{1,0:T(8,128)(2,1)}, bf16[64,2048]{1,0:T(8,128)(2,1)}, u32[]{:S(2)}, u32[]{:S(2)}) collective-permute-start(bf16[64,2048]{1,0:T(8,128)(2,1)} %param.20), channel_id=1, source_target_pairs={{0,4},{4,0},{1,5},{5,1},{2,6},{6,2},{3,7},{7,3},{8,12},{12,8},{9,1... | collective-permute-start | bytes 786440 | tf_op jit(solution)/shard_map/ppermute | solution.py:765
  10.2 75.8 %collective-permute-start.1 = (bf16[64,2048]{1,0:T(8,128)(2,1)}, bf16[64,2048]{1,0:T(8,128)(2,1)}, u32[]{:S(2)}, u32[]{:S(2)}) collective-permute-start(bf16[64,2048]{1,0:T(8,128)(2,1)} %param.20), channel_id=1, source_target_pairs={{0,8},{8,0},{16,24},{24,16},{1,9},{9,1},{17,25},{25,17},{2,10},{10... | collective-permute-start | bytes 786440 | tf_op jit(solution)/shard_map/ppermute | solution.py:591
  11.8 74.3 %collective-permute-start.2 = (bf16[64,2048]{1,0:T(8,128)(2,1)}, bf16[64,2048]{1,0:T(8,128)(2,1)}, u32[]{:S(2)}, u32[]{:S(2)}) collective-permute-start(bf16[64,2048]{1,0:T(8,128)(2,1)} %param.20), channel_id=1, source_target_pairs={{0,16},{16,0},{8,24},{24,8},{1,17},{17,1},{9,25},{25,9},{2,18},{18... | collective-permute-start | bytes 786440 | tf_op jit(solution)/shard_map/ppermute | solution.py:591
  23.4 62.5 %all-to-all-start = ((bf16[32,8,2176]{2,1,0:T(8,128)(2,1)}), bf16[32,8,2176]{2,1,0:T(8,128)(2,1)S(1)}, u32[]{:S(2)}, u32[]{:S(2)}) async-start(bf16[32,8,2176]{2,1,0:T(8,128)(2,1)} %pad_maximum_fusion.5), calls=%async_computation | async-start | bytes 2228224 | tf_op jit(solution)/shard_map/all_to_all | solution.py:715
  26.2 269.4 %all-gather.11.cloned.1.call-start = ((), (), s32[]{:S(2)}) async-start(), calls=%async_computation.13 | async-start | bytes 7864320 | tf_op jit(solution)/shard_map/all_gather | solution.py:584
  50.1 36.0 %collective-permute-start.3 = (bf16[64,2048]{1,0:T(8,128)(2,1)S(1)}, bf16[64,2048]{1,0:T(8,128)(2,1)}, u32[]{:S(2)}, u32[]{:S(2)}) collective-permute-start(bf16[64,2048]{1,0:T(8,128)(2,1)S(1)} %copy-done.36), channel_id=1, source_target_pairs={{0,24},{24,0},{8,16},{16,8},{1,25},{25,1},{9,17},{17,9},{2,26},{26... | collective-permute-start | bytes 786440 | tf_op jit(solution)/shard_map/ppermute | solution.py:591
  93.4 56.7 %all-to-all-start.1 = ((bf16[32,8,2048]{2,1,0:T(8,128)(2,1)}), bf16[32,8,2048]{2,1,0:T(8,128)(2,1)}, u32[]{:S(2)}, u32[]{:S(2)}) async-start(bf16[32,8,2048]{2,1,0:T(8,128)(2,1)} %bitcast.11), calls=%async_computation.1 | async-start | bytes 2097152 | tf_op jit(solution)/shard_map/all_to_all | solution.py:715
  98.3 243.9 %all-gather.9.cloned.1.call-start = ((), (), s32[]{:S(2)}) async-start(), calls=%async_computation.12 | async-start | bytes 7864320 | tf_op jit(solution)/shard_map/all_gather | solution.py:584
  109.0 69.7 %collective-permute-start.11 = (bf16[2,128,2048]{2,1,0:T(8,128)(2,1)}, bf16[2,128,2048]{2,1,0:T(8,128)(2,1)}, u32[]{:S(2)}, u32[]{:S(2)}) collective-permute-start(bf16[2,128,2048]{2,1,0:T(8,128)(2,1)} %bitcast.28.piece0), channel_id=1, source_target_pairs={{0,2},{2,0},{1,3},{3,1},{4,6},{6,4},{5,7},{7,5},{8,10},{10,8},{9,1... | collective-permute-start | bytes 3145736 | tf_op jit(solution)/shard_map/ppermute | solution.py:791
  127.8 50.9 %collective-permute-start.12 = (bf16[1024,1024]{1,0:T(8,128)(2,1)}, bf16[1024,1024]{1,0:T(8,128)(2,1)}, u32[]{:S(2)}, u32[]{:S(2)}) collective-permute-start(bf16[1024,1024]{1,0:T(8,128)(2,1)} %all-gather.7.cloned.1.call-done.own_ref), channel_id=1, source_target_pairs={{0,4},{4,0},{1,5},{5,1},{2,6},{6,2},{3,7},{7,3},{8,12},{12,8},{9,1... | collective-permute-start | bytes 6291464 | tf_op jit(solution)/shard_map/ppermute | solution.py:775
  202.9 388.7 %reduce-scatter.5.cloned.1.call-start = ((), (), s32[]{:S(2)}) async-start(), calls=%async_computation.7 | async-start | bytes 7864320 | tf_op jit(solution)/shard_map/reduce_scatter | solution.py:605
  240.7 46.8 %collective-permute-start.23 = (bf16[256,2048]{1,0:T(8,128)(2,1)S(1)}, bf16[256,2048]{1,0:T(8,128)(2,1)S(1)}, u32[]{:S(2)}, u32[]{:S(2)}) collective-permute-start(bf16[256,2048]{1,0:T(8,128)(2,1)S(1)} %get-tuple-element.185), channel_id=1, source_target_pairs={{0,2},{2,0},{1,3},{3,1},{4,6},{6,4},{5,7},{7,5},{8,10},{10,8},{9,1... | collective-permute-start | bytes 3145736 | tf_op jit(solution)/shard_map/ppermute | solution.py:640
  242.6 46.6 %collective-permute-start.24 = (bf16[256,2048]{1,0:T(8,128)(2,1)S(1)}, bf16[256,2048]{1,0:T(8,128)(2,1)S(1)}, u32[]{:S(2)}, u32[]{:S(2)}) collective-permute-start(bf16[256,2048]{1,0:T(8,128)(2,1)S(1)} %get-tuple-element.185), channel_id=1, source_target_pairs={{0,6},{6,0},{2,4},{4,2},{1,7},{7,1},{3,5},{5,3},{8,14},{14,8},{10,... | collective-permute-start | bytes 3145736 | tf_op jit(solution)/shard_map/ppermute | solution.py:641
  244.3 47.1 %collective-permute-start.25 = (bf16[256,2048]{1,0:T(8,128)(2,1)S(1)}, bf16[256,2048]{1,0:T(8,128)(2,1)S(1)}, u32[]{:S(2)}, u32[]{:S(2)}) collective-permute-start(bf16[256,2048]{1,0:T(8,128)(2,1)S(1)} %get-tuple-element.185), channel_id=1, source_target_pairs={{0,1},{1,0},{2,3},{3,2},{4,5},{5,4},{6,7},{7,6},{8,9},{9,8},{10,11... | collective-permute-start | bytes 3145736 | tf_op jit(solution)/shard_map/ppermute | solution.py:646
  337.1 275.4 %reduce-scatter.7.cloned.1.call-start = ((), (), s32[]{:S(2)}) async-start(), calls=%async_computation.8 | async-start | bytes 7864320 | tf_op jit(solution)/shard_map/reduce_scatter | solution.py:605
  413.0 47.8 %collective-permute-start.31 = (bf16[256,2048]{1,0:T(8,128)(2,1)}, bf16[256,2048]{1,0:T(8,128)(2,1)}, u32[]{:S(2)}, u32[]{:S(2)}) collective-permute-start(bf16[256,2048]{1,0:T(8,128)(2,1)} %get-tuple-element.146), channel_id=1, source_target_pairs={{0,2},{2,0},{1,3},{3,1},{4,6},{6,4},{5,7},{7,5},{8,10},{10,8},{9,1... | collective-permute-start | bytes 3145736 | tf_op jit(solution)/shard_map/ppermute | solution.py:658
  414.5 46.3 %collective-permute-start.32 = (bf16[256,2048]{1,0:T(8,128)(2,1)}, bf16[256,2048]{1,0:T(8,128)(2,1)}, u32[]{:S(2)}, u32[]{:S(2)}) collective-permute-start(bf16[256,2048]{1,0:T(8,128)(2,1)} %get-tuple-element.147), channel_id=1, source_target_pairs={{0,6},{6,0},{2,4},{4,2},{1,7},{7,1},{3,5},{5,3},{8,14},{14,8},{10,... | collective-permute-start | bytes 3145736 | tf_op jit(solution)/shard_map/ppermute | solution.py:658
  460.8 157.6 %reduce-scatter.11.cloned.1.call-start = ((), (), s32[]{:S(2)}) async-start(), calls=%async_computation.10 | async-start | bytes 1310720 | tf_op jit(solution)/shard_map/reduce_scatter | solution.py:605
  477.6 49.7 %collective-permute-start.37 = (bf16[2,256,2048]{2,1,0:T(8,128)(2,1)}, bf16[2,256,2048]{2,1,0:T(8,128)(2,1)}, u32[]{:S(2)}, u32[]{:S(2)}) collective-permute-start(bf16[2,256,2048]{2,1,0:T(8,128)(2,1)} %pad_maximum_fusion.2), channel_id=1, source_target_pairs={{0,4},{4,0},{1,5},{5,1},{2,6},{6,2},{3,7},{7,3},{8,12},{12,8},{9,1... | collective-permute-start | bytes 6291464 | tf_op jit(solution)/shard_map/ppermute | solution.py:863
  536.0 43.9 %collective-permute-start.40 = (bf16[2,128,2048]{2,1,0:T(8,128)(2,1)}, bf16[2,128,2048]{2,1,0:T(8,128)(2,1)}, u32[]{:S(2)}, u32[]{:S(2)}) collective-permute-start(bf16[2,128,2048]{2,1,0:T(8,128)(2,1)} %fusion.26), channel_id=1, source_target_pairs={{0,2},{2,0},{1,3},{3,1},{4,6},{6,4},{5,7},{7,5},{8,10},{10,8},{9,1... | collective-permute-start | bytes 3145736 | tf_op jit(solution)/shard_map/ppermute | solution.py:633
  554.5 54.1 %collective-permute-start.42 = (bf16[1024,1024]{1,0:T(8,128)(2,1)}, bf16[1024,1024]{1,0:T(8,128)(2,1)}, u32[]{:S(2)}, u32[]{:S(2)}) collective-permute-start(bf16[1024,1024]{1,0:T(8,128)(2,1)} %get-tuple-element.168), channel_id=1, source_target_pairs={{0,4},{4,0},{1,5},{5,1},{2,6},{6,2},{3,7},{7,3},{8,12},{12,8},{9,1... | collective-permute-start | bytes 6291464 | tf_op jit(solution)/shard_map/ppermute | solution.py:890
  588.7 86.0 %all-to-all-start.2 = ((bf16[32,8,4224]{2,1,0:T(8,128)(2,1)}), bf16[32,8,4224]{2,1,0:T(8,128)(2,1)S(1)}, u32[]{:S(2)}, u32[]{:S(2)}) async-start(bf16[32,8,4224]{2,1,0:T(8,128)(2,1)} %pad_maximum_fusion), calls=%async_computation.2 | async-start | bytes 4325376 | tf_op jit(solution)/shard_map/all_to_all | solution.py:715
  591.5 86.2 %reduce-scatter.9.cloned.1.call-start = ((), (), s32[]{:S(2)}) async-start(), calls=%async_computation.9 | async-start | bytes 2621440 | tf_op jit(solution)/shard_map/reduce_scatter | solution.py:605
  (72 other events, 965.3 us)
Sparse Core Ops, SparseCore 0:
  16.5 76.6 all-gather.6
  94.8 131.3 all-gather.10
  227.7 114.3 all-gather.8
  344.3 108.9 reduce-scatter.4
  460.9 108.0 reduce-scatter.6
  571.7 29.5 reduce-scatter.10
  614.8 61.0 reduce-scatter.8

commit v6 on v5

--- a/solution.py
+++ b/solution.py
@@ -837,7 +837,8 @@
             d_both, *d_leaving = tie(d_both, *d_leaving)
         part = feedforward_grads(normed_two_all, d_both, hidden, cot_all, z_size)
         if last:
-            part, *d_arrived = tie(part, *send_eight(d_leaving))
+            d_arrived = send_eight(d_leaving)
+            part, d_arrived[0] = tie(part, d_arrived[0])
         total = reduce_z(part)
         own, other = choose(here_x, total[:shard_rows], total[shard_rows : 2 * shard_rows])
         gate_kept.append(own)

time: 692 us -> 690 us (level)
  transfers between devices with their start and end apart: 55 -> 55, of which waited for: 29 -> 31; matrix products, arithmetic and copies ran while one was open for 14% -> 15% of each run, Pallas kernels for 25% -> 26%
where the time goes in v6:
time: 690 us; the launch traced here: 685 us
  waiting for transfers between devices  322 us (47%)
  Pallas kernels  175 us (25%)
  other arithmetic  72.3 us (10%)
  starting transfers between devices  59.5 us (9%)
  local copies, waits for them, and re-layouts  34.2 us (5%)
  between operations  15.3 us (2%)
  matrix products  7.37 us (1%)
    pallas_call x2, Pallas kernels, feedforward(): pl.pallas_call(functools.partial(feedforward_kernel, len(earlier), last),...  76.5 us
    all_to_all x3, waiting for transfers between devices, exchange(): lax.all_to_all(blocks, everywhere, split_axis=0, concat_axis=0, tiled=True)  59.5 us
    pallas_call x2, Pallas kernels, feedforward_grads(): pl.pallas_call(feedforward_grads_kernel, grid=(pieces,), in_specs=[pl.Blo...  42.5 us
    ppermute x2, waiting for transfers between devices, reduce_tensor(): lax.ppermute(moved, 'y', SWAP).astype(F32)  40 us
    ppermute x2, waiting for transfers between devices, reduce_x(): lax.ppermute(leaving, 'x', SWAP).astype(F32)  34.4 us
    pallas_call x1, Pallas kernels, attention_backward(): pl.pallas_call(functools.partial(attention_backward_kernel, query_cols //...  30.8 us
    ppermute x3, waiting for transfers between devices, send_eight(): lax.ppermute(part, axes, pairs)  25.4 us
    ppermute x1, waiting for transfers between devices, gather_planes(): lax.ppermute(rows, 'x', SWAP)  21.7 us
  transfers between devices with their start and end apart: 55, of which 31 were waited for; matrix products, arithmetic and copies ran while one was open for 15% of the time, Pallas kernels for 26%

profile of v6, /device:TPU:0, one launch (start us, length us, event | category | flops | bytes accessed | tf_op | source)
XLA Modules:
  0.0 685.5 jit_solution(16498567391065267609)
XLA Ops:
  36.5 13.6 %collective-permute-done.4 = bf16[256,1024]{1,0:T(8,128)(2,1)} collective-permute-done((bf16[256,1024]{1,0:T(8,128)(2,1)}, bf16[256,1024]{1,0:T(8,128)(2,1)}, u32[]{:S(2)}, u32[]{:S(2)}) %collective-permute-start.4) | collective-permute-done | bytes 524320 | tf_op jit(solution)/shard_map/ppermute | solution.py:759
  55.0 8.1 %collective-permute-done.5 = bf16[256,1024]{1,0:T(8,128)(2,1)} collective-permute-done((bf16[256,1024]{1,0:T(8,128)(2,1)}, bf16[256,1024]{1,0:T(8,128)(2,1)}, u32[]{:S(2)}, u32[]{:S(2)}) %collective-permute-start.5) | collective-permute-done | bytes 524320 | tf_op jit(solution)/shard_map/ppermute | solution.py:759
  66.2 19.7 %all-to-all-done = bf16[32,8,2176]{2,1,0:T(8,128)(2,1)S(1)} async-done(((bf16[32,8,2176]{2,1,0:T(8,128)(2,1)}), bf16[32,8,2176]{2,1,0:T(8,128)(2,1)S(1)}, u32[]{:S(2)}, u32[]{:S(2)}) %all-to-all-start) | async-done | bytes 1114144 | tf_op jit(solution)/shard_map/all_to_all | solution.py:715
  86.1 7.1 %all-gather.7.cloned.1.call-done.own_ref = bf16[1024,1024]{1,0:T(8,128)(2,1)} async-done(((bf16[256,1024]{1,0:T(8,128)(2,1)}), bf16[1024,1024]{1,0:T(8,128)(2,1)}) %all-gather.7.cloned.1.call-update) | async-done | bytes 2097168 | tf_op jit(solution)/shard_map/all_gather | solution.py:584
  130.3 19.8 %all-to-all-done.1 = bf16[32,8,2048]{2,1,0:T(8,128)(2,1)} async-done(((bf16[32,8,2048]{2,1,0:T(8,128)(2,1)}), bf16[32,8,2048]{2,1,0:T(8,128)(2,1)}, u32[]{:S(2)}, u32[]{:S(2)}) %all-to-all-start.1) | async-done | bytes 1048608 | tf_op jit(solution)/shard_map/all_to_all | solution.py:715
  155.8 16.0 %collective-permute-done.6 = bf16[256,2048]{1,0:T(8,128)(2,1)S(1)} collective-permute-done((bf16[256,2048]{1,0:T(8,128)(2,1)S(1)}, bf16[256,2048]{1,0:T(8,128)(2,1)S(1)}, u32[]{:S(2)}, u32[]{:S(2)}) %collective-permute-start.6) | collective-permute-done | bytes 1048608 | tf_op jit(solution)/shard_map/ppermute | solution.py:801
  184.7 17.1 %shard_map.213 = (bf16[1024,2048]{1,0:T(8,128)(2,1)}, bf16[1024,1024]{1,0:T(8,128)(2,1)}, bf16[1024,512]{1,0:T(8,128)(2,1)}, bf16[2,2,128,2048]{3,2,1,0:T(8,128)(2,1)}, bf16[2,2,128,2048]{3,2,1,0:T(8,128)(2,1)}) custom-call(s32[2]{0:T(128)} %pad_add_fusion.1.place_ref, bf16[2,128,2048]{2,1,0:T(8,128)(2,1)} %bitcast.28.piece0, ...), custom_call_target="tpu_custom_call" | custom-call | tf_op jit(solution)/shard_map/pallas_call | solution.py:294
  213.9 22.1 %collective-permute-done.17 = bf16[2,128,2048]{2,1,0:T(8,128)(2,1)} collective-permute-done((bf16[2,128,2048]{2,1,0:T(8,128)(2,1)}, bf16[2,128,2048]{2,1,0:T(8,128)(2,1)}, u32[]{:S(2)}, u32[]{:S(2)}) %collective-permute-start.17) | collective-permute-done | bytes 1048608 | tf_op jit(solution)/shard_map/ppermute | solution.py:633
  244.6 21.7 %collective-permute-done.18 = bf16[256,2048]{1,0:T(8,128)(2,1)S(1)} collective-permute-done((bf16[256,2048]{1,0:T(8,128)(2,1)S(1)}, bf16[256,2048]{1,0:T(8,128)(2,1)S(1)}, u32[]{:S(2)}, u32[]{:S(2)}) %collective-permute-start.18) | collective-permute-done | bytes 1048608 | tf_op jit(solution)/shard_map/ppermute | solution.py:639
  266.3 21.2 %collective-permute-done.23 = bf16[256,2048]{1,0:T(8,128)(2,1)S(1)} collective-permute-done((bf16[256,2048]{1,0:T(8,128)(2,1)S(1)}, bf16[256,2048]{1,0:T(8,128)(2,1)S(1)}, u32[]{:S(2)}, u32[]{:S(2)}) %collective-permute-start.23) | collective-permute-done | bytes 1048608 | tf_op jit(solution)/shard_map/ppermute | solution.py:640
  295.6 20.4 %shard_map.214 = (bf16[2048,512]{1,0:T(8,128)(2,1)}, bf16[2048,1024]{1,0:T(8,128)(2,1)}) custom-call(bf16[2048,2048]{1,0:T(8,128)(2,1)} %constant_dynamic-update-slice_fusion.8.normed_ref, bf16[2048,2048]{1,0:T(8,128)(2,1)} %copy-done.2, bf16[4,768,1024]{2,1,0:T(8,128)(2,1)} %bitcast.186), custom_call_target="tpu_custom_call" | custom-call | tf_op jit(solution)/shard_map/pallas_call | solution.py:446
  316.0 21.0 %shard_map.218 = bf16[4,768,1024]{2,1,0:T(8,128)(2,1)} custom-call(bf16[2048,2048]{1,0:T(8,128)(2,1)} %constant_dynamic-update-slice_fusion.8.normed_ref, bf16[2048,1024]{1,0:T(8,128)(2,1)} %get-tuple-element.137.refs_1_.d_both_ref, bf16[2048,512]{1,0:T(8,128)(2,1)} %get-tuple-element.136.refs_0_.hidden_ref, bf16[2048,2048]{1,0:T(8,128)(2,1)} %copy-done.2), custom_call_target="tpu_custom_call" | custom-call | tf_op jit(solution)/shard_map/pallas_call | solution.py:482
  342.1 56.1 %shard_map.215 = (bf16[2048,512]{1,0:T(8,128)(2,1)}, bf16[2048,1024]{1,0:T(8,128)(2,1)}, bf16[1024,2048]{1,0:T(8,128)(2,1)}, bf16[1024,2048]{1,0:T(8,128)(2,1)},...) custom-call(bf16[2048,2048]{1,0:T(8,128)(2,1)} %constant_dynamic-update-slice_fusion.8.normed_ref, ...), custom_call_target="tpu_custom_call" | custom-call | tf_op jit(solution)/shard_map/pallas_call | solution.py:446
  398.3 7.3 %collective-permute-done.29 = bf16[4,256,2048]{2,1,0:T(8,128)(2,1)S(1)} collective-permute-done((bf16[4,256,2048]{2,1,0:T(8,128)(2,1)}, bf16[4,256,2048]{2,1,0:T(8,128)(2,1)S(1)}, u32[]{:S(2)}, u32[]{:S(2)}) %collective-permute-start.29) | collective-permute-done | bytes 4194336 | tf_op jit(solution)/shard_map/ppermute | solution.py:651
  415.1 21.4 %shard_map.216 = bf16[4,768,1024]{2,1,0:T(8,128)(2,1)} custom-call(bf16[2048,2048]{1,0:T(8,128)(2,1)} %constant_dynamic-update-slice_fusion.8.normed_ref, bf16[2048,1024]{1,0:T(8,128)(2,1)} %get-tuple-element.141.d_both_ref, bf16[2048,512]{1,0:T(8,128)(2,1)} %get-tuple-element.142.hidden_ref, bf16[2048,2048]{1,0:T(8,128)(2,1)} %copy-done.2), custom_call_target="tpu_custom_call" | custom-call | tf_op jit(solution)/shard_map/pallas_call | solution.py:482
  438.0 22.6 %collective-permute-done.32 = bf16[256,2048]{1,0:T(8,128)(2,1)} collective-permute-done((bf16[256,2048]{1,0:T(8,128)(2,1)}, bf16[256,2048]{1,0:T(8,128)(2,1)}, u32[]{:S(2)}, u32[]{:S(2)}) %collective-permute-start.32) | collective-permute-done | bytes 1048608 | tf_op jit(solution)/shard_map/ppermute | solution.py:658
  480.1 13.5 %collective-permute-done.35.piece2 = bf16[2,128,2048]{2,1,0:T(8,128)(2,1)S(1)} collective-permute-done((bf16[2,128,2048]{2,1,0:T(8,128)(2,1)S(1)}, bf16[2,128,2048]{2,1,0:T(8,128)(2,1)S(1)}, u32[]{:S(2)}, u32[]{:S(2)}) %collective-permute-start.35) | collective-permute-done | bytes 1048608 | tf_op jit(solution)/shard_map/ppermute | solution.py:621
  497.3 30.8 %shard_map.217 = (bf16[2,2,128,2048]{3,2,1,0:T(8,128)(2,1)}, bf16[2,2,128,2048]{3,2,1,0:T(8,128)(2,1)}, bf16[1024,1024]{1,0:T(8,128)(2,1)}, bf16[1024,1024]{1,0:...) custom-call(s32[2]{0:T(128)} %pad_add_fusion.1.place_ref, bf16[2,128,2048]{2,1,0:T(8,128)(2,1)} %bitcast.210, ...), custom_call_target="tpu_custom_call" | custom-call | tf_op jit(solution)/shard_map/pallas_call | solution.py:327
  538.4 15.6 %collective-permute-done.41 = bf16[256,2048]{1,0:T(8,128)(2,1)S(1)} collective-permute-done((bf16[256,2048]{1,0:T(8,128)(2,1)}, bf16[256,2048]{1,0:T(8,128)(2,1)S(1)}, u32[]{:S(2)}, u32[]{:S(2)}) %collective-permute-start.41) | collective-permute-done | bytes 1048608 | tf_op jit(solution)/shard_map/ppermute | solution.py:891
  563.5 17.9 %collective-permute-done.40 = bf16[2,128,2048]{2,1,0:T(8,128)(2,1)} collective-permute-done((bf16[2,128,2048]{2,1,0:T(8,128)(2,1)}, bf16[2,128,2048]{2,1,0:T(8,128)(2,1)}, u32[]{:S(2)}, u32[]{:S(2)}) %collective-permute-start.40) | collective-permute-done | bytes 1048608 | tf_op jit(solution)/shard_map/ppermute | solution.py:633
  595.5 18.9 %collective-permute-done.42 = bf16[1024,1024]{1,0:T(8,128)(2,1)} collective-permute-done((bf16[1024,1024]{1,0:T(8,128)(2,1)}, bf16[1024,1024]{1,0:T(8,128)(2,1)}, u32[]{:S(2)}, u32[]{:S(2)}) %collective-permute-start.42) | collective-permute-done | bytes 2097184 | tf_op jit(solution)/shard_map/ppermute | solution.py:891
  628.8 10.0 %collective-permute-done.43.refs_1_ = bf16[256,1024]{1,0:T(8,128)(2,1)} collective-permute-done((bf16[256,1024]{1,0:T(8,128)(2,1)}, bf16[256,1024]{1,0:T(8,128)(2,1)}, u32[]{:S(2)}, u32[]{:S(2)}) %collective-permute-start.43) | collective-permute-done | bytes 524320 | tf_op jit(solution)/shard_map/ppermute | solution.py:898
  638.8 8.4 %collective-permute-done.44.refs_3_ = bf16[256,1024]{1,0:T(8,128)(2,1)} collective-permute-done((bf16[256,1024]{1,0:T(8,128)(2,1)}, bf16[256,1024]{1,0:T(8,128)(2,1)}, u32[]{:S(2)}, u32[]{:S(2)}) %collective-permute-start.44) | collective-permute-done | bytes 524320 | tf_op jit(solution)/shard_map/ppermute | solution.py:898
  651.4 20.0 %all-to-all-done.2 = bf16[32,8,4224]{2,1,0:T(8,128)(2,1)S(1)} async-done(((bf16[32,8,4224]{2,1,0:T(8,128)(2,1)}), bf16[32,8,4224]{2,1,0:T(8,128)(2,1)S(1)}, u32[]{:S(2)}, u32[]{:S(2)}) %all-to-all-start.2) | async-done | bytes 2162720 | tf_op jit(solution)/shard_map/all_to_all | solution.py:715
  (318 shorter events, 219.9 us)
Async XLA Ops:
  7.2 86.0 %all-gather.7.cloned.1.call-start = ((), (), s32[]{:S(2)}) async-start(), calls=%async_computation.11 | async-start | bytes 2621440 | tf_op jit(solution)/shard_map/all_gather | solution.py:584
  7.2 78.8 %collective-permute-start = (bf16[64,2048]{1,0:T(8,128)(2,1)}, bf16[64,2048]{1,0:T(8,128)(2,1)}, u32[]{:S(2)}, u32[]{:S(2)}) collective-permute-start(bf16[64,2048]{1,0:T(8,128)(2,1)} %param.20), channel_id=1, source_target_pairs={{0,4},{4,0},{1,5},{5,1},{2,6},{6,2},{3,7},{7,3},{8,12},{12,8},{9,1... | collective-permute-start | bytes 786440 | tf_op jit(solution)/shard_map/ppermute | solution.py:765
  10.2 75.8 %collective-permute-start.1 = (bf16[64,2048]{1,0:T(8,128)(2,1)}, bf16[64,2048]{1,0:T(8,128)(2,1)}, u32[]{:S(2)}, u32[]{:S(2)}) collective-permute-start(bf16[64,2048]{1,0:T(8,128)(2,1)} %param.20), channel_id=1, source_target_pairs={{0,8},{8,0},{16,24},{24,16},{1,9},{9,1},{17,25},{25,17},{2,10},{10... | collective-permute-start | bytes 786440 | tf_op jit(solution)/shard_map/ppermute | solution.py:591
  11.8 74.3 %collective-permute-start.2 = (bf16[64,2048]{1,0:T(8,128)(2,1)}, bf16[64,2048]{1,0:T(8,128)(2,1)}, u32[]{:S(2)}, u32[]{:S(2)}) collective-permute-start(bf16[64,2048]{1,0:T(8,128)(2,1)} %param.20), channel_id=1, source_target_pairs={{0,16},{16,0},{8,24},{24,8},{1,17},{17,1},{9,25},{25,9},{2,18},{18... | collective-permute-start | bytes 786440 | tf_op jit(solution)/shard_map/ppermute | solution.py:591
  23.4 62.5 %all-to-all-start = ((bf16[32,8,2176]{2,1,0:T(8,128)(2,1)}), bf16[32,8,2176]{2,1,0:T(8,128)(2,1)S(1)}, u32[]{:S(2)}, u32[]{:S(2)}) async-start(bf16[32,8,2176]{2,1,0:T(8,128)(2,1)} %pad_maximum_fusion.5), calls=%async_computation | async-start | bytes 2228224 | tf_op jit(solution)/shard_map/all_to_all | solution.py:715
  26.2 269.4 %all-gather.11.cloned.1.call-start = ((), (), s32[]{:S(2)}) async-start(), calls=%async_computation.13 | async-start | bytes 7864320 | tf_op jit(solution)/shard_map/all_gather | solution.py:584
  50.1 36.0 %collective-permute-start.3 = (bf16[64,2048]{1,0:T(8,128)(2,1)S(1)}, bf16[64,2048]{1,0:T(8,128)(2,1)}, u32[]{:S(2)}, u32[]{:S(2)}) collective-permute-start(bf16[64,2048]{1,0:T(8,128)(2,1)S(1)} %copy-done.36), channel_id=1, source_target_pairs={{0,24},{24,0},{8,16},{16,8},{1,25},{25,1},{9,17},{17,9},{2,26},{26... | collective-permute-start | bytes 786440 | tf_op jit(solution)/shard_map/ppermute | solution.py:591
  93.4 56.7 %all-to-all-start.1 = ((bf16[32,8,2048]{2,1,0:T(8,128)(2,1)}), bf16[32,8,2048]{2,1,0:T(8,128)(2,1)}, u32[]{:S(2)}, u32[]{:S(2)}) async-start(bf16[32,8,2048]{2,1,0:T(8,128)(2,1)} %bitcast.11), calls=%async_computation.1 | async-start | bytes 2097152 | tf_op jit(solution)/shard_map/all_to_all | solution.py:715
  98.3 243.9 %all-gather.9.cloned.1.call-start = ((), (), s32[]{:S(2)}) async-start(), calls=%async_computation.12 | async-start | bytes 7864320 | tf_op jit(solution)/shard_map/all_gather | solution.py:584
  109.0 69.7 %collective-permute-start.11 = (bf16[2,128,2048]{2,1,0:T(8,128)(2,1)}, bf16[2,128,2048]{2,1,0:T(8,128)(2,1)}, u32[]{:S(2)}, u32[]{:S(2)}) collective-permute-start(bf16[2,128,2048]{2,1,0:T(8,128)(2,1)} %bitcast.28.piece0), channel_id=1, source_target_pairs={{0,2},{2,0},{1,3},{3,1},{4,6},{6,4},{5,7},{7,5},{8,10},{10,8},{9,1... | collective-permute-start | bytes 3145736 | tf_op jit(solution)/shard_map/ppermute | solution.py:791
  127.8 50.9 %collective-permute-start.12 = (bf16[1024,1024]{1,0:T(8,128)(2,1)}, bf16[1024,1024]{1,0:T(8,128)(2,1)}, u32[]{:S(2)}, u32[]{:S(2)}) collective-permute-start(bf16[1024,1024]{1,0:T(8,128)(2,1)} %all-gather.7.cloned.1.call-done.own_ref), channel_id=1, source_target_pairs={{0,4},{4,0},{1,5},{5,1},{2,6},{6,2},{3,7},{7,3},{8,12},{12,8},{9,1... | collective-permute-start | bytes 6291464 | tf_op jit(solution)/shard_map/ppermute | solution.py:775
  202.9 390.2 %reduce-scatter.5.cloned.1.call-start = ((), (), s32[]{:S(2)}) async-start(), calls=%async_computation.7 | async-start | bytes 7864320 | tf_op jit(solution)/shard_map/reduce_scatter | solution.py:605
  240.7 46.8 %collective-permute-start.23 = (bf16[256,2048]{1,0:T(8,128)(2,1)S(1)}, bf16[256,2048]{1,0:T(8,128)(2,1)S(1)}, u32[]{:S(2)}, u32[]{:S(2)}) collective-permute-start(bf16[256,2048]{1,0:T(8,128)(2,1)S(1)} %get-tuple-element.181), channel_id=1, source_target_pairs={{0,2},{2,0},{1,3},{3,1},{4,6},{6,4},{5,7},{7,5},{8,10},{10,8},{9,1... | collective-permute-start | bytes 3145736 | tf_op jit(solution)/shard_map/ppermute | solution.py:640
  242.6 46.6 %collective-permute-start.24 = (bf16[256,2048]{1,0:T(8,128)(2,1)S(1)}, bf16[256,2048]{1,0:T(8,128)(2,1)S(1)}, u32[]{:S(2)}, u32[]{:S(2)}) collective-permute-start(bf16[256,2048]{1,0:T(8,128)(2,1)S(1)} %get-tuple-element.181), channel_id=1, source_target_pairs={{0,6},{6,0},{2,4},{4,2},{1,7},{7,1},{3,5},{5,3},{8,14},{14,8},{10,... | collective-permute-start | bytes 3145736 | tf_op jit(solution)/shard_map/ppermute | solution.py:641
  244.3 47.1 %collective-permute-start.25 = (bf16[256,2048]{1,0:T(8,128)(2,1)S(1)}, bf16[256,2048]{1,0:T(8,128)(2,1)S(1)}, u32[]{:S(2)}, u32[]{:S(2)}) collective-permute-start(bf16[256,2048]{1,0:T(8,128)(2,1)S(1)} %get-tuple-element.181), channel_id=1, source_target_pairs={{0,1},{1,0},{2,3},{3,2},{4,5},{5,4},{6,7},{7,6},{8,9},{9,8},{10,11... | collective-permute-start | bytes 3145736 | tf_op jit(solution)/shard_map/ppermute | solution.py:646
  337.1 281.2 %reduce-scatter.7.cloned.1.call-start = ((), (), s32[]{:S(2)}) async-start(), calls=%async_computation.8 | async-start | bytes 7864320 | tf_op jit(solution)/shard_map/reduce_scatter | solution.py:605
  413.0 47.6 %collective-permute-start.32 = (bf16[256,2048]{1,0:T(8,128)(2,1)}, bf16[256,2048]{1,0:T(8,128)(2,1)}, u32[]{:S(2)}, u32[]{:S(2)}) collective-permute-start(bf16[256,2048]{1,0:T(8,128)(2,1)} %get-tuple-element.146), channel_id=1, source_target_pairs={{0,6},{6,0},{2,4},{4,2},{1,7},{7,1},{3,5},{5,3},{8,14},{14,8},{10,... | collective-permute-start | bytes 3145736 | tf_op jit(solution)/shard_map/ppermute | solution.py:658
  414.5 47.5 %collective-permute-start.31 = (bf16[256,2048]{1,0:T(8,128)(2,1)}, bf16[256,2048]{1,0:T(8,128)(2,1)}, u32[]{:S(2)}, u32[]{:S(2)}) collective-permute-start(bf16[256,2048]{1,0:T(8,128)(2,1)} %get-tuple-element.145), channel_id=1, source_target_pairs={{0,2},{2,0},{1,3},{3,1},{4,6},{6,4},{5,7},{7,5},{8,10},{10,8},{9,1... | collective-permute-start | bytes 3145736 | tf_op jit(solution)/shard_map/ppermute | solution.py:658
  437.9 186.4 %reduce-scatter.11.cloned.1.call-start = ((), (), s32[]{:S(2)}) async-start(), calls=%async_computation.10 | async-start | bytes 1310720 | tf_op jit(solution)/shard_map/reduce_scatter | solution.py:605
  478.5 49.6 %collective-permute-start.37 = (bf16[2,256,2048]{2,1,0:T(8,128)(2,1)}, bf16[2,256,2048]{2,1,0:T(8,128)(2,1)}, u32[]{:S(2)}, u32[]{:S(2)}) collective-permute-start(bf16[2,256,2048]{2,1,0:T(8,128)(2,1)} %pad_maximum_fusion.2), channel_id=1, source_target_pairs={{0,4},{4,0},{1,5},{5,1},{2,6},{6,2},{3,7},{7,3},{8,12},{12,8},{9,1... | collective-permute-start | bytes 6291464 | tf_op jit(solution)/shard_map/ppermute | solution.py:864
  537.4 44.0 %collective-permute-start.40 = (bf16[2,128,2048]{2,1,0:T(8,128)(2,1)}, bf16[2,128,2048]{2,1,0:T(8,128)(2,1)}, u32[]{:S(2)}, u32[]{:S(2)}) collective-permute-start(bf16[2,128,2048]{2,1,0:T(8,128)(2,1)} %fusion.26), channel_id=1, source_target_pairs={{0,2},{2,0},{1,3},{3,1},{4,6},{6,4},{5,7},{7,5},{8,10},{10,8},{9,1... | collective-permute-start | bytes 3145736 | tf_op jit(solution)/shard_map/ppermute | solution.py:633
  555.3 59.1 %collective-permute-start.42 = (bf16[1024,1024]{1,0:T(8,128)(2,1)}, bf16[1024,1024]{1,0:T(8,128)(2,1)}, u32[]{:S(2)}, u32[]{:S(2)}) collective-permute-start(bf16[1024,1024]{1,0:T(8,128)(2,1)} %get-tuple-element.164), channel_id=1, source_target_pairs={{0,4},{4,0},{1,5},{5,1},{2,6},{6,2},{3,7},{7,3},{8,12},{12,8},{9,1... | collective-permute-start | bytes 6291464 | tf_op jit(solution)/shard_map/ppermute | solution.py:891
  590.3 81.1 %all-to-all-start.2 = ((bf16[32,8,4224]{2,1,0:T(8,128)(2,1)}), bf16[32,8,4224]{2,1,0:T(8,128)(2,1)S(1)}, u32[]{:S(2)}, u32[]{:S(2)}) async-start(bf16[32,8,4224]{2,1,0:T(8,128)(2,1)} %pad_maximum_fusion), calls=%async_computation.2 | async-start | bytes 4325376 | tf_op jit(solution)/shard_map/all_to_all | solution.py:715
  593.0 82.5 %reduce-scatter.9.cloned.1.call-start = ((), (), s32[]{:S(2)}) async-start(), calls=%async_computation.9 | async-start | bytes 2621440 | tf_op jit(solution)/shard_map/reduce_scatter | solution.py:605
  (72 other events, 986.7 us)
Sparse Core Ops, SparseCore 0:
  16.5 76.6 all-gather.6
  94.8 131.3 all-gather.10
  227.7 114.3 all-gather.8
  344.3 108.9 reduce-scatter.4
  455.5 111.2 reduce-scatter.6
  569.5 27.6 reduce-scatter.10
  620.6 54.8 reduce-scatter.8

commit v7 on v6

--- a/solution.py
+++ b/solution.py
@@ -769,7 +769,6 @@
     )
     output_pieces, ff_shards = rest[:count], rest[count:]
     crossed = [crossed] + [lax.ppermute(part, "x", SWAP) for part in output_pieces[1:]]
-    *crossed, fused_own = tie(*crossed, fused_own)
     output_own, output_other = join_pieces(output_pieces), join_pieces(crossed)
     ff_weights = [gather_z(ff_shards[0])]
     fused_other = lax.ppermute(fused_own, "x", SWAP)

time: 690 us -> 690 us (level)
    ppermute x3, waiting for transfers between devices: 14.2 us -> 3.09 us  [body(): lax.ppermute(part, 'x', SWAP)]
    all_to_all x3, waiting for transfers between devices: 59.5 us -> 66.8 us  [exchange(): lax.all_to_all(blocks, everywhere, split_axis=0, concat_axis=0, tiled=True)]
    unnamed x95 -> x87, local copies, waits for them, and re-layouts: 18.4 us -> 18.4 us
  transfers between devices with their start and end apart: 55 -> 55, of which waited for: 31 -> 29; matrix products, arithmetic and copies ran while one was open for 15% -> 15% of each run, Pallas kernels for 26% -> 26%
where the time goes in v7:
time: 690 us; the launch traced here: 685 us
  waiting for transfers between devices  316 us (46%)
  Pallas kernels  175 us (25%)
  other arithmetic  73.4 us (11%)
  starting transfers between devices  59.6 us (9%)
  local copies, waits for them, and re-layouts  38.8 us (6%)
  between operations  15.3 us (2%)
  matrix products  7.31 us (1%)
    pallas_call x2, Pallas kernels, feedforward(): pl.pallas_call(functools.partial(feedforward_kernel, len(earlier), last),...  76.5 us
    all_to_all x3, waiting for transfers between devices, exchange(): lax.all_to_all(blocks, everywhere, split_axis=0, concat_axis=0, tiled=True)  66.8 us
    pallas_call x2, Pallas kernels, feedforward_grads(): pl.pallas_call(feedforward_grads_kernel, grid=(pieces,), in_specs=[pl.Blo...  42.5 us
    ppermute x2, waiting for transfers between devices, reduce_tensor(): lax.ppermute(moved, 'y', SWAP).astype(F32)  40 us
    ppermute x2, waiting for transfers between devices, reduce_x(): lax.ppermute(leaving, 'x', SWAP).astype(F32)  34.4 us
    pallas_call x1, Pallas kernels, attention_backward(): pl.pallas_call(functools.partial(attention_backward_kernel, query_cols //...  30.8 us
    ppermute x3, waiting for transfers between devices, send_eight(): lax.ppermute(part, axes, pairs)  25.4 us
    ppermute x2, waiting for transfers between devices, body(): lax.ppermute(leaving, 'x', SWAP)  21.7 us
  transfers between devices with their start and end apart: 55, of which 29 were waited for; matrix products, arithmetic and copies ran while one was open for 15% of the time, Pallas kernels for 26%

profile of v7, /device:TPU:0, one launch (start us, length us, event | category | flops | bytes accessed | tf_op | source)
XLA Modules:
  0.0 685.4 jit_solution(1655407705190281553)
XLA Ops:
  36.5 13.6 %collective-permute-done.4 = bf16[256,1024]{1,0:T(8,128)(2,1)} collective-permute-done((bf16[256,1024]{1,0:T(8,128)(2,1)}, bf16[256,1024]{1,0:T(8,128)(2,1)}, u32[]{:S(2)}, u32[]{:S(2)}) %collective-permute-start.4) | collective-permute-done | bytes 524320 | tf_op jit(solution)/shard_map/ppermute | solution.py:759
  55.0 8.1 %collective-permute-done.5 = bf16[256,1024]{1,0:T(8,128)(2,1)} collective-permute-done((bf16[256,1024]{1,0:T(8,128)(2,1)}, bf16[256,1024]{1,0:T(8,128)(2,1)}, u32[]{:S(2)}, u32[]{:S(2)}) %collective-permute-start.5) | collective-permute-done | bytes 524320 | tf_op jit(solution)/shard_map/ppermute | solution.py:759
  66.2 19.7 %all-to-all-done = bf16[32,8,2176]{2,1,0:T(8,128)(2,1)S(1)} async-done(((bf16[32,8,2176]{2,1,0:T(8,128)(2,1)}), bf16[32,8,2176]{2,1,0:T(8,128)(2,1)S(1)}, u32[]{:S(2)}, u32[]{:S(2)}) %all-to-all-start) | async-done | bytes 1114144 | tf_op jit(solution)/shard_map/all_to_all | solution.py:715
  86.1 7.1 %all-gather.7.cloned.1.call-done.own_ref = bf16[1024,1024]{1,0:T(8,128)(2,1)} async-done(((bf16[256,1024]{1,0:T(8,128)(2,1)}), bf16[1024,1024]{1,0:T(8,128)(2,1)}) %all-gather.7.cloned.1.call-update) | async-done | bytes 2097168 | tf_op jit(solution)/shard_map/all_gather | solution.py:584
  123.0 27.1 %all-to-all-done.1 = bf16[32,8,2048]{2,1,0:T(8,128)(2,1)} async-done(((bf16[32,8,2048]{2,1,0:T(8,128)(2,1)}), bf16[32,8,2048]{2,1,0:T(8,128)(2,1)}, u32[]{:S(2)}, u32[]{:S(2)}) %all-to-all-start.1) | async-done | bytes 1048608 | tf_op jit(solution)/shard_map/all_to_all | solution.py:715
  157.9 13.9 %collective-permute-done.6 = bf16[256,2048]{1,0:T(8,128)(2,1)S(1)} collective-permute-done((bf16[256,2048]{1,0:T(8,128)(2,1)S(1)}, bf16[256,2048]{1,0:T(8,128)(2,1)S(1)}, u32[]{:S(2)}, u32[]{:S(2)}) %collective-permute-start.6) | collective-permute-done | bytes 1048608 | tf_op jit(solution)/shard_map/ppermute | solution.py:800
  184.7 17.1 %shard_map.213 = (bf16[1024,2048]{1,0:T(8,128)(2,1)}, bf16[1024,1024]{1,0:T(8,128)(2,1)}, bf16[1024,512]{1,0:T(8,128)(2,1)}, bf16[2,2,128,2048]{3,2,1,0:T(8,128)(2,1)}, bf16[2,2,128,2048]{3,2,1,0:T(8,128)(2,1)}) custom-call(s32[2]{0:T(128)} %pad_add_fusion.1.place_ref, bf16[2,128,2048]{2,1,0:T(8,128)(2,1)} %bitcast.28.piece0, ...), custom_call_target="tpu_custom_call" | custom-call | tf_op jit(solution)/shard_map/pallas_call | solution.py:294
  213.9 22.1 %collective-permute-done.17 = bf16[2,128,2048]{2,1,0:T(8,128)(2,1)} collective-permute-done((bf16[2,128,2048]{2,1,0:T(8,128)(2,1)}, bf16[2,128,2048]{2,1,0:T(8,128)(2,1)}, u32[]{:S(2)}, u32[]{:S(2)}) %collective-permute-start.17) | collective-permute-done | bytes 1048608 | tf_op jit(solution)/shard_map/ppermute | solution.py:633
  244.5 21.7 %collective-permute-done.18 = bf16[256,2048]{1,0:T(8,128)(2,1)S(1)} collective-permute-done((bf16[256,2048]{1,0:T(8,128)(2,1)S(1)}, bf16[256,2048]{1,0:T(8,128)(2,1)S(1)}, u32[]{:S(2)}, u32[]{:S(2)}) %collective-permute-start.18) | collective-permute-done | bytes 1048608 | tf_op jit(solution)/shard_map/ppermute | solution.py:639
  266.3 21.2 %collective-permute-done.23 = bf16[256,2048]{1,0:T(8,128)(2,1)S(1)} collective-permute-done((bf16[256,2048]{1,0:T(8,128)(2,1)S(1)}, bf16[256,2048]{1,0:T(8,128)(2,1)S(1)}, u32[]{:S(2)}, u32[]{:S(2)}) %collective-permute-start.23) | collective-permute-done | bytes 1048608 | tf_op jit(solution)/shard_map/ppermute | solution.py:640
  295.5 20.4 %shard_map.214 = (bf16[2048,512]{1,0:T(8,128)(2,1)}, bf16[2048,1024]{1,0:T(8,128)(2,1)}) custom-call(bf16[2048,2048]{1,0:T(8,128)(2,1)} %constant_dynamic-update-slice_fusion.8.normed_ref, bf16[2048,2048]{1,0:T(8,128)(2,1)} %copy-done.2, bf16[4,768,1024]{2,1,0:T(8,128)(2,1)} %bitcast.186), custom_call_target="tpu_custom_call" | custom-call | tf_op jit(solution)/shard_map/pallas_call | solution.py:446
  315.9 21.1 %shard_map.218 = bf16[4,768,1024]{2,1,0:T(8,128)(2,1)} custom-call(bf16[2048,2048]{1,0:T(8,128)(2,1)} %constant_dynamic-update-slice_fusion.8.normed_ref, bf16[2048,1024]{1,0:T(8,128)(2,1)} %get-tuple-element.127.refs_1_.d_both_ref, bf16[2048,512]{1,0:T(8,128)(2,1)} %get-tuple-element.126.refs_0_.hidden_ref, bf16[2048,2048]{1,0:T(8,128)(2,1)} %copy-done.2), custom_call_target="tpu_custom_call" | custom-call | tf_op jit(solution)/shard_map/pallas_call | solution.py:482
  342.1 56.1 %shard_map.215 = (bf16[2048,512]{1,0:T(8,128)(2,1)}, bf16[2048,1024]{1,0:T(8,128)(2,1)}, bf16[1024,2048]{1,0:T(8,128)(2,1)}, bf16[1024,2048]{1,0:T(8,128)(2,1)},...) custom-call(bf16[2048,2048]{1,0:T(8,128)(2,1)} %constant_dynamic-update-slice_fusion.8.normed_ref, ...), custom_call_target="tpu_custom_call" | custom-call | tf_op jit(solution)/shard_map/pallas_call | solution.py:446
  398.3 7.3 %collective-permute-done.29 = bf16[4,256,2048]{2,1,0:T(8,128)(2,1)S(1)} collective-permute-done((bf16[4,256,2048]{2,1,0:T(8,128)(2,1)}, bf16[4,256,2048]{2,1,0:T(8,128)(2,1)S(1)}, u32[]{:S(2)}, u32[]{:S(2)}) %collective-permute-start.29) | collective-permute-done | bytes 4194336 | tf_op jit(solution)/shard_map/ppermute | solution.py:651
  415.1 21.4 %shard_map.216 = bf16[4,768,1024]{2,1,0:T(8,128)(2,1)} custom-call(bf16[2048,2048]{1,0:T(8,128)(2,1)} %constant_dynamic-update-slice_fusion.8.normed_ref, bf16[2048,1024]{1,0:T(8,128)(2,1)} %get-tuple-element.131.d_both_ref, bf16[2048,512]{1,0:T(8,128)(2,1)} %get-tuple-element.132.hidden_ref, bf16[2048,2048]{1,0:T(8,128)(2,1)} %copy-done.2), custom_call_target="tpu_custom_call" | custom-call | tf_op jit(solution)/shard_map/pallas_call | solution.py:482
  438.0 22.6 %collective-permute-done.32 = bf16[256,2048]{1,0:T(8,128)(2,1)} collective-permute-done((bf16[256,2048]{1,0:T(8,128)(2,1)}, bf16[256,2048]{1,0:T(8,128)(2,1)}, u32[]{:S(2)}, u32[]{:S(2)}) %collective-permute-start.32) | collective-permute-done | bytes 1048608 | tf_op jit(solution)/shard_map/ppermute | solution.py:658
  480.1 13.5 %collective-permute-done.35.piece2 = bf16[2,128,2048]{2,1,0:T(8,128)(2,1)S(1)} collective-permute-done((bf16[2,128,2048]{2,1,0:T(8,128)(2,1)S(1)}, bf16[2,128,2048]{2,1,0:T(8,128)(2,1)S(1)}, u32[]{:S(2)}, u32[]{:S(2)}) %collective-permute-start.35) | collective-permute-done | bytes 1048608 | tf_op jit(solution)/shard_map/ppermute | solution.py:621
  497.3 30.8 %shard_map.217 = (bf16[2,2,128,2048]{3,2,1,0:T(8,128)(2,1)}, bf16[2,2,128,2048]{3,2,1,0:T(8,128)(2,1)}, bf16[1024,1024]{1,0:T(8,128)(2,1)}, bf16[1024,1024]{1,0:...) custom-call(s32[2]{0:T(128)} %pad_add_fusion.1.place_ref, bf16[2,128,2048]{2,1,0:T(8,128)(2,1)} %bitcast.210, ...), custom_call_target="tpu_custom_call" | custom-call | tf_op jit(solution)/shard_map/pallas_call | solution.py:327
  538.4 15.5 %collective-permute-done.41 = bf16[256,2048]{1,0:T(8,128)(2,1)S(1)} collective-permute-done((bf16[256,2048]{1,0:T(8,128)(2,1)}, bf16[256,2048]{1,0:T(8,128)(2,1)S(1)}, u32[]{:S(2)}, u32[]{:S(2)}) %collective-permute-start.41) | collective-permute-done | bytes 1048608 | tf_op jit(solution)/shard_map/ppermute | solution.py:890
  563.5 17.9 %collective-permute-done.40 = bf16[2,128,2048]{2,1,0:T(8,128)(2,1)} collective-permute-done((bf16[2,128,2048]{2,1,0:T(8,128)(2,1)}, bf16[2,128,2048]{2,1,0:T(8,128)(2,1)}, u32[]{:S(2)}, u32[]{:S(2)}) %collective-permute-start.40) | collective-permute-done | bytes 1048608 | tf_op jit(solution)/shard_map/ppermute | solution.py:633
  595.5 18.9 %collective-permute-done.42 = bf16[1024,1024]{1,0:T(8,128)(2,1)} collective-permute-done((bf16[1024,1024]{1,0:T(8,128)(2,1)}, bf16[1024,1024]{1,0:T(8,128)(2,1)}, u32[]{:S(2)}, u32[]{:S(2)}) %collective-permute-start.42) | collective-permute-done | bytes 2097184 | tf_op jit(solution)/shard_map/ppermute | solution.py:890
  628.8 10.0 %collective-permute-done.43.refs_1_ = bf16[256,1024]{1,0:T(8,128)(2,1)} collective-permute-done((bf16[256,1024]{1,0:T(8,128)(2,1)}, bf16[256,1024]{1,0:T(8,128)(2,1)}, u32[]{:S(2)}, u32[]{:S(2)}) %collective-permute-start.43) | collective-permute-done | bytes 524320 | tf_op jit(solution)/shard_map/ppermute | solution.py:897
  638.8 8.4 %collective-permute-done.44.refs_3_ = bf16[256,1024]{1,0:T(8,128)(2,1)} collective-permute-done((bf16[256,1024]{1,0:T(8,128)(2,1)}, bf16[256,1024]{1,0:T(8,128)(2,1)}, u32[]{:S(2)}, u32[]{:S(2)}) %collective-permute-start.44) | collective-permute-done | bytes 524320 | tf_op jit(solution)/shard_map/ppermute | solution.py:897
  651.4 20.0 %all-to-all-done.2 = bf16[32,8,4224]{2,1,0:T(8,128)(2,1)S(1)} async-done(((bf16[32,8,4224]{2,1,0:T(8,128)(2,1)}), bf16[32,8,4224]{2,1,0:T(8,128)(2,1)S(1)}, u32[]{:S(2)}, u32[]{:S(2)}) %all-to-all-start.2) | async-done | bytes 2162720 | tf_op jit(solution)/shard_map/all_to_all | solution.py:715
  (310 shorter events, 214.6 us)
Async XLA Ops:
  7.2 86.0 %all-gather.7.cloned.1.call-start = ((), (), s32[]{:S(2)}) async-start(), calls=%async_computation.11 | async-start | bytes 2621440 | tf_op jit(solution)/shard_map/all_gather | solution.py:584
  7.2 78.8 %collective-permute-start = (bf16[64,2048]{1,0:T(8,128)(2,1)}, bf16[64,2048]{1,0:T(8,128)(2,1)}, u32[]{:S(2)}, u32[]{:S(2)}) collective-permute-start(bf16[64,2048]{1,0:T(8,128)(2,1)} %param.20), channel_id=1, source_target_pairs={{0,4},{4,0},{1,5},{5,1},{2,6},{6,2},{3,7},{7,3},{8,12},{12,8},{9,1... | collective-permute-start | bytes 786440 | tf_op jit(solution)/shard_map/ppermute | solution.py:765
  10.2 75.8 %collective-permute-start.1 = (bf16[64,2048]{1,0:T(8,128)(2,1)}, bf16[64,2048]{1,0:T(8,128)(2,1)}, u32[]{:S(2)}, u32[]{:S(2)}) collective-permute-start(bf16[64,2048]{1,0:T(8,128)(2,1)} %param.20), channel_id=1, source_target_pairs={{0,8},{8,0},{16,24},{24,16},{1,9},{9,1},{17,25},{25,17},{2,10},{10... | collective-permute-start | bytes 786440 | tf_op jit(solution)/shard_map/ppermute | solution.py:591
  11.8 74.3 %collective-permute-start.2 = (bf16[64,2048]{1,0:T(8,128)(2,1)}, bf16[64,2048]{1,0:T(8,128)(2,1)}, u32[]{:S(2)}, u32[]{:S(2)}) collective-permute-start(bf16[64,2048]{1,0:T(8,128)(2,1)} %param.20), channel_id=1, source_target_pairs={{0,16},{16,0},{8,24},{24,8},{1,17},{17,1},{9,25},{25,9},{2,18},{18... | collective-permute-start | bytes 786440 | tf_op jit(solution)/shard_map/ppermute | solution.py:591
  23.4 62.5 %all-to-all-start = ((bf16[32,8,2176]{2,1,0:T(8,128)(2,1)}), bf16[32,8,2176]{2,1,0:T(8,128)(2,1)S(1)}, u32[]{:S(2)}, u32[]{:S(2)}) async-start(bf16[32,8,2176]{2,1,0:T(8,128)(2,1)} %pad_maximum_fusion.5), calls=%async_computation | async-start | bytes 2228224 | tf_op jit(solution)/shard_map/all_to_all | solution.py:715
  26.2 269.3 %all-gather.11.cloned.1.call-start = ((), (), s32[]{:S(2)}) async-start(), calls=%async_computation.13 | async-start | bytes 7864320 | tf_op jit(solution)/shard_map/all_gather | solution.py:584
  93.4 56.7 %all-to-all-start.1 = ((bf16[32,8,2048]{2,1,0:T(8,128)(2,1)}), bf16[32,8,2048]{2,1,0:T(8,128)(2,1)}, u32[]{:S(2)}, u32[]{:S(2)}) async-start(bf16[32,8,2048]{2,1,0:T(8,128)(2,1)} %bitcast.11), calls=%async_computation.1 | async-start | bytes 2097152 | tf_op jit(solution)/shard_map/all_to_all | solution.py:715
  98.3 243.9 %all-gather.9.cloned.1.call-start = ((), (), s32[]{:S(2)}) async-start(), calls=%async_computation.12 | async-start | bytes 7864320 | tf_op jit(solution)/shard_map/all_gather | solution.py:584
  100.8 53.2 %collective-permute-start.9 = (bf16[64,2048]{1,0:T(8,128)(2,1)}, bf16[64,2048]{1,0:T(8,128)(2,1)}, u32[]{:S(2)}, u32[]{:S(2)}) collective-permute-start(bf16[64,2048]{1,0:T(8,128)(2,1)} %collective-permute-done.3), channel_id=1, source_target_pairs={{0,4},{4,0},{1,5},{5,1},{2,6},{6,2},{3,7},{7,3},{8,12},{12,8},{9,1... | collective-permute-start | bytes 786440 | tf_op jit(solution)/shard_map/ppermute | solution.py:771
  109.0 69.7 %collective-permute-start.11 = (bf16[2,128,2048]{2,1,0:T(8,128)(2,1)}, bf16[2,128,2048]{2,1,0:T(8,128)(2,1)}, u32[]{:S(2)}, u32[]{:S(2)}) collective-permute-start(bf16[2,128,2048]{2,1,0:T(8,128)(2,1)} %bitcast.28.piece0), channel_id=1, source_target_pairs={{0,2},{2,0},{1,3},{3,1},{4,6},{6,4},{5,7},{7,5},{8,10},{10,8},{9,1... | collective-permute-start | bytes 3145736 | tf_op jit(solution)/shard_map/ppermute | solution.py:790
  110.4 68.2 %collective-permute-start.12 = (bf16[1024,1024]{1,0:T(8,128)(2,1)}, bf16[1024,1024]{1,0:T(8,128)(2,1)}, u32[]{:S(2)}, u32[]{:S(2)}) collective-permute-start(bf16[1024,1024]{1,0:T(8,128)(2,1)} %all-gather.7.cloned.1.call-done.own_ref), channel_id=1, source_target_pairs={{0,4},{4,0},{1,5},{5,1},{2,6},{6,2},{3,7},{7,3},{8,12},{12,8},{9,1... | collective-permute-start | bytes 6291464 | tf_op jit(solution)/shard_map/ppermute | solution.py:774
  202.8 390.2 %reduce-scatter.5.cloned.1.call-start = ((), (), s32[]{:S(2)}) async-start(), calls=%async_computation.7 | async-start | bytes 7864320 | tf_op jit(solution)/shard_map/reduce_scatter | solution.py:605
  240.7 46.8 %collective-permute-start.23 = (bf16[256,2048]{1,0:T(8,128)(2,1)S(1)}, bf16[256,2048]{1,0:T(8,128)(2,1)S(1)}, u32[]{:S(2)}, u32[]{:S(2)}) collective-permute-start(bf16[256,2048]{1,0:T(8,128)(2,1)S(1)} %get-tuple-element.171), channel_id=1, source_target_pairs={{0,2},{2,0},{1,3},{3,1},{4,6},{6,4},{5,7},{7,5},{8,10},{10,8},{9,1... | collective-permute-start | bytes 3145736 | tf_op jit(solution)/shard_map/ppermute | solution.py:640
  242.6 46.6 %collective-permute-start.24 = (bf16[256,2048]{1,0:T(8,128)(2,1)S(1)}, bf16[256,2048]{1,0:T(8,128)(2,1)S(1)}, u32[]{:S(2)}, u32[]{:S(2)}) collective-permute-start(bf16[256,2048]{1,0:T(8,128)(2,1)S(1)} %get-tuple-element.171), channel_id=1, source_target_pairs={{0,6},{6,0},{2,4},{4,2},{1,7},{7,1},{3,5},{5,3},{8,14},{14,8},{10,... | collective-permute-start | bytes 3145736 | tf_op jit(solution)/shard_map/ppermute | solution.py:641
  244.2 47.1 %collective-permute-start.25 = (bf16[256,2048]{1,0:T(8,128)(2,1)S(1)}, bf16[256,2048]{1,0:T(8,128)(2,1)S(1)}, u32[]{:S(2)}, u32[]{:S(2)}) collective-permute-start(bf16[256,2048]{1,0:T(8,128)(2,1)S(1)} %get-tuple-element.171), channel_id=1, source_target_pairs={{0,1},{1,0},{2,3},{3,2},{4,5},{5,4},{6,7},{7,6},{8,9},{9,8},{10,11... | collective-permute-start | bytes 3145736 | tf_op jit(solution)/shard_map/ppermute | solution.py:646
  337.0 281.2 %reduce-scatter.7.cloned.1.call-start = ((), (), s32[]{:S(2)}) async-start(), calls=%async_computation.8 | async-start | bytes 7864320 | tf_op jit(solution)/shard_map/reduce_scatter | solution.py:605
  413.0 47.6 %collective-permute-start.32 = (bf16[256,2048]{1,0:T(8,128)(2,1)}, bf16[256,2048]{1,0:T(8,128)(2,1)}, u32[]{:S(2)}, u32[]{:S(2)}) collective-permute-start(bf16[256,2048]{1,0:T(8,128)(2,1)} %get-tuple-element.136), channel_id=1, source_target_pairs={{0,6},{6,0},{2,4},{4,2},{1,7},{7,1},{3,5},{5,3},{8,14},{14,8},{10,... | collective-permute-start | bytes 3145736 | tf_op jit(solution)/shard_map/ppermute | solution.py:658
  414.5 47.5 %collective-permute-start.31 = (bf16[256,2048]{1,0:T(8,128)(2,1)}, bf16[256,2048]{1,0:T(8,128)(2,1)}, u32[]{:S(2)}, u32[]{:S(2)}) collective-permute-start(bf16[256,2048]{1,0:T(8,128)(2,1)} %get-tuple-element.135), channel_id=1, source_target_pairs={{0,2},{2,0},{1,3},{3,1},{4,6},{6,4},{5,7},{7,5},{8,10},{10,8},{9,1... | collective-permute-start | bytes 3145736 | tf_op jit(solution)/shard_map/ppermute | solution.py:658
  437.9 186.4 %reduce-scatter.11.cloned.1.call-start = ((), (), s32[]{:S(2)}) async-start(), calls=%async_computation.10 | async-start | bytes 1310720 | tf_op jit(solution)/shard_map/reduce_scatter | solution.py:605
  478.4 49.6 %collective-permute-start.37 = (bf16[2,256,2048]{2,1,0:T(8,128)(2,1)}, bf16[2,256,2048]{2,1,0:T(8,128)(2,1)}, u32[]{:S(2)}, u32[]{:S(2)}) collective-permute-start(bf16[2,256,2048]{2,1,0:T(8,128)(2,1)} %pad_maximum_fusion.2), channel_id=1, source_target_pairs={{0,4},{4,0},{1,5},{5,1},{2,6},{6,2},{3,7},{7,3},{8,12},{12,8},{9,1... | collective-permute-start | bytes 6291464 | tf_op jit(solution)/shard_map/ppermute | solution.py:863
  537.4 44.0 %collective-permute-start.40 = (bf16[2,128,2048]{2,1,0:T(8,128)(2,1)}, bf16[2,128,2048]{2,1,0:T(8,128)(2,1)}, u32[]{:S(2)}, u32[]{:S(2)}) collective-permute-start(bf16[2,128,2048]{2,1,0:T(8,128)(2,1)} %fusion.26), channel_id=1, source_target_pairs={{0,2},{2,0},{1,3},{3,1},{4,6},{6,4},{5,7},{7,5},{8,10},{10,8},{9,1... | collective-permute-start | bytes 3145736 | tf_op jit(solution)/shard_map/ppermute | solution.py:633
  555.3 59.1 %collective-permute-start.42 = (bf16[1024,1024]{1,0:T(8,128)(2,1)}, bf16[1024,1024]{1,0:T(8,128)(2,1)}, u32[]{:S(2)}, u32[]{:S(2)}) collective-permute-start(bf16[1024,1024]{1,0:T(8,128)(2,1)} %get-tuple-element.154), channel_id=1, source_target_pairs={{0,4},{4,0},{1,5},{5,1},{2,6},{6,2},{3,7},{7,3},{8,12},{12,8},{9,1... | collective-permute-start | bytes 6291464 | tf_op jit(solution)/shard_map/ppermute | solution.py:890
  590.2 81.1 %all-to-all-start.2 = ((bf16[32,8,4224]{2,1,0:T(8,128)(2,1)}), bf16[32,8,4224]{2,1,0:T(8,128)(2,1)S(1)}, u32[]{:S(2)}, u32[]{:S(2)}) async-start(bf16[32,8,4224]{2,1,0:T(8,128)(2,1)} %pad_maximum_fusion), calls=%async_computation.2 | async-start | bytes 4325376 | tf_op jit(solution)/shard_map/all_to_all | solution.py:715
  593.0 82.5 %reduce-scatter.9.cloned.1.call-start = ((), (), s32[]{:S(2)}) async-start(), calls=%async_computation.9 | async-start | bytes 2621440 | tf_op jit(solution)/shard_map/reduce_scatter | solution.py:605
  (68 other events, 955.7 us)
Sparse Core Ops, SparseCore 0:
  16.5 76.6 all-gather.6
  94.8 131.3 all-gather.10
  227.7 114.3 all-gather.8
  344.3 108.9 reduce-scatter.4
  455.5 111.2 reduce-scatter.6
  569.5 27.6 reduce-scatter.10
  620.6 54.8 reduce-scatter.8
